TPU v7x, 32 devices: a whole 2x2x4 slice. The times are simulated.
32 devices in a mesh: branch: 4 (over z), seq: 2 (over x), rep: 4 (over y, core).
Axes of the slice: x: 2, y: 2, z: 4, core: 2. Of those that a mesh axis runs over, the one named last changes fastest.
Arguments:
- noisy: bfloat16 [4, 1024, 5120], P('rep'), may hold values from -6 to 6
- generated: bfloat16 [4, 1024, 5120], P('rep', 'seq'), may hold values from -170 to 170
- caption: bfloat16 [4, 5120], P('rep'), may hold values from -0.59765625 to 0.59765625
- null_caption: bfloat16 [5120], replicated, may hold values from -0.59765625 to 0.59765625
- caption_drop: int32 [4], P('rep'), may hold values from 0 to 1, as said below
- timestep: int32 [4], P('rep'), may hold values from 0 to 999
- window_start: int32 [4], P('rep'), may hold values from 0 to 31736
- teacher_qkv: bfloat16 [3, 5120, 1024], P(None, None, ('branch', 'seq')), may hold values from -0.078125 to 0.078125
- teacher_out: bfloat16 [1024, 5120], P(('branch', 'seq')), may hold values from -0.1875 to 0.1875
- teacher_gain: float32 [5120], replicated, may hold values from 0.5 to 1.5
- teacher_qk_gain: float32 [2, 1024], P(None, ('branch', 'seq')), may hold values from 0.7 to 2.6
- critic_qkv: bfloat16 [3, 5120, 1024], P(None, None, ('branch', 'seq')), may hold values from -0.078125 to 0.078125
- critic_out: bfloat16 [1024, 5120], P(('branch', 'seq')), may hold values from -0.1875 to 0.1875
- critic_gain: float32 [5120], replicated, may hold values from 0.5 to 1.5
- critic_qk_gain: float32 [2, 1024], P(None, ('branch', 'seq')), may hold values from 0.7 to 2.6
Outputs:
- generator_grad: bfloat16 [4, 1024, 5120], P('rep', 'seq')
- critic_qkv_grad: float32 [3, 5120, 1024], P(None, 'rep', ('branch', 'seq'))
- critic_out_grad: float32 [1024, 5120], P(('branch', 'seq'), 'rep')
Inputs may be any that keep to these rules, and one draw needn't show every extreme that they name: `caption_drop`: each window's flag is drawn independently.
All inputs are finite; a program needn't handle non-finite values. Where the computation divides by a largest or mean magnitude, that divisor is 1e-20 or more.
Results may differ from a plain program's by a relative error of at most 0.018.
The roundings to bfloat16 on the way count: a program that leaves them out, or rounds other values in their place, can miss the bound.
Values may be sent and summed in bfloat16 or wider, within the bound.
No kernel may reach another device: no remote copies, remote signals or barrier semaphores. Data moves between devices by JAX's collectives and lax.ppermute only.
A program may use at most 192 MiB of HBM per device.

v0:
```python
import jax
import jax.numpy as jnp
from jax import lax
from jax.sharding import PartitionSpec as P

LEN = 1024
GRID_H = 30
GRID_W = 52


guidance = 5.0
score_scale = 128.0 ** (-0.5)
norm_eps = 1e-06


def rope_tables(first_token):
    token_index = first_token + jnp.arange(LEN, dtype=jnp.int32)
    plane_size = GRID_H * GRID_W
    frame_index = token_index // plane_size
    remainder = token_index - frame_index * plane_size
    row_index = remainder // GRID_W
    column_index = remainder - row_index * GRID_W
    pair_index = jnp.arange(64, dtype=jnp.int32)
    in_frames = pair_index < 22
    in_rows = jnp.logical_and(pair_index >= 22, pair_index < 43)
    local_rank = jnp.where(
        in_frames, pair_index, jnp.where(in_rows, pair_index - 22, pair_index - 43)
    ).astype(jnp.float32)
    axis_width = jnp.where(in_frames, 44.0, 42.0).astype(jnp.float32)
    frequency = jnp.exp(-jnp.log(10000.0) * 2.0 * local_rank / axis_width)
    chosen = jnp.where(
        in_frames[None, :],
        frame_index[:, None],
        jnp.where(in_rows[None, :], row_index[:, None], column_index[:, None]),
    ).astype(jnp.float32)
    angles = chosen * frequency[None, :]
    angles = jnp.concatenate([angles, angles], axis=1)
    return (jnp.cos(angles), jnp.sin(angles))


def rotate_half(values):
    return jnp.concatenate([-values[..., 64:], values[..., :64]], axis=-1)


def rotate_back(values):
    return jnp.concatenate([values[..., 64:], -values[..., :64]], axis=-1)


def norm_tokens(inputs, gain_values):
    scaled = (
        inputs
        * lax.rsqrt(jnp.mean(inputs * inputs, axis=-1, keepdims=True) + norm_eps)
        * gain_values
    )
    return scaled.astype(jnp.bfloat16)


def undo_norm(raw_values, inverse, gain_values, grad_normed):
    scaled = gain_values * grad_normed
    return inverse * scaled - raw_values * inverse * inverse * inverse * jnp.mean(
        scaled * raw_values, axis=-1, keepdims=True
    )


def head_forward(hidden, weights, qk_gains, cosine_table, sine_table):
    projected = jnp.einsum("bsd,kdc->kbsc", hidden, weights, preferred_element_type=jnp.float32)
    batch_size = hidden.shape[0]
    length = hidden.shape[1]
    query_raw = projected[0].reshape(batch_size, length, -1, 128)
    key_raw = projected[1].reshape(batch_size, length, -1, 128)
    value_rows = projected[2].reshape(batch_size, length, -1, 128).astype(jnp.bfloat16)
    gain_query = qk_gains[0].reshape(-1, 128)
    gain_key = qk_gains[1].reshape(-1, 128)
    inv_query = lax.rsqrt(jnp.mean(query_raw * query_raw, axis=-1, keepdims=True) + norm_eps)
    inv_key = lax.rsqrt(jnp.mean(key_raw * key_raw, axis=-1, keepdims=True) + norm_eps)
    normed_query = query_raw * inv_query * gain_query
    normed_key = key_raw * inv_key * gain_key
    cosine_h = cosine_table[:, :, None, :]
    sine_h = sine_table[:, :, None, :]
    rope_query = (normed_query * cosine_h + rotate_half(normed_query) * sine_h).astype(jnp.bfloat16)
    rope_key = (normed_key * cosine_h + rotate_half(normed_key) * sine_h).astype(jnp.bfloat16)
    scores = (
        jnp.einsum("bqhe,bkhe->bhqk", rope_query, rope_key, preferred_element_type=jnp.float32)
        * score_scale
    )
    exponent = jnp.exp(scores)
    probability = exponent / jnp.sum(exponent, axis=-1, keepdims=True)
    prob_rounded = probability.astype(jnp.bfloat16)
    attended = jnp.einsum(
        "bhqk,bkhe->bqhe", prob_rounded, value_rows, preferred_element_type=jnp.float32
    )
    attended = attended.astype(jnp.bfloat16).reshape(batch_size, length, -1)
    saved_state = (
        query_raw,
        key_raw,
        inv_query,
        inv_key,
        rope_query,
        rope_key,
        value_rows,
        probability,
        prob_rounded,
    )
    return (attended, saved_state)


def head_backward(hidden, grad_attn, saved_state, qk_gains, cosine_table, sine_table):
    (
        query_raw,
        key_raw,
        inv_query,
        inv_key,
        rope_query,
        rope_key,
        value_rows,
        probability,
        prob_rounded,
    ) = saved_state
    batch_size = hidden.shape[0]
    length = hidden.shape[1]
    grad_heads = grad_attn.reshape(batch_size, length, -1, 128)
    grad_prob = jnp.einsum(
        "bqhe,bkhe->bhqk", grad_heads, value_rows, preferred_element_type=jnp.float32
    )
    grad_score = (
        probability
        * (grad_prob - jnp.sum(grad_prob * probability, axis=-1, keepdims=True))
        * score_scale
    )
    grad_score = grad_score.astype(jnp.bfloat16)
    grad_qrot = jnp.einsum(
        "bhqk,bkhe->bqhe", grad_score, rope_key, preferred_element_type=jnp.float32
    )
    grad_krot = jnp.einsum(
        "bhqk,bqhe->bkhe", grad_score, rope_query, preferred_element_type=jnp.float32
    )
    grad_value = jnp.einsum(
        "bhqk,bqhe->bkhe", prob_rounded, grad_heads, preferred_element_type=jnp.float32
    )
    cosine_h = cosine_table[:, :, None, :]
    sine_h = sine_table[:, :, None, :]
    grad_qnorm = grad_qrot * cosine_h + rotate_back(grad_qrot * sine_h)
    grad_knorm = grad_krot * cosine_h + rotate_back(grad_krot * sine_h)
    grad_query = undo_norm(query_raw, inv_query, qk_gains[0].reshape(-1, 128), grad_qnorm)
    grad_key = undo_norm(key_raw, inv_key, qk_gains[1].reshape(-1, 128), grad_knorm)
    grad_stack = jnp.stack(
        [
            grad_query.reshape(batch_size, length, -1),
            grad_key.reshape(batch_size, length, -1),
            grad_value.reshape(batch_size, length, -1),
        ]
    ).astype(jnp.bfloat16)
    return jnp.einsum("bsd,kbsc->kdc", hidden, grad_stack, preferred_element_type=jnp.float32)


def body(
    noisy,
    generated,
    caption,
    null_caption,
    caption_drop,
    timestep,
    window_start,
    teacher_qkv,
    teacher_out,
    teacher_gain,
    teacher_qk_gain,
    critic_qkv,
    critic_out,
    critic_gain,
    critic_qk_gain,
):
    length = noisy.shape[1]
    width = noisy.shape[2]
    fraction = (timestep.astype(jnp.float32) + 1.0) / 1001.0
    noise_level = (5.0 * fraction / (1.0 + 4.0 * fraction))[:, None, None]
    used_caption = jnp.where(caption_drop[:, None] == 1, null_caption[None, :], caption)
    cond_shift = used_caption.astype(jnp.float32)[:, None, :]
    null_shift = null_caption.astype(jnp.float32)[None, None, :]
    latent = noisy.astype(jnp.float32)
    cond_normed = norm_tokens(latent + cond_shift, teacher_gain)
    null_normed = norm_tokens(latent + null_shift, teacher_gain)
    critic_normed = norm_tokens(latent + cond_shift, critic_gain)
    cosine_table, sine_table = jax.vmap(rope_tables)(window_start)
    cond_attn, unused = head_forward(
        cond_normed, teacher_qkv, teacher_qk_gain, cosine_table, sine_table
    )
    null_attn, unused = head_forward(
        null_normed, teacher_qkv, teacher_qk_gain, cosine_table, sine_table
    )
    fake_attn, saved_state = head_forward(
        critic_normed, critic_qkv, critic_qk_gain, cosine_table, sine_table
    )
    share_rows = length // lax.axis_size("seq")
    row_start = lax.axis_index("seq") * share_rows
    target = generated.astype(jnp.float32)
    cond_part = jnp.einsum(
        "bsc,cd->sbd", cond_attn, teacher_out, preferred_element_type=jnp.float32
    )
    null_part = jnp.einsum(
        "bsc,cd->sbd", null_attn, teacher_out, preferred_element_type=jnp.float32
    )
    guided_seq = lax.psum_scatter(
        (guidance * cond_part - (guidance - 1.0) * null_part).astype(jnp.bfloat16),
        "seq",
        scatter_dimension=0,
        tiled=True,
    )
    guided_rows = jnp.transpose(lax.psum(guided_seq, "branch").astype(jnp.float32), (1, 0, 2))
    fake_local = jnp.einsum(
        "bsc,cd->bsd", fake_attn, critic_out, preferred_element_type=jnp.float32
    )
    fake_full = lax.psum(fake_local.astype(jnp.bfloat16), ("branch", "seq")).astype(jnp.float32)
    target_full = lax.all_gather(generated, "seq", axis=1, tiled=True).astype(jnp.float32)
    fake_rows = lax.dynamic_slice_in_dim(fake_full, row_start, share_rows, 1)
    latent_rows = lax.dynamic_slice_in_dim(latent, row_start, share_rows, 1)
    cond_rows = latent_rows + cond_shift
    null_rows = latent_rows + null_shift
    real_velocity = guidance * cond_rows - (guidance - 1.0) * null_rows + guided_rows
    fake_velocity = cond_rows + fake_rows
    real_pred = latent_rows - noise_level * real_velocity
    fake_pred = latent_rows - noise_level * fake_velocity
    fake_pred_full = latent - noise_level * (latent + cond_shift + fake_full)
    cotangent = (-noise_level * (fake_pred_full - target_full) / 64.0).astype(jnp.bfloat16)
    out_grads = jnp.einsum("bsc,bsd->cd", fake_attn, cotangent, preferred_element_type=jnp.float32)
    grad_attn = jnp.einsum(
        "bsd,cd->bsc", cotangent, critic_out, preferred_element_type=jnp.float32
    ).astype(jnp.bfloat16)
    abs_total = lax.psum(jnp.sum(jnp.abs(real_pred - target), axis=(1, 2)), "seq")
    spread = abs_total / (length * width)
    generator_grad = ((fake_pred - real_pred) / (spread[:, None, None] + 1e-05)).astype(
        jnp.bfloat16
    )
    proj_share, out_share = (
        lax.psum_scatter(
            head_backward(
                critic_normed, grad_attn, saved_state, critic_qk_gain, cosine_table, sine_table
            ).astype(jnp.bfloat16),
            "rep",
            scatter_dimension=1,
            tiled=True,
        ).astype(jnp.float32),
        lax.psum_scatter(
            out_grads.astype(jnp.bfloat16), "rep", scatter_dimension=1, tiled=True
        ).astype(jnp.float32),
    )
    return (generator_grad, proj_share, out_share)


def solution(mesh):
    in_specs = (
        P("rep", None, None),
        P("rep", "seq", None),
        P("rep", None),
        P(),
        P("rep"),
        P("rep"),
        P("rep"),
        P(None, None, ("branch", "seq")),
        P(("branch", "seq"), None),
        P(),
        P(None, ("branch", "seq")),
        P(None, None, ("branch", "seq")),
        P(("branch", "seq"), None),
        P(),
        P(None, ("branch", "seq")),
    )
    out_specs = (
        P("rep", "seq", None),
        P(None, "rep", ("branch", "seq")),
        P(("branch", "seq"), "rep"),
    )
    return jax.shard_map(body, mesh=mesh, in_specs=in_specs, out_specs=out_specs, check_vma=False)
```

profile of v0, /device:TPU:0, one launch (start us, length us, event | category | flops | bytes accessed | tf_op | source)
XLA Modules:
  0.0 812.3 jit_solution(154347781953120975)
XLA Ops:
  8.0 0.0 copy-start
  8.0 0.0 all-gather.2.cloned.1.call-start
  8.1 0.7 all-gather.2.cloned.1.call-update
  8.8 0.0 all-reduce.3.cloned.1.call-start
  10.1 6.3 copy.18
  16.6 11.9 %multiply_reduce_fusion = (f32[1024]{0:T(1024)S(1)}, f32[1024]{0:T(1024)S(1)}) fusion(bf16[1,1024,5120]{2,1,0:T(8,128)(2,1)} %param.15, f32[5120]{0:T(1024)S(1)} %convert_element_type.334, f32[5120]{0:T(1024)S(1)} %bitcast.380), kind=kLoop, calls=%fused_computation.3 | loop fusion | flops 36698112 | bytes 10534912 | tf_op jit(solution)/shard_map/reduce_sum | solution.py:52
  28.5 6.9 fusion.10
  35.4 0.1 fusion.108
  35.5 0.1 fusion.105
  35.6 1.1 fusion.157
  36.7 0.2 fusion.111
  36.9 0.9 fusion.153
  37.8 0.9 fusion.155
  38.7 4.3 fusion.26
  43.0 2.0 copy-done.5
  45.1 0.9 fusion.33
  46.0 0.7 copy-done.19
  46.7 5.8 convert_bitcast_fusion
  52.5 0.0 all-reduce.3.cloned.1.call-update
  52.5 0.0 reduce-scatter.4.cloned.1.call-start
  52.6 0.0 slice-start
  52.6 6.4 copy.20
  59.0 10.0 %fusion.5 = f32[1024,384]{0,1:S(1)} fusion(bf16[5120,384]{0,1:T(8,128)(2,1)} %bitcast.378, bf16[1,1024,5120]{2,1,0:T(8,128)(2,1)} %param.15, f32[1024]{0:T(1024)S(1)} %add_rsqrt_fusion.2, f32[5120]{0:T(1024)S(1)} %convert_element_type.334, f32[5120]{0:T(1024)S(1)} %copy-done.31), kind=kOutput, calls=%fused_computation.12 | convolution fusion | flops 4052746240 | bytes 16035840
  69.1 0.1 fusion.96
  69.2 4.3 fusion.2
  73.6 0.1 fusion.102
  73.7 0.3 fusion.103
  74.2 0.7 copy-done.8
  74.9 6.2 fusion.28
  81.1 6.4 fusion.27
  87.5 11.7 %fusion.36 = f32[1024,5120]{1,0:T(8,128)} fusion(bf16[128,5120]{1,0:T(8,128)(2,1)S(1)} %copy-done, f32[1024,1024]{0,1:T(8,128)} %get-tuple-element.54, f32[1024]{0:T(1024)S(1)} %get-tuple-element.53, f32[3,1,1024,128]{2,3,1,0:T(8,128)} %bitcast.375), kind=kOutput, calls=%fused_computation.55 | convolution fusion | flops 1613889536 | bytes 26742784 | tf_op jit(solution)/shard_map/bsc,cd->sbd/dot_general | solution.py:197
  99.2 12.8 %fusion.18 = bf16[1024,1,5120]{2,0,1:T(8,128)(2,1)} fusion(bf16[128,5120]{1,0:T(8,128)(2,1)S(1)} %copy-done, f32[1024,5120]{1,0:T(8,128)} %fusion.36, f32[1024,1024]{0,1:T(8,128)} %get-tuple-element.56, f32[1024]{0:T(1024)S(1)} %get-tuple-element.55, f32[3,1,1024,128]{2,3,1,0:T(8,128)S(1)} %bitcast.371), kind=kOutput, calls=%fused_computation.28 | convolution fusion | flops 1634861056 | bytes 37228544 | tf_op jit(solution)/shard_map/bsc,cd->sbd/dot_general | solution.py:200
  112.1 0.0 reduce-scatter.4.cloned.1.call-update
  112.1 0.0 reduce-scatter.8.cloned.1.call-start
  112.8 30.1 %all-gather.2.cloned.1.call-done = bf16[1,1024,5120]{2,1,0:T(8,128)(2,1)} async-done(((bf16[1,512,5120]{2,1,0:T(8,128)(2,1)}), bf16[1,1024,5120]{2,1,0:T(8,128)(2,1)}) %all-gather.2.cloned.1.call-update) | async-done | bytes 10485776 | tf_op jit(solution)/shard_map/all_gather | solution.py:214
  143.0 339.1 %all-reduce.3.cloned.1.call-done = bf16[1,1024,5120]{2,1,0:T(8,128)(2,1)} async-done(((bf16[1,1024,5120]{2,1,0:T(8,128)(2,1)}), bf16[1,1024,5120]{2,1,0:T(8,128)(2,1)}) %all-reduce.3.cloned.1.call-update) | async-done | bytes 10485776 | tf_op jit(solution)/shard_map/psum | solution.py:213
  482.1 13.9 %fusion.7 = bf16[1024,5120]{1,0:T(8,128)(2,1)S(1)} fusion(bf16[1,1024,5120]{2,1,0:T(8,128)(2,1)} %all-gather.2.cloned.1.call-done, bf16[1,1024,5120]{2,1,0:T(8,128)(2,1)} %param.15, f32[]{:T(128)} %bitcast, f32[]{:T(128)} %bitcast.92, f32[5120]{0:T(1024)S(1)} %bitcast.383, bf16[1,1024,5120]{2,1,0:T(8,128)(2,1)} %all-reduce.3.cloned.1.call-done), kind=kLoop, calls=%fused_computation.13 | loop fusion | flops 57671680 | bytes 41963528 | tf_op jit(solution)/shard_map/reshape.74
  496.1 2.9 convolution_convert_fusion.3
  499.0 1.0 multiply_reduce_fusion.2
  500.1 1.2 multiply_convert_fusion.4
  501.3 2.3 convolution_bitcast_fusion.1
  503.6 3.9 fusion.85
  507.6 2.5 fusion.109
  510.2 2.6 convolution_convert_fusion
  512.8 0.0 reduce-scatter.8.cloned.1.call-update
  512.8 0.0 reduce-scatter.6.cloned.1.call-start
  512.9 3.4 fusion.113
  516.4 3.5 fusion.34
  519.9 0.5 slice-done.4
  520.4 1.4 slice-done.5
  521.8 6.2 fusion.22
  528.0 0.0 reduce-scatter.6.cloned.1.call-update
  528.1 0.0 all-reduce.5.cloned.1.call-start
  528.1 0.0 reduce-scatter.4.cloned.1.call-done
  528.1 0.5 all-reduce.5.cloned.1.call-update
  528.6 13.9 %convert_element_type.317 = f32[1,1024,5120]{2,1,0:T(8,128)} convert(bf16[1,1024,5120]{2,1,0:T(8,128)(2,1)} %param.15) | non-fusion elementwise | flops 5242880 | bytes 31457280 | tf_op jit(solution)/shard_map/convert_element_type | solution.py:180
  542.5 14.5 %convert_element_type.333 = f32[1,1024,5120]{2,1,0:T(8,128)} convert(bf16[1,1024,5120]{2,1,0:T(8,128)(2,1)} %all-reduce.3.cloned.1.call-done) | non-fusion elementwise | flops 5242880 | bytes 31457280 | tf_op jit(solution)/shard_map/convert_element_type | solution.py:213
  557.0 1.9 convert_element_type.369
  558.8 25.3 %reduce-scatter.6.cloned.1.call-done = bf16[3,1280,128]{1,2,0:T(8,128)(2,1)} async-done(((bf16[3,5120,128]{1,2,0:T(8,128)(2,1)}), bf16[3,1280,128]{1,2,0:T(8,128)(2,1)}) %reduce-scatter.6.cloned.1.call-update) | async-done | bytes 983056 | tf_op jit(solution)/shard_map/reduce_scatter | solution.py:235
  584.2 2.8 copy.22
  586.9 188.4 %all-reduce.5.cloned.1.call-done = bf16[1,512,5120]{2,1,0:T(8,128)(2,1)} async-done(((bf16[1,512,5120]{2,1,0:T(8,128)(2,1)}), bf16[1,512,5120]{2,1,0:T(8,128)(2,1)}) %all-reduce.5.cloned.1.call-update) | async-done | bytes 5242896 | tf_op jit(solution)/shard_map/psum | solution.py:209
  775.3 9.9 %abs_reduce_fusion = f32[]{:T(128)} fusion(bf16[1,512,5120]{2,1,0:T(8,128)(2,1)} %param.16, bf16[1,512,5120]{2,1,0:T(8,128)(2,1)} %all-reduce.5.cloned.1.call-done, f32[5120]{0:T(1024)S(1)} %convert_element_type.334, f32[5120]{0:T(1024)S(1)} %bitcast.385, f32[]{:T(128)} %bitcast, f32[1,1024,5120]{2,1,0:T(8,128)} %convert_element_type.317, s32[]{:T(128)S(6)} %select_n.143), kind=kLoop, calls=%fused_computation.19 | loop fusion | flops 34078720 | bytes 21012492 | tf_op jit(solution)/shard_map/reduce_sum | solution.py:229
  785.2 5.5 psum.23
  791.4 13.3 %divide_convert_fusion = bf16[1,512,5120]{2,1,0:T(8,128)(2,1)} fusion(f32[1,1024,5120]{2,1,0:T(8,128)} %convert_element_type.333, s32[]{:T(128)S(6)} %select_n.143, f32[1,1024,5120]{2,1,0:T(8,128)} %convert_element_type.317, f32[]{:T(128)} %bitcast.88, f32[5120]{0:T(1024)S(1)} %bitcast.386, f32[]{:T(128)} %bitcast, ...), kind=kLoop, calls=%fused_computation.18 | loop fusion | flops 39321600 | bytes 31498252 | tf_op jit(solution)/shard_map/convert_element_type | solution.py:231
  (98 shorter events, 0.6 us)
Async XLA Ops:
  8.0 79.5 %copy-start = (bf16[128,5120]{1,0:T(8,128)(2,1)S(1)}, bf16[128,5120]{1,0:T(8,128)(2,1)}, u32[]{:S(2)}) copy-start(bf16[128,5120]{1,0:T(8,128)(2,1)} %param.23) | copy-start | bytes 3932164
  8.0 2.1 copy-start.27
  8.0 134.9 %all-gather.2.cloned.1.call-start = ((), (), s32[]{:S(2)}) async-start(), calls=%async_computation.6 | async-start | bytes 15728640 | tf_op jit(solution)/shard_map/all_gather | solution.py:214
  8.8 7.7 copy-start.28
  8.8 473.3 %all-reduce.3.cloned.1.call-start = ((), (), s32[]{:S(2)}) async-start(), calls=%async_computation.3 | async-start | bytes 20971520 | tf_op jit(solution)/shard_map/psum | solution.py:213
  16.6 11.9 %copy-start.2 = (bf16[1,1024,5120]{2,1,0:T(8,128)(2,1)S(1)}, bf16[1,1024,5120]{2,1,0:T(8,128)(2,1)}, u32[]{:S(2)}) copy-start(bf16[1,1024,5120]{2,1,0:T(8,128)(2,1)} %param.15) | copy-start | bytes 31457284
  16.6 11.9 %copy-start.32 = (f32[5120]{0:T(1024)S(1)}, f32[5120]{0:T(1024)}, u32[]{:S(2)}) copy-start(f32[5120]{0:T(1024)} %param.28) | copy-start | bytes 61444
  28.5 7.0 copy-start.29
  35.4 7.6 copy-start.3
  36.7 6.3 copy-start.7
  43.0 2.1 copy-start.5
  45.1 1.6 copy-start.21
  46.0 0.7 copy-start.19
  52.5 6.5 copy-start.31
  52.5 475.6 %reduce-scatter.4.cloned.1.call-start = ((), (), s32[]{:S(2)}) async-start(), calls=%async_computation.4 | async-start | bytes 15728640 | tf_op jit(solution)/shard_map/reduce_scatter | solution.py:203
  52.6 16.6 %slice-start = ((s8[10485760]{0:T(1024)(128)(4,1)}), s8[2097152]{0:T(1024)(128)(4,1)S(1)}, s32[]{:S(2)}) async-start(s8[10485760]{0:T(1024)(128)(4,1)} %bitcast.350), calls=%async_computation.9 | async-start | bytes 4194304
  59.0 10.2 %slice-start.1 = ((s8[10485760]{0:T(1024)(128)(4,1)}), s8[4194304]{0:T(1024)(128)(4,1)S(1)}, s32[]{:S(2)}) async-start(s8[10485760]{0:T(1024)(128)(4,1)} %bitcast.350), calls=%async_computation.10 | async-start | bytes 8388608
  59.0 10.2 %slice-start.2 = ((s8[10485760]{0:T(1024)(128)(4,1)}), s8[4194304]{0:T(1024)(128)(4,1)S(1)}, s32[]{:S(2)}) async-start(s8[10485760]{0:T(1024)(128)(4,1)} %bitcast.350), calls=%async_computation.11 | async-start | bytes 8388608
  59.0 10.2 %copy-start.13 = (bf16[3,5120,128]{1,2,0:T(8,128)(2,1)S(1)}, bf16[3,5120,128]{1,2,0:T(8,128)(2,1)}, u32[]{:S(2)}) copy-start(bf16[3,5120,128]{1,2,0:T(8,128)(2,1)} %copy.20) | copy-start | bytes 11796484
  69.0 5.2 copy-start.9
  69.2 4.5 copy-start.30
  73.6 7.5 copy-start.11
  73.7 1.1 copy-start.8
  87.5 11.7 %copy-start.10 = (f32[1024,384]{0,1:S(1)}, f32[1024,384]{0,1}, u32[]{:S(2)}) copy-start(f32[1024,384]{0,1} %copy-done.9) | copy-start | bytes 4718596
  112.1 444.9 %reduce-scatter.8.cloned.1.call-start = ((), (), s32[]{:S(2)}) async-start(), calls=%async_computation.8 | async-start | bytes 1638400 | tf_op jit(solution)/shard_map/reduce_scatter | solution.py:243
  482.1 14.0 %copy-start.22 = (bf16[128,5120]{1,0:T(8,128)(2,1)S(1)}, bf16[128,5120]{1,0:T(8,128)(2,1)}, u32[]{:S(2)}) copy-start(bf16[128,5120]{1,0:T(8,128)(2,1)} %param.27) | copy-start | bytes 3932164
  496.0 2.9 copy-start.4
  496.0 2.9 copy-start.6
  498.9 1.0 copy-start.33
  500.0 1.3 copy-start.18
  500.0 1.3 copy-start.23
  500.0 1.3 copy-start.24
  500.0 3.5 copy-start.12
  500.0 3.5 copy-start.25
  500.0 3.5 copy-start.26
  507.5 2.7 copy-start.20
  507.5 2.6 copy-start.14
  507.6 2.6 copy-start.15
  507.6 2.5 copy-start.16
  507.6 2.5 copy-start.17
  512.8 7.1 slice-start.3
  512.8 71.3 %reduce-scatter.6.cloned.1.call-start = ((), (), s32[]{:S(2)}) async-start(), calls=%async_computation.7 | async-start | bytes 4915200 | tf_op jit(solution)/shard_map/reduce_scatter | solution.py:235
  516.3 4.1 slice-start.4
  516.4 5.4 slice-start.5
  528.1 247.3 %all-reduce.5.cloned.1.call-start = ((), (), s32[]{:S(2)}) async-start(), calls=%async_computation.5 | async-start | bytes 10485760 | tf_op jit(solution)/shard_map/psum | solution.py:209
  791.4 13.3 %copy-start.1 = (bf16[128,5120]{1,0:T(8,128)(2,1)S(1)}, bf16[128,5120]{1,0:T(8,128)(2,1)}, u32[]{:S(2)}) copy-start(bf16[128,5120]{1,0:T(8,128)(2,1)} %param.23) | copy-start | bytes 3932164
Sparse Core Ops, SparseCore 0:
  10.4 132.5 all-gather.1
  145.3 167.4 reduce-scatter.3
  512.9 25.4 reduce-scatter.7
  541.4 42.7 reduce-scatter.5
  586.4 188.9 all-reduce.4
Sparse Core Ops, SparseCore 1:
  52.6 429.5 all-reduce.2
where the time goes:
time: 821 us; the launch traced here: 812 us
  waiting for transfers between devices  584 us (71%)
  matrix products  91.8 us (11%)
  other arithmetic  90.4 us (11%)
  local copies, waits for them, and re-layouts  21 us (3%)
  between operations  19.2 us (2%)
    psum x1, waiting for transfers between devices, body(): lax.psum(fake_local.astype(jnp.bfloat16), ('branch', 'seq'))  339 us
    psum x1, waiting for transfers between devices, body(): lax.psum(guided_seq, 'branch').astype(jnp.float32)  188 us
    all_gather x1, waiting for transfers between devices, body(): lax.all_gather(generated, 'seq', axis=1, tiled=True).astype(jnp.float32)  30.1 us
    reduce_scatter x1, waiting for transfers between devices, body(): lax.psum_scatter(head_backward(critic_normed, grad_attn, saved_state, cri...  25.3 us
    unnamed x3, matrix products  21.2 us
    unnamed x83, local copies, waits for them, and re-layouts  21 us
    dot_general x3, matrix products, head_forward(): jnp.einsum('bqhe,bkhe->bhqk', rope_query, rope_key, preferred_element_typ...  16.9 us
  transfers between devices with their start and end apart: 6, of which 4 were waited for; matrix products, arithmetic and copies ran while one was open for 21% of the time, Pallas kernels for 0%

commit v1 on v0

v1 whole, which is shorter than its diff:
```python
import functools
import jax
import jax.numpy as jnp
from jax import lax
from jax.experimental import pallas as pl
from jax.experimental.pallas import tpu as pltpu
from jax.sharding import PartitionSpec as P

GRID_H = 30
GRID_W = 52

guidance = 5.0
norm_eps = 1e-06

ANY = pl.BlockSpec(memory_space=pl.ANY)
SMEM = pl.BlockSpec(memory_space=pltpu.SMEM)
F32, BF16 = jnp.float32, jnp.bfloat16


def swap(size, bit):
    return [(i, i ^ bit) for i in range(size)]


def bits_of(size):
    return [1 << k for k in range(size.bit_length() - 1)]


def move(value, axis, bit):
    return lax.ppermute(value, axis, swap(lax.axis_size(axis), bit))


def rope_tables(first_token, length):
    token_index = first_token + jnp.arange(length, dtype=jnp.int32)
    plane_size = GRID_H * GRID_W
    frame_index = token_index // plane_size
    remainder = token_index - frame_index * plane_size
    row_index = remainder // GRID_W
    column_index = remainder - row_index * GRID_W
    pair_index = jnp.arange(64, dtype=jnp.int32)
    in_frames = pair_index < 22
    in_rows = jnp.logical_and(pair_index >= 22, pair_index < 43)
    local_rank = jnp.where(
        in_frames, pair_index, jnp.where(in_rows, pair_index - 22, pair_index - 43)
    ).astype(jnp.float32)
    axis_width = jnp.where(in_frames, 44.0, 42.0).astype(jnp.float32)
    frequency = jnp.exp(-jnp.log(10000.0) * 2.0 * local_rank / axis_width)
    chosen = jnp.where(
        in_frames[None, :],
        frame_index[:, None],
        jnp.where(in_rows[None, :], row_index[:, None], column_index[:, None]),
    ).astype(jnp.float32)
    angles = chosen * frequency[None, :]
    angles = jnp.concatenate([angles, angles], axis=1)
    return (jnp.cos(angles), jnp.sin(angles))


def dot(left, right):
    return jnp.dot(left, right, preferred_element_type=F32)


def contract(left, right, left_dim, right_dim):
    return lax.dot_general(
        left, right, (((left_dim,), (right_dim,)), ((), ())), preferred_element_type=F32
    )


def rotate_half(values):
    half = values.shape[-1] // 2
    return jnp.concatenate([-values[..., half:], values[..., :half]], axis=-1)


def rotate_back(values):
    half = values.shape[-1] // 2
    return jnp.concatenate([values[..., half:], -values[..., :half]], axis=-1)


def resident(shape):
    return pl.BlockSpec(shape, lambda *_: (0,) * len(shape), pipeline_mode=pl.Buffered(1))


def project_kernel(variants, keep, held, noisy_ref, shift_ref, gain_ref, weight_ref, *refs):
    refs = refs[held:]
    out_ref = refs[0]
    hidden_ref = refs[1] if keep else None
    joined, normed = refs[-2:]
    tile, width = noisy_ref.shape
    head = weight_ref.shape[2]

    @pl.when(pl.program_id(0) == 0)
    def _():
        for k in range(3):
            joined[:, k * head : (k + 1) * head] = weight_ref[k]

    def step(t, carry):
        at = pl.ds(pl.multiple_of(t * 16, 16), 16)
        latent = noisy_ref[at, :].astype(F32)
        for v in range(variants):
            shifted = latent + shift_ref[v : v + 1, :]
            mean = jnp.sum(shifted * shifted, axis=-1, keepdims=True) / width
            scaled = shifted * lax.rsqrt(mean + norm_eps) * gain_ref[...]
            normed[v, at, :] = scaled.astype(BF16)
        return carry

    lax.fori_loop(0, tile // 16, step, 0)
    for v in range(variants):
        out_ref[v] = dot(normed[v], joined[...])
    if keep:
        hidden_ref[...] = normed[0]


def project(noisy, shifts, gain, weight, keep, start, count, into=()):
    length, width = noisy.shape
    head = weight.shape[2]
    variants = shifts.shape[0]
    tile = min(256, count)
    first = start // tile
    out_shape = [jax.ShapeDtypeStruct((variants, length, 3 * head), F32)]
    out_specs = [pl.BlockSpec((variants, tile, 3 * head), lambda i: (0, first + i, 0))]
    if keep:
        out_shape.append(jax.ShapeDtypeStruct((length, width), BF16))
        out_specs.append(pl.BlockSpec((tile, width), lambda i: (first + i, 0)))
    return pl.pallas_call(
        functools.partial(project_kernel, variants, keep, len(into)),
        grid=(count // tile,),
        in_specs=[
            pl.BlockSpec((tile, width), lambda i: (first + i, 0)),
            resident((variants, width)),
            resident((1, width)),
            resident(weight.shape),
        ]
        + [ANY] * len(into),
        out_specs=out_specs,
        out_shape=out_shape,
        input_output_aliases={4 + n: n for n in range(len(into))},
        scratch_shapes=[
            pltpu.VMEM((width, 3 * head), BF16),
            pltpu.VMEM((variants, tile, width), BF16),
        ],
        cost_estimate=pl.CostEstimate(
            flops=2 * variants * count * width * 3 * head,
            bytes_accessed=2 * count * width * (2 if keep else 1) + 6 * width * head,
            transcendentals=0,
        ),
    )(noisy, shifts, gain, weight, *into)


def rope_rows(raw, gain, cosine, sine):
    inverse = lax.rsqrt(jnp.mean(raw * raw, axis=-1, keepdims=True) + norm_eps)
    normed = raw * inverse * gain
    return (normed * cosine + rotate_half(normed) * sine).astype(BF16)


def softmax_rows(query, key, scale):
    exponent = jnp.exp(contract(query, key, 1, 1) * scale)
    return exponent / jnp.sum(exponent, axis=-1, keepdims=True)


def attend_kernel(variants, qkv_ref, gain_ref, cos_ref, sin_ref, out_ref, *refs):
    keys, values = refs[-2:]
    saves = refs[:-2]
    head = out_ref.shape[1]
    tile = out_ref.shape[0]
    scale = head ** (-0.5)
    i = pl.program_id(0)

    @pl.when(i == 0)
    def _():
        for v in range(variants):
            keys[v] = rope_rows(
                qkv_ref[v, :, head : 2 * head], gain_ref[1:2, :], cos_ref[...], sin_ref[...]
            )
            values[v] = qkv_ref[v, :, 2 * head :].astype(BF16)
        if saves:
            saves[1][...] = keys[0]
            saves[2][...] = values[0]

    at = pl.ds(pl.multiple_of(i * tile, tile), tile)
    results = []
    for v in range(variants):
        query = rope_rows(qkv_ref[v, at, :head], gain_ref[0:1, :], cos_ref[at, :], sin_ref[at, :])
        if saves:
            saves[0][...] = query
        prob = softmax_rows(query, keys[v], scale).astype(BF16)
        results.append(dot(prob, values[v]).astype(BF16))
    if variants == 1:
        out_ref[...] = results[0]
    else:
        guided = guidance * results[0].astype(F32) - (guidance - 1.0) * results[1].astype(F32)
        out_ref[...] = guided.astype(BF16)


def attend(qkv, gains, cosine, sine, keep):
    variants, length, triple = qkv.shape
    head = triple // 3
    tile = min(256, length)
    count = 4 if keep else 1
    row = pl.BlockSpec((tile, head), lambda i: (i, 0))
    whole = pl.BlockSpec((length, head), lambda i: (0, 0))
    return pl.pallas_call(
        functools.partial(attend_kernel, variants),
        grid=(length // tile,),
        in_specs=[
            resident(qkv.shape),
            resident(gains.shape),
            resident(cosine.shape),
            resident(sine.shape),
        ],
        out_specs=[row, row, whole, whole][:count],
        out_shape=[jax.ShapeDtypeStruct((length, head), BF16)] * count,
        scratch_shapes=[
            pltpu.VMEM((variants, length, head), BF16),
            pltpu.VMEM((variants, length, head), BF16),
        ],
        cost_estimate=pl.CostEstimate(
            flops=16 * variants * length * length * head,
            bytes_accessed=4 * variants * length * triple,
            transcendentals=variants * length * length,
        ),
    )(qkv, gains, cosine, sine)


class Plan:
    def __init__(self):
        self.operands = []
        self.chunks = []

    def add(self, array):
        self.operands.append(array)
        return len(self.operands) - 1


def fetch(chunk, refs, target, sems, place, along):
    copies = []
    for n, (op, lead, js, jb) in enumerate(chunk):
        source = refs[op]
        for index in lead:
            source = source.at[index]
        head = source.shape[along]
        first = pl.multiple_of(place(js, jb) * head, head)
        spot = (pl.ds(first, head), slice(None)) if along == 0 else (slice(None), pl.ds(first, head))
        copies.append(pltpu.make_async_copy(source, target.at[spot], sems.at[n]))
    return copies


def post_kernel(attn_plan, plan, seqs, n_attn, n_out, scal, noise_ref, *refs):
    attn_refs, refs = refs[:n_attn], refs[n_attn:]
    out_refs, refs = refs[:n_out], refs[n_out:]
    noisy_ref, target_ref, shift_ref, term_ref, grad_ref, part_ref = refs[:6]
    heads, weights, attn_sems, sems = refs[6:]
    i = pl.program_id(0)
    seq, branch = scal[0], scal[1]

    def place(js, jb):
        return (branch ^ jb) * seqs + (seq ^ js)

    def chunk_copies(k):
        return fetch(plan[k], out_refs, weights.at[k % 2], sems.at[k % 2], place, 0)

    @pl.when(i == 0)
    def _():
        copies = fetch(attn_plan, attn_refs, heads, attn_sems, place, 1)
        for copy in copies + chunk_copies(0):
            copy.start()
        for copy in copies:
            copy.wait()
        grad_ref[...] = jnp.zeros_like(grad_ref)

    for k in range(len(plan)):
        @pl.when(i == k)
        def _():
            if k + 1 < len(plan):
                for copy in chunk_copies(k + 1):
                    copy.start()
            for copy in chunk_copies(k):
                copy.wait()

    slot = i % 2
    noise = noise_ref[0]
    head = heads.shape[1] // (plan_heads(plan))
    own = pl.ds(pl.multiple_of(branch * (seqs * head), head), seqs * head)
    term = dot(heads[...], weights[slot])
    term_ref[0] = term
    latent = noisy_ref[...].astype(F32)
    fake_pred = latent - noise * (latent + shift_ref[...] + term)
    cotangent = (-noise * (fake_pred - target_ref[...].astype(F32)) / 64.0).astype(BF16)
    grad_ref[...] += contract(cotangent, weights[slot, own, :], 1, 1)
    part_ref[0] = contract(heads[:, own], cotangent, 0, 0).astype(BF16)


def plan_heads(plan):
    return len(plan[0])


def post(attn, out, scal, noise, noisy, target, shift, seqs, head):
    rows = target.shape[0]
    total = plan_heads(out.chunks)
    cols = out.operands[0].shape[-1]
    count = len(out.chunks)
    n_attn, n_out = len(attn.operands), len(out.operands)
    return pl.pallas_call(
        functools.partial(post_kernel, attn.chunks[0], out.chunks, seqs, n_attn, n_out),
        grid_spec=pltpu.PrefetchScalarGridSpec(
            num_scalar_prefetch=1,
            grid=(count,),
            in_specs=[SMEM]
            + [ANY] * (n_attn + n_out)
            + [
                pl.BlockSpec((rows, cols), lambda i, s: (s[0], s[2 + i])),
                pl.BlockSpec((rows, cols), lambda i, s: (0, s[2 + i])),
                pl.BlockSpec((1, cols), lambda i, s: (0, s[2 + i])),
            ],
            out_specs=[
                pl.BlockSpec((1, rows, cols), lambda i, s: (i, 0, 0)),
                pl.BlockSpec((rows, seqs * head), lambda i, s: (0, 0)),
                pl.BlockSpec((1, seqs * head, cols), lambda i, s: (i, 0, 0)),
            ],
            scratch_shapes=[
                pltpu.VMEM((rows, total * head), BF16),
                pltpu.VMEM((2, total * head, cols), BF16),
                pltpu.SemaphoreType.DMA((total,)),
                pltpu.SemaphoreType.DMA((2, total)),
            ],
        ),
        out_shape=[
            jax.ShapeDtypeStruct((count, rows, cols), F32),
            jax.ShapeDtypeStruct((rows, seqs * head), F32),
            jax.ShapeDtypeStruct((count, seqs * head, cols), BF16),
        ],
        cost_estimate=pl.CostEstimate(
            flops=2 * rows * count * cols * head * (total + 2 * seqs),
            bytes_accessed=count * cols * (2 * total * head + 8 * rows),
            transcendentals=0,
        ),
    )(scal, noise, *attn.operands, *out.operands, noisy, target, shift)


def guide_kernel(attn_plan, plan, seqs, n_attn, n_out, scal, noise_ref, *refs):
    attn_refs, refs = refs[:n_attn], refs[n_attn:]
    out_refs, refs = refs[:n_out], refs[n_out:]
    noisy_ref, target_ref, cond_ref, null_ref, first_ref, second_ref, diff_ref, sum_ref = refs[:8]
    heads, weights, attn_sems, sems = refs[8:]
    i = pl.program_id(0)
    seq, branch = scal[0], scal[1]

    def place(js, jb):
        return (branch ^ jb) * seqs + (seq ^ js)

    def chunk_copies(k):
        return fetch(plan[k], out_refs, weights.at[k % 2], sems.at[k % 2], place, 0)

    @pl.when(i == 0)
    def _():
        copies = fetch(attn_plan, attn_refs, heads, attn_sems, place, 1)
        for copy in copies + chunk_copies(0):
            copy.start()
        for copy in copies:
            copy.wait()
        sum_ref[...] = jnp.zeros_like(sum_ref)

    for k in range(len(plan)):
        @pl.when(i == k)
        def _():
            if k + 1 < len(plan):
                for copy in chunk_copies(k + 1):
                    copy.start()
            for copy in chunk_copies(k):
                copy.wait()

    slot = i % 2
    noise = noise_ref[0]
    guided = dot(heads[...], weights[slot])
    latent = noisy_ref[...].astype(F32)
    cond = latent + cond_ref[...]
    null = latent + null_ref[...]
    real_pred = latent - noise * (guidance * cond - (guidance - 1.0) * null + guided)
    distance = jnp.abs(real_pred - target_ref[...].astype(F32))
    sum_ref[...] += jnp.sum(distance.reshape(-1, 8, distance.shape[1]), axis=0)

    @pl.when(slot == 0)
    def _():
        diff_ref[...] = (latent - noise * (cond + first_ref[0])) - real_pred

    @pl.when(slot == 1)
    def _():
        diff_ref[...] = (latent - noise * (cond + second_ref[0])) - real_pred


def guide(attn, out, scal, noise, noisy, target, cond, null, first, second, seqs, head):
    rows, width = target.shape
    total = plan_heads(out.chunks)
    cols = out.operands[0].shape[-1]
    count = len(out.chunks)
    n_attn, n_out = len(attn.operands), len(out.operands)
    return pl.pallas_call(
        functools.partial(guide_kernel, attn.chunks[0], out.chunks, seqs, n_attn, n_out),
        grid_spec=pltpu.PrefetchScalarGridSpec(
            num_scalar_prefetch=1,
            grid=(count,),
            in_specs=[SMEM]
            + [ANY] * (n_attn + n_out)
            + [
                pl.BlockSpec((rows, cols), lambda i, s: (s[0], s[2 + i])),
                pl.BlockSpec((rows, cols), lambda i, s: (0, s[2 + i])),
                pl.BlockSpec((1, cols), lambda i, s: (0, s[2 + i])),
                pl.BlockSpec((1, cols), lambda i, s: (0, s[2 + i])),
                pl.BlockSpec((1, rows, cols), lambda i, s: (i // 2, 0, 0)),
                pl.BlockSpec((1, rows, cols), lambda i, s: (i // 2, 0, 0)),
            ],
            out_specs=[
                pl.BlockSpec((rows, cols), lambda i, s: (0, s[2 + i])),
                pl.BlockSpec((8, cols), lambda i, s: (0, 0)),
            ],
            scratch_shapes=[
                pltpu.VMEM((rows, total * head), BF16),
                pltpu.VMEM((2, total * head, cols), BF16),
                pltpu.SemaphoreType.DMA((total,)),
                pltpu.SemaphoreType.DMA((2, total)),
            ],
        ),
        out_shape=[jax.ShapeDtypeStruct((rows, width), F32), jax.ShapeDtypeStruct((8, cols), F32)],
        cost_estimate=pl.CostEstimate(
            flops=2 * rows * width * head * total,
            bytes_accessed=width * (2 * total * head + 12 * rows),
            transcendentals=0,
        ),
    )(scal, noise, *attn.operands, *out.operands, noisy, target, cond, null, first, second)


def backward_kernel(
    q_ref, k_ref, v_ref, go_ref, qkv_ref, gain_ref, cos_ref, sin_ref, out_ref, key_sum, value_sum
):
    tile, head = q_ref.shape
    scale = head ** (-0.5)
    i = pl.program_id(0)
    at = pl.ds(pl.multiple_of(i * tile, tile), tile)

    @pl.when(i == 0)
    def _():
        key_sum[...] = jnp.zeros_like(key_sum)
        value_sum[...] = jnp.zeros_like(value_sum)

    def unroll(raw, grad_rot, gain, cosine, sine):
        grad_normed = grad_rot * cosine + rotate_back(grad_rot * sine)
        inverse = lax.rsqrt(jnp.mean(raw * raw, axis=-1, keepdims=True) + norm_eps)
        scaled = gain * grad_normed
        mean = jnp.mean(scaled * raw, axis=-1, keepdims=True)
        return inverse * scaled - raw * inverse * inverse * inverse * mean

    probability = softmax_rows(q_ref[...], k_ref[...], scale)
    grad_prob = contract(go_ref[...], v_ref[...], 1, 1)
    inner = jnp.sum(grad_prob * probability, axis=-1, keepdims=True)
    grad_score = (probability * (grad_prob - inner) * scale).astype(BF16)
    grad_query = unroll(
        qkv_ref[0, at, :head],
        dot(grad_score, k_ref[...]),
        gain_ref[0:1, :],
        cos_ref[at, :],
        sin_ref[at, :],
    )
    out_ref[:head, at] = grad_query.T.astype(BF16)
    key_sum[...] += contract(grad_score, q_ref[...], 0, 0)
    value_sum[...] += contract(probability.astype(BF16), go_ref[...], 0, 0)

    @pl.when(i == pl.num_programs(0) - 1)
    def _():
        grad_key = unroll(
            qkv_ref[0, :, head : 2 * head],
            key_sum[...],
            gain_ref[1:2, :],
            cos_ref[...],
            sin_ref[...],
        )
        out_ref[head : 2 * head, :] = grad_key.T.astype(BF16)
        out_ref[2 * head :, :] = value_sum[...].T.astype(BF16)


def backward(query, key, value, grad_attn, qkv, gains, cosine, sine):
    length, head = query.shape
    tile = min(256, length)
    row = pl.BlockSpec((tile, head), lambda i: (i, 0))
    return pl.pallas_call(
        backward_kernel,
        grid=(length // tile,),
        in_specs=[
            row,
            resident((length, head)),
            resident((length, head)),
            row,
            resident(qkv.shape),
            resident(gains.shape),
            resident(cosine.shape),
            resident(sine.shape),
        ],
        out_specs=pl.BlockSpec((3 * head, length), lambda i: (0, 0)),
        out_shape=jax.ShapeDtypeStruct((3 * head, length), BF16),
        scratch_shapes=[pltpu.VMEM((length, head), F32), pltpu.VMEM((length, head), F32)],
        cost_estimate=pl.CostEstimate(
            flops=20 * length * length * head,
            bytes_accessed=12 * length * head,
            transcendentals=length * length,
        ),
    )(query, key, value, grad_attn, qkv, gains, cosine, sine)


def weight_kernel(scal, grad_ref, hidden_ref, out_ref):
    out_ref[0] = dot(grad_ref[...], hidden_ref[...]).astype(BF16)


def weight_grad(grads, hidden, blocks, cols):
    features, length = grads.shape
    count = blocks.shape[0]
    parts = 2
    tile = cols // parts
    return pl.pallas_call(
        weight_kernel,
        grid_spec=pltpu.PrefetchScalarGridSpec(
            num_scalar_prefetch=1,
            grid=(count, parts),
            in_specs=[
                pl.BlockSpec((features, length), lambda i, p, s: (0, 0)),
                pl.BlockSpec((length, tile), lambda i, p, s: (0, s[i] * parts + p)),
            ],
            out_specs=pl.BlockSpec((1, features, tile), lambda i, p, s: (i, 0, p)),
        ),
        out_shape=jax.ShapeDtypeStruct((count, features, cols), BF16),
        cost_estimate=pl.CostEstimate(
            flops=2 * count * cols * features * length,
            bytes_accessed=2 * count * cols * (length + features),
            transcendentals=0,
        ),
    )(blocks, grads, hidden)


def spread_heads(value, axis, order, which):
    held, orders = [value], list(order)
    for d in range(1, lax.axis_size(axis)):
        held.append(move(value, axis, d))
        orders += [(js ^ d, jb) if which == 0 else (js, jb ^ d) for js, jb in order]
    return held, orders


def gather_out(weight):
    size = lax.axis_size("rep")
    cols = weight.shape[1] // size
    half = cols // 2
    near, far = 1, [bit for bit in bits_of(size) if bit > 1]
    mine = lax.dynamic_slice_in_dim(weight, lax.axis_index("rep") * cols, cols, 1)[None]
    first, second = Plan(), Plan()
    held, base = spread_heads(mine, "branch", [(0, 0)], 1)
    value = jnp.concatenate([v[:, :, :half] for v in held], axis=0)
    others, order = spread_heads(value, "seq", base, 0)
    pieces = [jnp.concatenate(others, axis=0)]
    for bit in far:
        pieces += [move(piece, "rep", bit) for piece in pieces]
    pieces += [move(piece, "rep", near) for piece in pieces]
    for piece in pieces:
        op = first.add(piece)
        first.chunks.append([(op, (n,), js, jb) for n, (js, jb) in enumerate(order)])

    value, order = jnp.concatenate([v[:, :, half:] for v in held], axis=0)[None], base
    for bit in far:
        value = jnp.concatenate([value, move(value, "rep", bit)], axis=0)
    held = [(value, 0)]
    for bit in bits_of(lax.axis_size("seq")):
        held += [(move(v, "seq", bit), js ^ bit) for v, js in held]
    groups = [held, [(move(v, "rep", near), js) for v, js in held]]
    for group in groups:
        ops = [(second.add(v), js) for v, js in group]
        for q in range(value.shape[0]):
            second.chunks.append(
                [(op, (q, n), js, jb) for op, js in ops for n, (_, jb) in enumerate(order)]
            )
    return first, second


def gather_heads(attended, rows):
    seqs = lax.axis_size("seq")
    mine = lax.axis_index("seq")

    def share(d):
        return lax.dynamic_slice_in_dim(attended, (mine ^ d) * rows, rows, 0)

    held = [share(0)] + [move(share(d), "seq", d) for d in range(1, seqs)]
    value, order = jnp.stack(held), [(d, 0) for d in range(seqs)]
    plan, chunk = Plan(), []
    branch_bits = bits_of(lax.axis_size("branch"))
    for bit in branch_bits[:-1]:
        value = jnp.concatenate([value, move(value, "branch", bit)], axis=0)
        order = order + [(js, jb ^ bit) for js, jb in order]
    op = plan.add(value)
    chunk = [(op, (n,), js, jb) for n, (js, jb) in enumerate(order)]
    for bit in branch_bits[-1:]:
        op = plan.add(move(value, "branch", bit))
        chunk += [(op, (n,), js, jb ^ bit) for n, (js, jb) in enumerate(order)]
    plan.chunks.append(chunk)
    return plan


def body(
    noisy,
    generated,
    caption,
    null_caption,
    caption_drop,
    timestep,
    window_start,
    teacher_qkv,
    teacher_out,
    teacher_gain,
    teacher_qk_gain,
    critic_qkv,
    critic_out,
    critic_gain,
    critic_qk_gain,
):
    length, width = noisy.shape[1:]
    head = critic_out.shape[0]
    seqs, reps = lax.axis_size("seq"), lax.axis_size("rep")
    seq, rep, branch = lax.axis_index("seq"), lax.axis_index("rep"), lax.axis_index("branch")
    rows, cols = length // seqs, width // reps
    fraction = (timestep.astype(F32) + 1.0) / 1001.0
    noise = 5.0 * fraction / (1.0 + 4.0 * fraction)
    used_caption = jnp.where(caption_drop[0] == 1, null_caption, caption[0])
    cond_shift = used_caption.astype(F32)[None, :]
    null_shift = null_caption.astype(F32)[None, :]
    both_shift = jnp.concatenate([cond_shift, null_shift], axis=0)
    latent = noisy[0]
    target = generated[0]

    critic_first, critic_second = gather_out(critic_out)
    cosine, sine = rope_tables(window_start[0], length)
    fake_qkv, hidden = project(latent, cond_shift, critic_gain[None], critic_qkv, True, 0, length)
    fake_attn, fake_q, fake_k, fake_v = attend(fake_qkv, critic_qk_gain, cosine, sine, True)
    fake_plan = gather_heads(fake_attn, rows)
    teacher_first, teacher_second = gather_out(teacher_out)
    half = length // 2
    both_qkv = ()
    for start in (0, half):
        both_qkv = project(
            latent, both_shift, teacher_gain[None], teacher_qkv, False, start, half, into=both_qkv
        )
    (both_qkv,) = both_qkv
    (guided_attn,) = attend(both_qkv, teacher_qk_gain, cosine, sine, False)
    guided_plan = gather_heads(guided_attn, rows)

    far = [bit for bit in bits_of(reps) if bit > 1]
    chunks = [0]
    for bit in far:
        chunks += [j ^ bit for j in chunks]
    chunks += [j ^ 1 for j in chunks]
    order = jnp.array(chunks, jnp.int32) ^ rep
    base = jnp.stack([seq, branch]).astype(jnp.int32)
    first_scal = jnp.concatenate([base, order * 2])
    second_scal = jnp.concatenate([base, order * 2 + 1])
    all_scal = jnp.concatenate([base, (order[:, None] * 2 + jnp.arange(2)[None]).reshape(-1)])
    first_term, first_grad, first_part = post(
        fake_plan, critic_first, first_scal, noise, latent, target, cond_shift, seqs, head
    )
    second_term, second_grad, second_part = post(
        fake_plan, critic_second, second_scal, noise, latent, target, cond_shift, seqs, head
    )

    grad_all = (first_grad + second_grad).astype(BF16)

    def grad_block(d):
        return lax.dynamic_slice_in_dim(grad_all, (seq ^ d) * head, head, 1)

    grad_attn = jnp.zeros((length, head), BF16)
    for d in range(seqs):
        piece = move(grad_block(d), "seq", d) if d else grad_block(0)
        grad_attn = lax.dynamic_update_slice(grad_attn, piece, ((seq ^ d) * rows, 0))

    grads = backward(fake_q, fake_k, fake_v, grad_attn, fake_qkv, critic_qk_gain, cosine, sine)
    kept = len(chunks) // 2
    sent = weight_grad(grads, hidden, order[kept:], cols)
    mine = weight_grad(grads, hidden, order[:kept], cols)

    def reduce_rep(mine, sent):
        moved = move(sent, "rep", 1)
        value = mine.astype(F32) + moved.astype(F32)
        for bit in far[::-1]:
            split = value.shape[0] // 2
            moved = move(value[split:].astype(BF16), "rep", bit)
            value = value[:split] + moved.astype(F32)
        return value[0]

    proj_sum = reduce_rep(mine, sent)
    proj_grad = jnp.transpose(proj_sum.reshape(3, head, cols), (0, 2, 1))

    parts = jnp.concatenate([first_part, second_part], axis=2)
    out_sum = reduce_rep(parts[:kept], parts[kept:])
    out_grad = lax.dynamic_slice_in_dim(out_sum, seq * head, head, 0)
    for d in range(1, seqs):
        block = lax.dynamic_slice_in_dim(out_sum, (seq ^ d) * head, head, 0).astype(BF16)
        out_grad += move(block, "seq", d).astype(F32)

    teacher_plan = Plan()
    shift_ops = len(teacher_first.operands)
    teacher_plan.operands = teacher_first.operands + teacher_second.operands
    for one, two in zip(teacher_first.chunks, teacher_second.chunks):
        teacher_plan.chunks.append(one)
        teacher_plan.chunks.append([(op + shift_ops, lead, js, jb) for op, lead, js, jb in two])
    diff, partial = guide(
        guided_plan,
        teacher_plan,
        all_scal,
        noise,
        latent,
        target,
        cond_shift,
        null_shift,
        first_term,
        second_term,
        seqs,
        head,
    )
    total = jnp.broadcast_to(jnp.sum(partial), (8, 128))
    total = total + sum(move(total, "seq", d) for d in range(1, seqs))
    spread = total[0, 0] / (length * width)
    result = (diff / (spread + 1e-05)).astype(BF16)
    return result[None], proj_grad, out_grad


def solution(mesh):
    in_specs = (
        P("rep", None, None),
        P("rep", "seq", None),
        P("rep", None),
        P(),
        P("rep"),
        P("rep"),
        P("rep"),
        P(None, None, ("branch", "seq")),
        P(("branch", "seq"), None),
        P(),
        P(None, ("branch", "seq")),
        P(None, None, ("branch", "seq")),
        P(("branch", "seq"), None),
        P(),
        P(None, ("branch", "seq")),
    )
    out_specs = (
        P("rep", "seq", None),
        P(None, "rep", ("branch", "seq")),
        P(("branch", "seq"), "rep"),
    )
    return jax.shard_map(
        body,
        mesh=mesh,
        in_specs=in_specs,
        out_specs=out_specs,
        check_vma=False,
    )
```

time: 821 us -> 335 us (0.41)
  waiting for transfers between devices: 584 us -> 96 us
  Pallas kernels: 0 us -> 143 us
  matrix products: 91.8 us -> 0 us
  other arithmetic: 90.4 us -> 27.3 us
  starting transfers between devices: 0.25 us -> 35.2 us
  between operations: 19.2 us -> 3.72 us
    psum x2 -> x0, waiting for transfers between devices: 528 us -> none  [the longest x1 339 us: body(): lax.psum(fake_local.astype(jnp.bfloat16), ('branch', 'seq'))]
    pallas_call x0 -> x11, Pallas kernels: none -> 143 us  [the longest x3 56.6 us: project(): pl.pallas_call(functools.partial(project_kernel, variants, keep, len(into...]
    ppermute x0 -> x35, waiting for transfers between devices: none -> 96 us  [move(): return lax.ppermute(value, axis, swap(lax.axis_size(axis), bit))]
    dot_general x14 -> x0, matrix products: 70.5 us -> none  [the longest x3 16.9 us: head_forward(): jnp.einsum('bqhe,bkhe->bhqk', rope_query, rope_key, preferred_element_typ...]
    convert_element_type x6 -> x1, other arithmetic: 44.7 us -> 0.07 us  [body(): grad_all = (first_grad + second_grad).astype(BF16)]
    ppermute x0 -> x35, starting transfers between devices: none -> 35.2 us  [move(): return lax.ppermute(value, axis, swap(lax.axis_size(axis), bit))]
    all_gather x1 -> x0, waiting for transfers between devices: 30.1 us -> none  [body(): lax.all_gather(generated, 'seq', axis=1, tiled=True).astype(jnp.float32)]
    reduce_scatter x3 -> x0, waiting for transfers between devices: 25.3 us -> none  [the longest x1 25.3 us: body(): lax.psum_scatter(head_backward(critic_normed, grad_attn, saved_state, cri...]
  transfers between devices with their start and end apart: 6 -> 35, of which waited for: 4 -> 9; matrix products, arithmetic and copies ran while one was open for 21% -> 14% of each run, Pallas kernels for 0% -> 43%
where the time goes in v1:
time: 335 us; the launch traced here: 334 us
  Pallas kernels  143 us (43%)
  waiting for transfers between devices  96 us (29%)
  starting transfers between devices  35.2 us (11%)
  local copies, waits for them, and re-layouts  28.7 us (9%)
  other arithmetic  27.3 us (8%)
  between operations  3.72 us (1%)
    ppermute x35, waiting for transfers between devices, move(): return lax.ppermute(value, axis, swap(lax.axis_size(axis), bit))  96 us
    pallas_call x3, Pallas kernels, project(): pl.pallas_call(functools.partial(project_kernel, variants, keep, len(into...  56.6 us
    ppermute x35, starting transfers between devices, move(): return lax.ppermute(value, axis, swap(lax.axis_size(axis), bit))  35.2 us
    pallas_call x2, Pallas kernels, post(): pl.pallas_call(functools.partial(post_kernel, attn.chunks[0], out.chunks,...  24.2 us
    pallas_call x1, Pallas kernels, guide(): pl.pallas_call(functools.partial(guide_kernel, attn.chunks[0], out.chunks...  24.2 us
    pallas_call x2, Pallas kernels, attend(): pl.pallas_call(functools.partial(attend_kernel, variants), grid=(length /...  15.7 us
    pallas_call x2, Pallas kernels, weight_grad(): pl.pallas_call(weight_kernel, grid_spec=pltpu.PrefetchScalarGridSpec(num_...  14 us
    slice x8, local copies, waits for them, and re-layouts, gather_out(): v[:, :, half:]  8.77 us
  transfers between devices with their start and end apart: 35, of which 9 were waited for; matrix products, arithmetic and copies ran while one was open for 14% of the time, Pallas kernels for 43%

profile of v1, /device:TPU:0, one launch (start us, length us, event | category | flops | bytes accessed | tf_op | source)
XLA Modules:
  0.0 334.3 jit_solution(2006518570972970127)
XLA Ops:
  0.7 1.3 copy-done
  2.0 3.1 collective-permute-start.17
  5.1 2.6 collective-permute-start.18
  7.7 1.0 dynamic-slice_bitcast_fusion.1
  8.7 1.0 collective-permute-start.3
  9.7 3.5 %collective-permute-start.4 = (bf16[1,128,1280]{2,1,0:T(8,128)(2,1)S(1)}, bf16[1,128,1280]{2,1,0:T(8,128)(2,1)}, u32[]{:S(2)}, u32[]{:S(2)}) collective-permute-start(bf16[1,128,1280]{2,1,0:T(8,128)(2,1)S(1)} %dynamic-slice_bitcast_fusion.1), channel_id=1, source_target_pairs={{0,16},{8,24},{16,0},{24,8},{1,17},{9,25},{17,1},{25,9},{2,18},{10... | collective-permute-start | bytes 983048 | tf_op jit(solution)/shard_map/ppermute | solution.py:29
  13.9 0.8 fusion.12
  16.8 17.0 %shard_map.175.refs_0_ = f32[2,1024,384]{2,1,0:T(8,128)} custom-call(bf16[1024,5120]{1,0:T(8,128)(2,1)} %bitcast.35, f32[2,5120]{1,0:T(2,128)} %pad_maximum_fusion.9.shift_ref, f32[1,5120]{1,0:T(1,128)} %bitcast.57, bf16[3,5120,128]{2,1,0:T(8,128)(2,1)} %weight_ref.4), custom_call_target="tpu_custom_call" | custom-call | flops 4026531840 | bytes 9175040 | tf_op jit(solution)/shard_map/pallas_call | solution.py:122
  33.8 17.0 %shard_map.176.qkv_ref = f32[2,1024,384]{2,1,0:T(8,128)} custom-call(bf16[1024,5120]{1,0:T(8,128)(2,1)} %bitcast.36, f32[2,5120]{1,0:T(2,128)} %pad_maximum_fusion.9.shift_ref, f32[1,5120]{1,0:T(1,128)} %bitcast.58, bf16[3,5120,128]{2,1,0:T(8,128)(2,1)} %weight_ref.4, f32[2,1024,384]{2,1,0:T(8,128)} %shard_map.175.refs_0_), custom_call_target="tpu_custom_call", output_to_operand_aliasing={{}: (4, {})} | custom-call | flops 4026531840 | bytes 9175040 | tf_op jit(solution)/shard_map/pallas_call | solution.py:122
  50.9 22.5 %shard_map.178 = (f32[1,1024,384]{2,1,0:T(8,128)}, bf16[1024,5120]{1,0:T(8,128)(2,1)}) custom-call(bf16[1024,5120]{1,0:T(8,128)(2,1)} %bitcast.37, f32[1,5120]{1,0:T(1,128)} %bitcast.51, f32[1,5120]{1,0:T(1,128)} %bitcast.59, bf16[3,5120,128]{2,1,0:T(8,128)(2,1)} %weight_ref.5), custom_call_target="tpu_custom_call" | custom-call | flops 4026531840 | bytes 24903680 | tf_op jit(solution)/shard_map/pallas_call | solution.py:122
  73.9 2.9 fusion.1
  76.8 0.7 fusion.9
  79.0 1.8 collective-permute-start.24
  80.8 6.3 %shard_map.179 = (bf16[1024,128]{1,0:T(8,128)(2,1)}, bf16[1024,128]{1,0:T(8,128)(2,1)}, bf16[1024,128]{1,0:T(8,128)(2,1)}, bf16[1024,128]{1,0:T(8,128)(2,1)}) custom-call(f32[1,1024,384]{2,1,0:T(8,128)} %get-tuple-element.17.qkv_ref, f32[2,128]{1,0:T(2,128)} %gain_ref.5, f32[1024,128]{1,0:T(8,128)} %get-tuple-element.32.cos_ref, ...), custom_call_target="tpu_custom_call" | custom-call | flops 2147483648 | bytes 1572864 | tf_op jit(solution)/shard_map/pallas_call | solution.py:199
  87.1 1.6 dynamic-slice_bitcast_fusion.2
  88.7 0.9 pad_maximum_fusion.3
  89.7 1.5 collective-permute-start.20
  91.2 9.4 %shard_map.177 = bf16[1024,128]{1,0:T(8,128)(2,1)} custom-call(f32[2,1024,384]{2,1,0:T(8,128)} %shard_map.176.qkv_ref, f32[2,128]{1,0:T(2,128)} %gain_ref.3, f32[1024,128]{1,0:T(8,128)} %get-tuple-element.32.cos_ref, f32[1024,128]{1,0:T(8,128)} %get-tuple-element.31.sin_ref), custom_call_target="tpu_custom_call" | custom-call | flops 4294967296 | bytes 3145728 | tf_op jit(solution)/shard_map/pallas_call | solution.py:199
  101.2 6.3 %collective-permute-done.14 = bf16[512,128]{1,0:T(8,128)(2,1)S(1)} collective-permute-done((bf16[512,128]{1,0:T(8,128)(2,1)}, bf16[512,128]{1,0:T(8,128)(2,1)S(1)}, u32[]{:S(2)}, u32[]{:S(2)}) %collective-permute-start.14) | collective-permute-done | bytes 131104 | tf_op jit(solution)/shard_map/ppermute | solution.py:29
  107.5 1.5 collective-permute-start.25
  109.5 2.0 constant_dynamic-update-slice_fusion.5.refs_2_
  112.0 1.7 fusion.13
  113.7 1.8 fusion.14
  115.4 1.7 fusion.15
  117.2 1.6 collective-permute-start.10
  119.4 18.7 %collective-permute-done = bf16[512,128]{1,0:T(8,128)(2,1)S(1)} collective-permute-done((bf16[512,128]{1,0:T(8,128)(2,1)S(1)}, bf16[512,128]{1,0:T(8,128)(2,1)S(1)}, u32[]{:S(2)}, u32[]{:S(2)}) %collective-permute-start) | collective-permute-done | bytes 131104 | tf_op jit(solution)/shard_map/ppermute | solution.py:29
  138.7 0.9 pad_maximum_fusion.2
  139.6 1.5 collective-permute-start.6
  141.1 12.2 %collective-permute-done.10 = bf16[1,4,128,640]{3,2,1,0:T(8,128)(2,1)} collective-permute-done((bf16[1,4,128,640]{3,2,1,0:T(8,128)(2,1)S(1)}, bf16[1,4,128,640]{3,2,1,0:T(8,128)(2,1)}, u32[]{:S(2)}, u32[]{:S(2)}) %collective-permute-start.10) | collective-permute-done | bytes 655392 | tf_op jit(solution)/shard_map/ppermute | solution.py:29
  153.9 1.0 pad_maximum_fusion.6.refs_0_
  154.9 1.8 collective-permute-done.6
  156.7 1.6 collective-permute-start.16
  160.4 2.0 constant_dynamic-update-slice_fusion.refs_2_
  162.4 2.3 pad_maximum_fusion.refs_6_
  164.7 17.1 %collective-permute-done.16.refs_1_ = bf16[4,512,128]{2,1,0:T(8,128)(2,1)S(1)} collective-permute-done((bf16[4,512,128]{2,1,0:T(8,128)(2,1)S(1)}, bf16[4,512,128]{2,1,0:T(8,128)(2,1)S(1)}, u32[]{:S(2)}, u32[]{:S(2)}) %collective-permute-start.16) | collective-permute-done | bytes 524320 | tf_op jit(solution)/shard_map/ppermute | solution.py:29
  182.3 1.1 collective-permute-start.11
  183.9 12.1 %shard_map.181 = (f32[4,512,640]{2,1,0:T(8,128)}, f32[512,256]{1,0:T(8,128)}, bf16[4,256,640]{2,1,0:T(8,128)(2,1)}) custom-call(s32[6]{0:T(128)} %pad_add_fusion.3.scal, f32[1]{0:T(128)S(6)} %div.47.noise_ref, bf16[4,512,128]{2,1,0:T(8,128)(2,1)} %copy-done.6, bf16[4,512,128]{2,1,0:T(8,128)(2,1)} %copy-done.8, bf16[2,4,128,640]{3,2,1,0:T(8,128)(2,1)} %copy-done.5, ...), custom_call_target="tpu_custom_call" | custom-call | flops 4026531840 | bytes 15728640 | tf_op jit(solution)/shard_map/pallas_call | solution.py:300
  196.1 12.1 %shard_map.180 = (f32[4,512,640]{2,1,0:T(8,128)}, f32[512,256]{1,0:T(8,128)}, bf16[4,256,640]{2,1,0:T(8,128)(2,1)}) custom-call(s32[6]{0:T(128)} %pad_add_fusion.1.scal, f32[1]{0:T(128)S(6)} %div.47.noise_ref, bf16[4,512,128]{2,1,0:T(8,128)(2,1)} %copy-done.6, bf16[4,512,128]{2,1,0:T(8,128)(2,1)} %copy-done.8, ...), custom_call_target="tpu_custom_call" | custom-call | flops 4026531840 | bytes 15728640 | tf_op jit(solution)/shard_map/pallas_call | solution.py:300
  208.2 1.5 constant_dynamic-update-slice_fusion.11
  210.1 1.6 copy-done.4
  211.9 0.7 copy-done.15
  212.7 3.0 collective-permute-start.2
  215.9 1.4 collective-permute-start.29
  217.9 20.9 %collective-permute-done.2.refs_1_ = bf16[4,512,128]{2,1,0:T(8,128)(2,1)S(1)} collective-permute-done((bf16[4,512,128]{2,1,0:T(8,128)(2,1)S(1)}, bf16[4,512,128]{2,1,0:T(8,128)(2,1)S(1)}, u32[]{:S(2)}, u32[]{:S(2)}) %collective-permute-start.2) | collective-permute-done | bytes 524320 | tf_op jit(solution)/shard_map/ppermute | solution.py:29
  240.5 0.7 copy-done.20
  241.2 8.7 %shard_map.183.grad_ref = bf16[384,1024]{1,0:T(8,128)(2,1)} custom-call(bf16[1024,128]{1,0:T(8,128)(2,1)} %get-tuple-element.23.q_ref, bf16[1024,128]{1,0:T(8,128)(2,1)} %get-tuple-element.24.k_ref, bf16[1024,128]{1,0:T(8,128)(2,1)} %get-tuple-element.25.v_ref, bf16[1024,128]{1,0:T(8,128)(2,1)} %copy-done.20, f32[1,1024,384]{2,1,0:T(8,128)} %get-tuple-element.17.qkv_ref, ...), custom_call_target="tpu_custom_call" | custom-call | flops 2684354560 | bytes 1572864 | tf_op jit(solution)/shard_map/pallas_call | solution.py:481
  250.0 7.0 %shard_map.185 = bf16[2,384,1280]{2,1,0:T(8,128)(2,1)} custom-call(s32[2]{0:T(128)} %get-tuple-element.66.scal, bf16[384,1024]{1,0:T(8,128)(2,1)} %shard_map.183.grad_ref, bf16[1024,5120]{1,0:T(8,128)(2,1)} %get-tuple-element.28.hidden_ref), custom_call_target="tpu_custom_call" | custom-call | flops 2013265920 | bytes 7208960 | tf_op jit(solution)/shard_map/pallas_call | solution.py:514
  257.0 2.0 convert_add_fusion.1
  259.1 1.5 collective-permute-start.33
  260.7 24.2 %shard_map.182 = (f32[512,5120]{1,0:T(8,128)}, f32[8,640]{1,0:T(8,128)}) custom-call(s32[10]{0:T(128)} %pad_add_fusion.scal, f32[1]{0:T(128)S(6)} %div.47.noise_ref, bf16[4,512,128]{2,1,0:T(8,128)(2,1)} %copy-done.7, bf16[4,512,128]{2,1,0:T(8,128)(2,1)} %copy-done.11, bf16[8,128,640]{2,1,0:T(8,128)(2,1)} %constant_dynamic-update-slice_fusion.refs_2_, ...), custom_call_target="tpu_custom_call" | custom-call | flops 5368709120 | bytes 41943040 | tf_op jit(solution)/shard_map/pallas_call | solution.py:394
  284.8 1.3 reduce_sum.9
  286.8 1.4 collective-permute-start.28
  288.2 2.2 collective-permute-done.28
  292.3 7.0 %shard_map.184 = bf16[2,384,1280]{2,1,0:T(8,128)(2,1)} custom-call(s32[2]{0:T(128)} %get-tuple-element.65.scal, bf16[384,1024]{1,0:T(8,128)(2,1)} %shard_map.183.grad_ref, bf16[1024,5120]{1,0:T(8,128)(2,1)} %get-tuple-element.28.hidden_ref), custom_call_target="tpu_custom_call" | custom-call | flops 2013265920 | bytes 7208960 | tf_op jit(solution)/shard_map/pallas_call | solution.py:514
  299.3 2.4 slice_add_fusion.1
  301.7 2.0 fusion.3
  303.7 1.4 collective-permute-start.34
  305.1 2.0 convert_add_fusion
  307.1 1.0 slice.137
  308.7 3.5 %fusion = bf16[1,512,5120]{2,1,0:T(8,128)(2,1)} fusion(f32[512,5120]{1,0:T(8,128)S(1)} %copy-done.2, f32[]{:T(128)} %bitcast.18), kind=kLoop, calls=%fused_computation.1 | loop fusion | flops 5242880 | bytes 15728644 | tf_op jit(solution)/shard_map/broadcast_in_dim | solution.py:721
  312.7 2.1 bitcast_add_fusion
  314.8 16.3 %collective-permute-done.31 = bf16[1,384,1280]{2,1,0:T(8,128)(2,1)} collective-permute-done((bf16[1,384,1280]{2,1,0:T(8,128)(2,1)}, bf16[1,384,1280]{2,1,0:T(8,128)(2,1)}, u32[]{:S(2)}, u32[]{:S(2)}) %collective-permute-start.31) | collective-permute-done | bytes 983072 | tf_op jit(solution)/shard_map/ppermute | solution.py:29
  331.1 1.4 slice_add_fusion
  332.5 1.8 copy.21
  (128 shorter events, 15.4 us)
Async XLA Ops:
  0.6 1.3 copy-start
  2.0 14.0 %copy-start.22 = (bf16[1,5120]{1,0:T(2,128)(2,1)S(1)}, bf16[1,5120]{1,0:T(2,128)(2,1)}, u32[]{:S(2)}) copy-start(bf16[1,5120]{1,0:T(2,128)(2,1)} %param.18) | copy-start | bytes 30724
  2.0 14.1 %copy-start.23 = (bf16[5120]{0:T(1024)(128)(2,1)S(1)}, bf16[5120]{0:T(1024)(128)(2,1)}, u32[]{:S(2)}) copy-start(bf16[5120]{0:T(1024)(128)(2,1)} %param.19) | copy-start | bytes 30724
  2.0 74.7 %collective-permute-start.17 = (bf16[1,128,1280]{2,1,0:T(8,128)(2,1)S(1)}, bf16[1,128,1280]{2,1,0:T(8,128)(2,1)S(1)}, u32[]{:S(2)}, u32[]{:S(2)}) collective-permute-start(bf16[1,128,1280]{2,1,0:T(8,128)(2,1)S(1)} %dynamic-slice_bitcast_fusion), channel_id=1, source_target_pairs={{0,8},{8,0},{16,24},{24,16},{1,9},{9,1},{17,25},{25,17},{2,10},{10... | collective-permute-start | bytes 983048 | tf_op jit(solution)/shard_map/ppermute | solution.py:29
  5.1 72.4 %collective-permute-start.18 = (bf16[1,128,1280]{2,1,0:T(8,128)(2,1)S(1)}, bf16[1,128,1280]{2,1,0:T(8,128)(2,1)S(1)}, u32[]{:S(2)}, u32[]{:S(2)}) collective-permute-start(bf16[1,128,1280]{2,1,0:T(8,128)(2,1)S(1)} %dynamic-slice_bitcast_fusion), channel_id=1, source_target_pairs={{0,16},{8,24},{16,0},{24,8},{1,17},{9,25},{17,1},{25,9},{2,18},{10... | collective-permute-start | bytes 983048 | tf_op jit(solution)/shard_map/ppermute | solution.py:29
  7.7 70.5 %collective-permute-start.19 = (bf16[1,128,1280]{2,1,0:T(8,128)(2,1)S(1)}, bf16[1,128,1280]{2,1,0:T(8,128)(2,1)S(1)}, u32[]{:S(2)}, u32[]{:S(2)}) collective-permute-start(bf16[1,128,1280]{2,1,0:T(8,128)(2,1)S(1)} %dynamic-slice_bitcast_fusion), channel_id=1, source_target_pairs={{0,24},{8,16},{16,8},{24,0},{1,25},{9,17},{17,9},{25,1},{2,26},{10... | collective-permute-start | bytes 983048 | tf_op jit(solution)/shard_map/ppermute | solution.py:29
  8.7 102.7 %collective-permute-start.3 = (bf16[1,128,1280]{2,1,0:T(8,128)(2,1)S(1)}, bf16[1,128,1280]{2,1,0:T(8,128)(2,1)}, u32[]{:S(2)}, u32[]{:S(2)}) collective-permute-start(bf16[1,128,1280]{2,1,0:T(8,128)(2,1)S(1)} %dynamic-slice_bitcast_fusion.1), channel_id=1, source_target_pairs={{0,8},{8,0},{16,24},{24,16},{1,9},{9,1},{17,25},{25,17},{2,10},{10... | collective-permute-start | bytes 983048 | tf_op jit(solution)/shard_map/ppermute | solution.py:29
  9.7 104.0 %collective-permute-start.4 = (bf16[1,128,1280]{2,1,0:T(8,128)(2,1)S(1)}, bf16[1,128,1280]{2,1,0:T(8,128)(2,1)}, u32[]{:S(2)}, u32[]{:S(2)}) collective-permute-start(bf16[1,128,1280]{2,1,0:T(8,128)(2,1)S(1)} %dynamic-slice_bitcast_fusion.1), channel_id=1, source_target_pairs={{0,16},{8,24},{16,0},{24,8},{1,17},{9,25},{17,1},{25,9},{2,18},{10... | collective-permute-start | bytes 983048 | tf_op jit(solution)/shard_map/ppermute | solution.py:29
  16.1 17.7 %copy-start.18 = (f32[5120]{0:T(1024)}, f32[5120]{0:T(1024)S(1)}, u32[]{:S(2)}) copy-start(f32[5120]{0:T(1024)S(1)} %get-tuple-element.63) | copy-start | bytes 61444
  16.1 17.7 %copy-start.21 = (f32[5120]{0:T(1024)}, f32[5120]{0:T(1024)S(1)}, u32[]{:S(2)}) copy-start(f32[5120]{0:T(1024)S(1)} %get-tuple-element.64) | copy-start | bytes 61444
  76.8 38.7 %collective-permute-start.5 = (bf16[1,128,1280]{2,1,0:T(8,128)(2,1)S(1)}, bf16[1,128,1280]{2,1,0:T(8,128)(2,1)}, u32[]{:S(2)}, u32[]{:S(2)}) collective-permute-start(bf16[1,128,1280]{2,1,0:T(8,128)(2,1)S(1)} %dynamic-slice_bitcast_fusion.1), channel_id=1, source_target_pairs={{0,24},{8,16},{16,8},{24,0},{1,25},{9,17},{17,9},{25,1},{2,26},{10... | collective-permute-start | bytes 983048 | tf_op jit(solution)/shard_map/ppermute | solution.py:29
  79.0 21.6 %collective-permute-start.24 = (bf16[1,4,128,640]{3,2,1,0:T(8,128)(2,1)S(1)}, bf16[1,4,128,640]{3,2,1,0:T(8,128)(2,1)S(1)}, u32[]{:S(2)}, u32[]{:S(2)}) collective-permute-start(bf16[1,4,128,640]{3,2,1,0:T(8,128)(2,1)S(1)} %maximum_bitcast_fusion.1), channel_id=1, source_target_pairs={{0,2},{1,3},{2,0},{3,1},{4,6},{5,7},{6,4},{7,5},{8,10},{9,11},{10,... | collective-permute-start | bytes 1966088 | tf_op jit(solution)/shard_map/ppermute | solution.py:29
  89.7 19.3 %collective-permute-start.20 = (bf16[4,128,640]{2,1,0:T(8,128)(2,1)}, bf16[4,128,640]{2,1,0:T(8,128)(2,1)}, u32[]{:S(2)}, u32[]{:S(2)}) collective-permute-start(bf16[4,128,640]{2,1,0:T(8,128)(2,1)} %pad_maximum_fusion.3), channel_id=1, source_target_pairs={{0,4},{4,0},{1,5},{5,1},{2,6},{6,2},{3,7},{7,3},{8,12},{12,8},{9,1... | collective-permute-start | bytes 1966088 | tf_op jit(solution)/shard_map/ppermute | solution.py:29
  100.6 6.9 %collective-permute-start.14 = (bf16[512,128]{1,0:T(8,128)(2,1)}, bf16[512,128]{1,0:T(8,128)(2,1)S(1)}, u32[]{:S(2)}, u32[]{:S(2)}) collective-permute-start(bf16[512,128]{1,0:T(8,128)(2,1)} %get-tuple-element.60), channel_id=1, source_target_pairs={{0,4},{4,0},{1,5},{5,1},{2,6},{6,2},{3,7},{7,3},{8,12},{12,8},{9,1... | collective-permute-start | bytes 393224 | tf_op jit(solution)/shard_map/ppermute | solution.py:29
  101.2 37.0 %copy-start.5 = (bf16[2,4,128,640]{3,2,1,0:T(8,128)(2,1)}, bf16[2,4,128,640]{3,2,1,0:T(8,128)(2,1)S(1)}, u32[]{:S(2)}) copy-start(bf16[2,4,128,640]{3,2,1,0:T(8,128)(2,1)S(1)} %pad_maximum_fusion.1.refs_2_) | copy-start | bytes 3932164
  107.5 6.2 %copy-start.16 = (bf16[512,128]{1,0:T(8,128)(2,1)}, bf16[512,128]{1,0:T(8,128)(2,1)S(1)}, u32[]{:S(2)}) copy-start(bf16[512,128]{1,0:T(8,128)(2,1)S(1)} %collective-permute-done.14) | copy-start | bytes 393220
  107.5 30.7 %collective-permute-start.25 = (bf16[2,4,128,640]{3,2,1,0:T(8,128)(2,1)S(1)}, bf16[2,4,128,640]{3,2,1,0:T(8,128)(2,1)}, u32[]{:S(2)}, u32[]{:S(2)}) collective-permute-start(bf16[2,4,128,640]{3,2,1,0:T(8,128)(2,1)S(1)} %pad_maximum_fusion.1.refs_2_), channel_id=1, source_target_pairs={{0,4},{4,0},{1,5},{5,1},{2,6},{6,2},{3,7},{7,3},{8,12},{12,8},{9,1... | collective-permute-start | bytes 3932168 | tf_op jit(solution)/shard_map/ppermute | solution.py:29
  109.0 30.6 %collective-permute-start.15 = (bf16[2,512,128]{2,1,0:T(8,128)(2,1)S(1)}, bf16[2,512,128]{2,1,0:T(8,128)(2,1)}, u32[]{:S(2)}, u32[]{:S(2)}) collective-permute-start(bf16[2,512,128]{2,1,0:T(8,128)(2,1)S(1)} %pad_maximum_fusion.8), channel_id=1, source_target_pairs={{0,8},{8,0},{16,24},{24,16},{1,9},{9,1},{17,25},{25,17},{2,10},{10... | collective-permute-start | bytes 786440 | tf_op jit(solution)/shard_map/ppermute | solution.py:29
  111.5 5.7 %copy-start.10 = (bf16[1,128,640]{2,1,0:T(8,128)(2,1)S(1)}, bf16[1,128,640]{2,1,0:T(8,128)(2,1)}, u32[]{:S(2)}) copy-start(bf16[1,128,640]{2,1,0:T(8,128)(2,1)} %get-tuple-element.45) | copy-start | bytes 491524
  111.5 41.9 %collective-permute-start.21 = (bf16[8,128,640]{2,1,0:T(8,128)(2,1)}, bf16[8,128,640]{2,1,0:T(8,128)(2,1)}, u32[]{:S(2)}, u32[]{:S(2)}) collective-permute-start(bf16[8,128,640]{2,1,0:T(8,128)(2,1)} %constant_dynamic-update-slice_fusion.5.refs_2_), channel_id=1, source_target_pairs={{0,2},{1,3},{2,0},{3,1},{4,6},{5,7},{6,4},{7,5},{8,10},{9,11},{10,... | collective-permute-start | bytes 3932168 | tf_op jit(solution)/shard_map/ppermute | solution.py:29
  113.7 5.2 %copy-start.19 = (bf16[1024,128]{1,0:T(8,128)(2,1)S(1)}, bf16[1024,128]{1,0:T(8,128)(2,1)}, u32[]{:S(2)}) copy-start(bf16[1024,128]{1,0:T(8,128)(2,1)} %shard_map.177) | copy-start | bytes 786436
  117.1 24.0 %copy-start.24 = (s32[4]{0:T(128)S(1)}, s32[4]{0:T(128)}, u32[]{:S(2)}) copy-start(s32[4]{0:T(128)} %constant.90.clone) | copy-start | bytes 52
  117.2 36.7 %copy-start.17 = (bf16[512,128]{1,0:T(8,128)(2,1)S(1)}, bf16[512,128]{1,0:T(8,128)(2,1)}, u32[]{:S(2)}) copy-start(bf16[512,128]{1,0:T(8,128)(2,1)} %copy-done.16) | copy-start | bytes 393220
  117.2 36.1 %collective-permute-start.10 = (bf16[1,4,128,640]{3,2,1,0:T(8,128)(2,1)S(1)}, bf16[1,4,128,640]{3,2,1,0:T(8,128)(2,1)}, u32[]{:S(2)}, u32[]{:S(2)}) collective-permute-start(bf16[1,4,128,640]{3,2,1,0:T(8,128)(2,1)S(1)} %maximum_bitcast_fusion), channel_id=1, source_target_pairs={{0,2},{1,3},{2,0},{3,1},{4,6},{5,7},{6,4},{7,5},{8,10},{9,11},{10,... | collective-permute-start | bytes 1966088 | tf_op jit(solution)/shard_map/ppermute | solution.py:29
  118.9 19.3 %collective-permute-start = (bf16[512,128]{1,0:T(8,128)(2,1)S(1)}, bf16[512,128]{1,0:T(8,128)(2,1)S(1)}, u32[]{:S(2)}, u32[]{:S(2)}) collective-permute-start(bf16[512,128]{1,0:T(8,128)(2,1)S(1)} %get-tuple-element.62), channel_id=1, source_target_pairs={{0,4},{4,0},{1,5},{5,1},{2,6},{6,2},{3,7},{7,3},{8,12},{12,8},{9,1... | collective-permute-start | bytes 393224 | tf_op jit(solution)/shard_map/ppermute | solution.py:29
  138.2 22.2 %copy-start.14 = (bf16[512,128]{1,0:T(8,128)(2,1)}, bf16[512,128]{1,0:T(8,128)(2,1)S(1)}, u32[]{:S(2)}) copy-start(bf16[512,128]{1,0:T(8,128)(2,1)S(1)} %collective-permute-done) | copy-start | bytes 393220
  138.2 44.1 %collective-permute-start.26 = (bf16[2,4,128,640]{3,2,1,0:T(8,128)(2,1)S(1)}, bf16[2,4,128,640]{3,2,1,0:T(8,128)(2,1)}, u32[]{:S(2)}, u32[]{:S(2)}) collective-permute-start(bf16[2,4,128,640]{3,2,1,0:T(8,128)(2,1)S(1)} %pad_maximum_fusion.1.refs_2_), channel_id=1, source_target_pairs={{0,1},{1,0},{2,3},{3,2},{4,5},{5,4},{6,7},{7,6},{8,9},{9,8},{10,11... | collective-permute-start | bytes 3932168 | tf_op jit(solution)/shard_map/ppermute | solution.py:29
  138.2 45.2 %collective-permute-start.27 = (bf16[2,4,128,640]{3,2,1,0:T(8,128)(2,1)}, bf16[2,4,128,640]{3,2,1,0:T(8,128)(2,1)}, u32[]{:S(2)}, u32[]{:S(2)}) collective-permute-start(bf16[2,4,128,640]{3,2,1,0:T(8,128)(2,1)} %collective-permute-done.25.refs_3_), channel_id=1, source_target_pairs={{0,1},{1,0},{2,3},{3,2},{4,5},{5,4},{6,7},{7,6},{8,9},{9,8},{10,11... | collective-permute-start | bytes 3932168 | tf_op jit(solution)/shard_map/ppermute | solution.py:29
  139.6 17.0 %collective-permute-start.6 = (bf16[4,128,640]{2,1,0:T(8,128)(2,1)}, bf16[4,128,640]{2,1,0:T(8,128)(2,1)}, u32[]{:S(2)}, u32[]{:S(2)}) collective-permute-start(bf16[4,128,640]{2,1,0:T(8,128)(2,1)} %pad_maximum_fusion.2), channel_id=1, source_target_pairs={{0,4},{4,0},{1,5},{5,1},{2,6},{6,2},{3,7},{7,3},{8,12},{12,8},{9,1... | collective-permute-start | bytes 1966088 | tf_op jit(solution)/shard_map/ppermute | solution.py:29
  153.3 42.8 %collective-permute-start.22 = (bf16[8,128,640]{2,1,0:T(8,128)(2,1)}, bf16[8,128,640]{2,1,0:T(8,128)(2,1)}, u32[]{:S(2)}, u32[]{:S(2)}) collective-permute-start(bf16[8,128,640]{2,1,0:T(8,128)(2,1)} %constant_dynamic-update-slice_fusion.5.refs_2_), channel_id=1, source_target_pairs={{0,1},{1,0},{2,3},{3,2},{4,5},{5,4},{6,7},{7,6},{8,9},{9,8},{10,11... | collective-permute-start | bytes 3932168 | tf_op jit(solution)/shard_map/ppermute | solution.py:29
  153.3 42.8 %collective-permute-start.23 = (bf16[8,128,640]{2,1,0:T(8,128)(2,1)}, bf16[8,128,640]{2,1,0:T(8,128)(2,1)}, u32[]{:S(2)}, u32[]{:S(2)}) collective-permute-start(bf16[8,128,640]{2,1,0:T(8,128)(2,1)} %collective-permute-done.21.refs_3_), channel_id=1, source_target_pairs={{0,1},{1,0},{2,3},{3,2},{4,5},{5,4},{6,7},{7,6},{8,9},{9,8},{10,11... | collective-permute-start | bytes 3932168 | tf_op jit(solution)/shard_map/ppermute | solution.py:29
  154.9 9.8 %copy-start.6 = (bf16[4,512,128]{2,1,0:T(8,128)(2,1)}, bf16[4,512,128]{2,1,0:T(8,128)(2,1)S(1)}, u32[]{:S(2)}) copy-start(bf16[4,512,128]{2,1,0:T(8,128)(2,1)S(1)} %pad_maximum_fusion.6.refs_0_) | copy-start | bytes 1572868
  156.7 25.2 %collective-permute-start.16 = (bf16[4,512,128]{2,1,0:T(8,128)(2,1)S(1)}, bf16[4,512,128]{2,1,0:T(8,128)(2,1)S(1)}, u32[]{:S(2)}, u32[]{:S(2)}) collective-permute-start(bf16[4,512,128]{2,1,0:T(8,128)(2,1)S(1)} %pad_maximum_fusion.6.refs_0_), channel_id=1, source_target_pairs={{0,16},{8,24},{16,0},{24,8},{1,17},{9,25},{17,1},{25,9},{2,18},{10... | collective-permute-start | bytes 1572872 | tf_op jit(solution)/shard_map/ppermute | solution.py:29
  181.9 2.1 copy-start.8
  181.9 30.0 %collective-permute-start.1 = (bf16[2,512,128]{2,1,0:T(8,128)(2,1)S(1)}, bf16[2,512,128]{2,1,0:T(8,128)(2,1)S(1)}, u32[]{:S(2)}, u32[]{:S(2)}) collective-permute-start(bf16[2,512,128]{2,1,0:T(8,128)(2,1)S(1)} %pad_maximum_fusion.7), channel_id=1, source_target_pairs={{0,8},{8,0},{16,24},{24,16},{1,9},{9,1},{17,25},{25,17},{2,10},{10... | collective-permute-start | bytes 786440 | tf_op jit(solution)/shard_map/ppermute | solution.py:29
  182.3 56.5 %collective-permute-start.11 = (bf16[2,4,128,640]{3,2,1,0:T(8,128)(2,1)}, bf16[2,4,128,640]{3,2,1,0:T(8,128)(2,1)}, u32[]{:S(2)}, u32[]{:S(2)}) collective-permute-start(bf16[2,4,128,640]{3,2,1,0:T(8,128)(2,1)} %pad_maximum_fusion.refs_6_), channel_id=1, source_target_pairs={{0,4},{4,0},{1,5},{5,1},{2,6},{6,2},{3,7},{7,3},{8,12},{12,8},{9,1... | collective-permute-start | bytes 3932168 | tf_op jit(solution)/shard_map/ppermute | solution.py:29
  183.4 55.9 %collective-permute-start.7 = (bf16[8,128,640]{2,1,0:T(8,128)(2,1)}, bf16[8,128,640]{2,1,0:T(8,128)(2,1)}, u32[]{:S(2)}, u32[]{:S(2)}) collective-permute-start(bf16[8,128,640]{2,1,0:T(8,128)(2,1)} %constant_dynamic-update-slice_fusion.refs_2_), channel_id=1, source_target_pairs={{0,2},{1,3},{2,0},{3,1},{4,6},{5,7},{6,4},{7,5},{8,10},{9,11},{10,... | collective-permute-start | bytes 3932168 | tf_op jit(solution)/shard_map/ppermute | solution.py:29
  208.2 1.7 copy-start.9
  210.1 1.6 copy-start.4
  211.7 0.9 copy-start.15
  211.7 4.0 %copy-start.12 = (f32[512,256]{1,0:T(8,128)S(1)}, f32[512,256]{1,0:T(8,128)}, u32[]{:S(2)}) copy-start(f32[512,256]{1,0:T(8,128)} %get-tuple-element.27) | copy-start | bytes 1572868
  211.7 4.0 %copy-start.13 = (f32[512,256]{1,0:T(8,128)S(1)}, f32[512,256]{1,0:T(8,128)}, u32[]{:S(2)}) copy-start(f32[512,256]{1,0:T(8,128)} %get-tuple-element.26) | copy-start | bytes 1572868
  211.8 45.2 %collective-permute-start.32 = (bf16[2,256,1280]{2,1,0:T(8,128)(2,1)S(1)}, bf16[2,256,1280]{2,1,0:T(8,128)(2,1)}, u32[]{:S(2)}, u32[]{:S(2)}) collective-permute-start(bf16[2,256,1280]{2,1,0:T(8,128)(2,1)S(1)} %slice.121), channel_id=1, source_target_pairs={{0,1},{1,0},{2,3},{3,2},{4,5},{5,4},{6,7},{7,6},{8,9},{9,8},{10,11... | collective-permute-start | bytes 3932168 | tf_op jit(solution)/shard_map/ppermute | solution.py:29
  212.7 37.3 %copy-start.7 = (bf16[4,512,128]{2,1,0:T(8,128)(2,1)}, bf16[4,512,128]{2,1,0:T(8,128)(2,1)S(1)}, u32[]{:S(2)}) copy-start(bf16[4,512,128]{2,1,0:T(8,128)(2,1)S(1)} %pad_maximum_fusion.5.refs_0_) | copy-start | bytes 1572868
  212.7 26.1 %collective-permute-start.2 = (bf16[4,512,128]{2,1,0:T(8,128)(2,1)S(1)}, bf16[4,512,128]{2,1,0:T(8,128)(2,1)S(1)}, u32[]{:S(2)}, u32[]{:S(2)}) collective-permute-start(bf16[4,512,128]{2,1,0:T(8,128)(2,1)S(1)} %pad_maximum_fusion.5.refs_0_), channel_id=1, source_target_pairs={{0,16},{8,24},{16,0},{24,8},{1,17},{9,25},{17,1},{25,9},{2,18},{10... | collective-permute-start | bytes 1572872 | tf_op jit(solution)/shard_map/ppermute | solution.py:29
  215.9 23.5 %collective-permute-start.29 = (bf16[512,128]{1,0:T(8,128)(2,1)S(1)}, bf16[512,128]{1,0:T(8,128)(2,1)S(1)}, u32[]{:S(2)}, u32[]{:S(2)}) collective-permute-start(bf16[512,128]{1,0:T(8,128)(2,1)S(1)} %get-tuple-element.57), channel_id=1, source_target_pairs={{0,4},{4,0},{1,5},{5,1},{2,6},{6,2},{3,7},{7,3},{8,12},{12,8},{9,1... | collective-permute-start | bytes 393224 | tf_op jit(solution)/shard_map/ppermute | solution.py:29
  238.8 11.2 %copy-start.11 = (bf16[4,512,128]{2,1,0:T(8,128)(2,1)}, bf16[4,512,128]{2,1,0:T(8,128)(2,1)S(1)}, u32[]{:S(2)}) copy-start(bf16[4,512,128]{2,1,0:T(8,128)(2,1)S(1)} %collective-permute-done.2.refs_1_) | copy-start | bytes 1572868
  238.8 20.3 %collective-permute-start.12 = (bf16[2,4,128,640]{3,2,1,0:T(8,128)(2,1)}, bf16[2,4,128,640]{3,2,1,0:T(8,128)(2,1)}, u32[]{:S(2)}, u32[]{:S(2)}) collective-permute-start(bf16[2,4,128,640]{3,2,1,0:T(8,128)(2,1)} %pad_maximum_fusion.refs_6_), channel_id=1, source_target_pairs={{0,1},{1,0},{2,3},{3,2},{4,5},{5,4},{6,7},{7,6},{8,9},{9,8},{10,11... | collective-permute-start | bytes 3932168 | tf_op jit(solution)/shard_map/ppermute | solution.py:29
  238.8 21.8 %collective-permute-start.8 = (bf16[8,128,640]{2,1,0:T(8,128)(2,1)}, bf16[8,128,640]{2,1,0:T(8,128)(2,1)}, u32[]{:S(2)}, u32[]{:S(2)}) collective-permute-start(bf16[8,128,640]{2,1,0:T(8,128)(2,1)} %constant_dynamic-update-slice_fusion.refs_2_), channel_id=1, source_target_pairs={{0,1},{1,0},{2,3},{3,2},{4,5},{5,4},{6,7},{7,6},{8,9},{9,8},{10,11... | collective-permute-start | bytes 3932168 | tf_op jit(solution)/shard_map/ppermute | solution.py:29
  239.3 21.3 %collective-permute-start.13 = (bf16[2,4,128,640]{3,2,1,0:T(8,128)(2,1)}, bf16[2,4,128,640]{3,2,1,0:T(8,128)(2,1)}, u32[]{:S(2)}, u32[]{:S(2)}) collective-permute-start(bf16[2,4,128,640]{3,2,1,0:T(8,128)(2,1)} %collective-permute-done.11.refs_7_), channel_id=1, source_target_pairs={{0,1},{1,0},{2,3},{3,2},{4,5},{5,4},{6,7},{7,6},{8,9},{9,8},{10,11... | collective-permute-start | bytes 3932168 | tf_op jit(solution)/shard_map/ppermute | solution.py:29
  239.4 21.2 %collective-permute-start.9 = (bf16[8,128,640]{2,1,0:T(8,128)(2,1)}, bf16[8,128,640]{2,1,0:T(8,128)(2,1)}, u32[]{:S(2)}, u32[]{:S(2)}) collective-permute-start(bf16[8,128,640]{2,1,0:T(8,128)(2,1)} %collective-permute-done.7.refs_3_), channel_id=1, source_target_pairs={{0,1},{1,0},{2,3},{3,2},{4,5},{5,4},{6,7},{7,6},{8,9},{9,8},{10,11... | collective-permute-start | bytes 3932168 | tf_op jit(solution)/shard_map/ppermute | solution.py:29
  240.5 0.7 copy-start.20
  257.0 48.1 %collective-permute-start.30 = (bf16[2,384,1280]{2,1,0:T(8,128)(2,1)}, bf16[2,384,1280]{2,1,0:T(8,128)(2,1)}, u32[]{:S(2)}, u32[]{:S(2)}) collective-permute-start(bf16[2,384,1280]{2,1,0:T(8,128)(2,1)} %shard_map.185), channel_id=1, source_target_pairs={{0,1},{1,0},{2,3},{3,2},{4,5},{5,4},{6,7},{7,6},{8,9},{9,8},{10,11... | collective-permute-start | bytes 5898248 | tf_op jit(solution)/shard_map/ppermute | solution.py:29
  259.1 40.2 %collective-permute-start.33 = (bf16[1,256,1280]{2,1,0:T(8,128)(2,1)S(1)}, bf16[1,256,1280]{2,1,0:T(8,128)(2,1)}, u32[]{:S(2)}, u32[]{:S(2)}) collective-permute-start(bf16[1,256,1280]{2,1,0:T(8,128)(2,1)S(1)} %slice.138), channel_id=1, source_target_pairs={{0,2},{1,3},{2,0},{3,1},{4,6},{5,7},{6,4},{7,5},{8,10},{9,11},{10,... | collective-permute-start | bytes 1966088 | tf_op jit(solution)/shard_map/ppermute | solution.py:29
  286.8 3.7 %collective-permute-start.28 = (f32[8,128]{1,0:T(8,128)S(1)}, f32[8,128]{1,0:T(8,128)S(1)}, u32[]{:S(2)}, u32[]{:S(2)}) collective-permute-start(f32[8,128]{1,0:T(8,128)S(1)} %broadcast_in_dim.111), channel_id=1, source_target_pairs={{0,4},{4,0},{1,5},{5,1},{2,6},{6,2},{3,7},{7,3},{8,12},{12,8},{9,1... | collective-permute-start | bytes 12296 | tf_op jit(solution)/shard_map/ppermute | solution.py:29
  299.3 5.8 %copy-start.3 = (bf16[2,384,1280]{2,1,0:T(8,128)(2,1)S(1)}, bf16[2,384,1280]{2,1,0:T(8,128)(2,1)}, u32[]{:S(2)}) copy-start(bf16[2,384,1280]{2,1,0:T(8,128)(2,1)} %shard_map.184) | copy-start | bytes 5898244
  301.7 7.0 %copy-start.2 = (f32[512,5120]{1,0:T(8,128)S(1)}, f32[512,5120]{1,0:T(8,128)}, u32[]{:S(2)}) copy-start(f32[512,5120]{1,0:T(8,128)} %get-tuple-element.21) | copy-start | bytes 31457284
  303.7 8.9 %collective-permute-start.34 = (bf16[128,1280]{1,0:T(8,128)(2,1)}, bf16[128,1280]{1,0:T(8,128)(2,1)}, u32[]{:S(2)}, u32[]{:S(2)}) collective-permute-start(bf16[128,1280]{1,0:T(8,128)(2,1)} %fusion.3), channel_id=1, source_target_pairs={{0,4},{4,0},{1,5},{5,1},{2,6},{6,2},{3,7},{7,3},{8,12},{12,8},{9,1... | collective-permute-start | bytes 983048 | tf_op jit(solution)/shard_map/ppermute | solution.py:29
  308.2 22.9 %collective-permute-start.31 = (bf16[1,384,1280]{2,1,0:T(8,128)(2,1)}, bf16[1,384,1280]{2,1,0:T(8,128)(2,1)}, u32[]{:S(2)}, u32[]{:S(2)}) collective-permute-start(bf16[1,384,1280]{2,1,0:T(8,128)(2,1)} %slice.137), channel_id=1, source_target_pairs={{0,2},{1,3},{2,0},{3,1},{4,6},{5,7},{6,4},{7,5},{8,10},{9,11},{10,... | collective-permute-start | bytes 2949128 | tf_op jit(solution)/shard_map/ppermute | solution.py:29
  332.5 1.8 copy-start.1

commit v2 on v1

v2 whole, which is shorter than its diff:
```python
import functools
import jax
import jax.numpy as jnp
from jax import lax
from jax.experimental import pallas as pl
from jax.experimental.pallas import tpu as pltpu
from jax.sharding import PartitionSpec as P

GRID_H = 30
GRID_W = 52

guidance = 5.0
norm_eps = 1e-06

ANY = pl.BlockSpec(memory_space=pl.ANY)
SMEM = pl.BlockSpec(memory_space=pltpu.SMEM)
F32, BF16 = jnp.float32, jnp.bfloat16


def swap(size, bit):
    return [(i, i ^ bit) for i in range(size)]


def bits_of(size):
    return [1 << k for k in range(size.bit_length() - 1)]


def move(value, axis, bit):
    return lax.ppermute(value, axis, swap(lax.axis_size(axis), bit))


def rope_tables(first_token, length):
    token_index = first_token + jnp.arange(length, dtype=jnp.int32)
    plane_size = GRID_H * GRID_W
    frame_index = token_index // plane_size
    remainder = token_index - frame_index * plane_size
    row_index = remainder // GRID_W
    column_index = remainder - row_index * GRID_W
    pair_index = jnp.arange(64, dtype=jnp.int32)
    in_frames = pair_index < 22
    in_rows = jnp.logical_and(pair_index >= 22, pair_index < 43)
    local_rank = jnp.where(
        in_frames, pair_index, jnp.where(in_rows, pair_index - 22, pair_index - 43)
    ).astype(jnp.float32)
    axis_width = jnp.where(in_frames, 44.0, 42.0).astype(jnp.float32)
    frequency = jnp.exp(-jnp.log(10000.0) * 2.0 * local_rank / axis_width)
    chosen = jnp.where(
        in_frames[None, :],
        frame_index[:, None],
        jnp.where(in_rows[None, :], row_index[:, None], column_index[:, None]),
    ).astype(jnp.float32)
    angles = chosen * frequency[None, :]
    angles = jnp.concatenate([angles, angles], axis=1)
    return (jnp.cos(angles), jnp.sin(angles))


def dot(left, right):
    return jnp.dot(left, right, preferred_element_type=F32)


def contract(left, right, left_dim, right_dim):
    return lax.dot_general(
        left, right, (((left_dim,), (right_dim,)), ((), ())), preferred_element_type=F32
    )


def rotate_half(values):
    half = values.shape[-1] // 2
    return jnp.concatenate([-values[..., half:], values[..., :half]], axis=-1)


def rotate_back(values):
    half = values.shape[-1] // 2
    return jnp.concatenate([values[..., half:], -values[..., :half]], axis=-1)


def resident(shape):
    return pl.BlockSpec(shape, lambda *_: (0,) * len(shape), pipeline_mode=pl.Buffered(1))


def project_kernel(variants, keep, noisy_ref, shift_ref, gain_ref, weight_ref, *refs):
    out_ref = refs[0]
    hidden_ref = refs[1] if keep else None
    joined, normed = refs[-2:]
    tile, width = noisy_ref.shape
    head = weight_ref.shape[2]

    @pl.when(pl.program_id(0) == 0)
    def _():
        for k in range(3):
            joined[:, k * head : (k + 1) * head] = weight_ref[k]

    def step(t, carry):
        for u in range(2):
            at = pl.ds(pl.multiple_of(t * 32 + u * 16, 16), 16)
            latent = noisy_ref[at, :].astype(F32)
            for v in range(variants):
                shifted = latent + shift_ref[v : v + 1, :]
                mean = jnp.sum(shifted * shifted, axis=-1, keepdims=True) / width
                scaled = shifted * lax.rsqrt(mean + norm_eps) * gain_ref[...]
                normed[v, at, :] = scaled.astype(BF16)
        return carry

    lax.fori_loop(0, tile // 32, step, 0)
    for v in range(variants):
        out_ref[v] = dot(normed[v], joined[...])
    if keep:
        hidden_ref[...] = normed[0]


def project(noisy, shifts, gain, weight, keep):
    length, width = noisy.shape
    head = weight.shape[2]
    variants = shifts.shape[0]
    tile = min(256, length)
    out_shape = [jax.ShapeDtypeStruct((variants, length, 3 * head), F32)]
    out_specs = [pl.BlockSpec((variants, tile, 3 * head), lambda i: (0, i, 0))]
    if keep:
        out_shape.append(jax.ShapeDtypeStruct((length, width), BF16))
        out_specs.append(pl.BlockSpec((tile, width), lambda i: (i, 0)))
    return pl.pallas_call(
        functools.partial(project_kernel, variants, keep),
        grid=(length // tile,),
        in_specs=[
            pl.BlockSpec((tile, width), lambda i: (i, 0)),
            resident((variants, width)),
            resident((1, width)),
            resident(weight.shape),
        ],
        out_specs=out_specs,
        out_shape=out_shape,
        scratch_shapes=[
            pltpu.VMEM((width, 3 * head), BF16),
            pltpu.VMEM((variants, tile, width), BF16),
        ],
        cost_estimate=pl.CostEstimate(
            flops=2 * variants * length * width * 3 * head,
            bytes_accessed=2 * length * width * (2 if keep else 1) + 6 * width * head,
            transcendentals=0,
        ),
    )(noisy, shifts, gain, weight)


def rope_rows(raw, gain, cosine, sine):
    inverse = lax.rsqrt(jnp.mean(raw * raw, axis=-1, keepdims=True) + norm_eps)
    normed = raw * inverse * gain
    return (normed * cosine + rotate_half(normed) * sine).astype(BF16)


def softmax_rows(query, key, scale):
    exponent = jnp.exp(contract(query, key, 1, 1) * scale)
    return exponent / jnp.sum(exponent, axis=-1, keepdims=True)


def attend_kernel(variants, seqs, per, scal, qkv_ref, gain_ref, cos_ref, sin_ref, *refs):
    shares, saves = refs[:seqs], refs[seqs:-2]
    keys, values = refs[-2:]
    tile, head = shares[0].shape
    scale = head ** (-0.5)
    i = pl.program_id(0)

    @pl.when(i == 0)
    def _():
        for v in range(variants):
            keys[v] = rope_rows(
                qkv_ref[v, :, head : 2 * head], gain_ref[1:2, :], cos_ref[...], sin_ref[...]
            )
            values[v] = qkv_ref[v, :, 2 * head :].astype(BF16)
        if saves:
            saves[1][...] = keys[0]
            saves[2][...] = values[0]

    at = pl.ds(pl.multiple_of(i * tile, tile), tile)
    results = []
    for v in range(variants):
        query = rope_rows(qkv_ref[v, at, :head], gain_ref[0:1, :], cos_ref[at, :], sin_ref[at, :])
        if saves:
            saves[0][...] = query
        prob = softmax_rows(query, keys[v], scale).astype(BF16)
        results.append(dot(prob, values[v]).astype(BF16))
    result = results[0]
    if variants > 1:
        guided = guidance * results[0].astype(F32) - (guidance - 1.0) * results[1].astype(F32)
        result = guided.astype(BF16)
    for d, share in enumerate(shares):

        @pl.when(i // per == (scal[0] ^ d))
        def _():
            share[...] = result


def attend(scal, seqs, qkv, gains, cosine, sine, keep):
    variants, length, triple = qkv.shape
    head = triple // 3
    rows = length // seqs
    tile = min(256, rows)
    per = rows // tile
    saved = 3 if keep else 0
    row = pl.BlockSpec((tile, head), lambda i, s: (i, 0))
    whole = pl.BlockSpec((length, head), lambda i, s: (0, 0))
    flat = jax.ShapeDtypeStruct((length, head), BF16)

    def share(d):
        return pl.BlockSpec(
            (tile, head), lambda i, s: (jnp.clip(i - (s[0] ^ d) * per, 0, per - 1), 0)
        )

    results = pl.pallas_call(
        functools.partial(attend_kernel, variants, seqs, per),
        grid_spec=pltpu.PrefetchScalarGridSpec(
            num_scalar_prefetch=1,
            grid=(length // tile,),
            in_specs=[
                resident(qkv.shape),
                resident(gains.shape),
                resident(cosine.shape),
                resident(sine.shape),
            ],
            out_specs=[share(d) for d in range(seqs)] + [row, whole, whole][:saved],
            scratch_shapes=[
                pltpu.VMEM((variants, length, head), BF16),
                pltpu.VMEM((variants, length, head), BF16),
            ],
        ),
        out_shape=[jax.ShapeDtypeStruct((rows, head), BF16)] * seqs + [flat] * saved,
        cost_estimate=pl.CostEstimate(
            flops=16 * variants * length * length * head,
            bytes_accessed=4 * variants * length * triple,
            transcendentals=variants * length * length,
        ),
    )(scal, qkv, gains, cosine, sine)
    return results[:seqs], results[seqs:]


class Plan:
    def __init__(self):
        self.operands = []
        self.chunks = []

    def add(self, array):
        self.operands.append(array)
        return len(self.operands) - 1


def fetch(chunk, refs, target, sems, place, along, columns=None):
    copies = []
    for n, (op, lead, js, jb) in enumerate(chunk):
        source = refs[op]
        for index in lead:
            source = source.at[index]
        if columns is not None:
            source = source.at[:, columns]
        head = source.shape[along]
        first = pl.multiple_of(place(js, jb) * head, head)
        spot = (pl.ds(first, head), slice(None)) if along == 0 else (slice(None), pl.ds(first, head))
        copies.append(pltpu.make_async_copy(source, target.at[spot], sems.at[n]))
    return copies


def stream(attn_plan, plan, seqs, scal, attn_refs, out_refs, heads, weights, attn_sems, sems):
    i = pl.program_id(0)
    seq, branch = scal[0], scal[1]
    cols = weights.shape[2]

    def place(js, jb):
        return (branch ^ jb) * seqs + (seq ^ js)

    def copies_of(k):
        columns = pl.ds((k % 2) * cols, cols)
        return fetch(plan[k // 2], out_refs, weights.at[k % 2], sems.at[k % 2], place, 0, columns)

    @pl.when(i == 0)
    def _():
        copies = fetch(attn_plan, attn_refs, heads, attn_sems, place, 1)
        for copy in copies + copies_of(0):
            copy.start()
        for copy in copies:
            copy.wait()

    steps = 2 * len(plan)
    for k in range(steps):

        @pl.when(i == k)
        def _():
            if k + 1 < steps:
                for copy in copies_of(k + 1):
                    copy.start()
            for copy in copies_of(k):
                copy.wait()

    return i % 2


def row_blocks(rows):
    block = min(128, rows)
    return [slice(start, start + block) for start in range(0, rows, block)]


def post_kernel(attn_plan, plan, seqs, n_attn, n_out, resume, scal, noise_ref, *refs):
    attn_refs, refs = refs[:n_attn], refs[n_attn:]
    out_refs, refs = refs[:n_out], refs[n_out:]
    noisy_ref, target_ref, shift_ref = refs[:3]
    refs = refs[3:]
    if resume:
        before_ref, refs = refs[0], refs[1:]
    term_ref, part_ref, grad_ref = refs[:3]
    heads, weights, cotangents, attn_sems, sems = refs[3:]
    slot = stream(
        attn_plan, plan, seqs, scal, attn_refs, out_refs, heads, weights, attn_sems, sems
    )

    @pl.when(pl.program_id(0) == 0)
    def _():
        grad_ref[...] = before_ref[...] if resume else jnp.zeros_like(grad_ref)

    noise = noise_ref[0]
    own_size = part_ref.shape[1]
    own = pl.ds(pl.multiple_of(scal[1] * own_size, own_size), own_size)
    for at in row_blocks(noisy_ref.shape[0]):
        term = dot(heads[at, :], weights[slot])
        term_ref[0, at, :] = term.astype(BF16)
        latent = noisy_ref[at, :].astype(F32)
        fake_pred = latent - noise * (latent + shift_ref[...] + term)
        cotangent = (noise * (-1.0 / 64.0)) * (fake_pred - target_ref[at, :].astype(F32))
        cotangents[at, :] = cotangent.astype(BF16)
        grad_ref[at, :] += contract(cotangents[at, :], weights[slot, own, :], 1, 1)
    part_ref[0] = contract(heads[:, own], cotangents[...], 0, 0).astype(BF16)


def plan_heads(plan):
    return len(plan[0])


def post(attn, out, blocks, scal, noise, noisy, target, shift, seqs, head, before):
    rows = target.shape[0]
    total = plan_heads(out.chunks)
    cols = out.operands[0].shape[-1] // 2
    chunks = len(out.chunks)
    n_attn, n_out = len(attn.operands), len(out.operands)
    kernel = functools.partial(
        post_kernel, attn.chunks[0], out.chunks, seqs, n_attn, n_out, len(before)
    )
    grad_spec = pl.BlockSpec((rows, seqs * head), lambda i, s: (0, 0))

    def spot(i, s):
        return s[2 + blocks + i // 2] * 2 + i % 2

    return pl.pallas_call(
        kernel,
        grid_spec=pltpu.PrefetchScalarGridSpec(
            num_scalar_prefetch=1,
            grid=(2 * chunks,),
            in_specs=[SMEM]
            + [ANY] * (n_attn + n_out)
            + [
                pl.BlockSpec((rows, cols), lambda i, s: (s[0], spot(i, s))),
                pl.BlockSpec((rows, cols), lambda i, s: (0, spot(i, s))),
                pl.BlockSpec((1, cols), lambda i, s: (0, spot(i, s))),
            ]
            + [grad_spec] * len(before),
            out_specs=[
                pl.BlockSpec((1, rows, cols), lambda i, s: (i // 2, 0, i % 2)),
                pl.BlockSpec((1, seqs * head, cols), lambda i, s: (i // 2, 0, i % 2)),
                grad_spec,
            ],
            scratch_shapes=[
                pltpu.VMEM((rows, total * head), BF16),
                pltpu.VMEM((2, total * head, cols), BF16),
                pltpu.VMEM((rows, cols), BF16),
                pltpu.SemaphoreType.DMA((total,)),
                pltpu.SemaphoreType.DMA((2, total)),
            ],
        ),
        out_shape=[
            jax.ShapeDtypeStruct((chunks, rows, 2 * cols), BF16),
            jax.ShapeDtypeStruct((chunks, seqs * head, 2 * cols), BF16),
            jax.ShapeDtypeStruct((rows, seqs * head), F32),
        ],
        cost_estimate=pl.CostEstimate(
            flops=4 * rows * chunks * cols * head * (total + 2 * seqs),
            bytes_accessed=2 * chunks * cols * (2 * total * head + 8 * rows),
            transcendentals=0,
        ),
    )(scal, noise, *attn.operands, *out.operands, noisy, target, shift, *before)


def guide_kernel(attn_plan, plan, seqs, n_attn, n_out, scal, noise_ref, *refs):
    attn_refs, refs = refs[:n_attn], refs[n_attn:]
    out_refs, refs = refs[:n_out], refs[n_out:]
    noisy_ref, target_ref, cond_ref, null_ref, near_ref, far_ref, diff_ref, total_ref = refs[:8]
    sum_ref, heads, weights, attn_sems, sems = refs[8:]
    slot = stream(
        attn_plan, plan, seqs, scal, attn_refs, out_refs, heads, weights, attn_sems, sems
    )

    @pl.when(pl.program_id(0) == 0)
    def _():
        sum_ref[...] = jnp.zeros_like(sum_ref)

    noise = noise_ref[0]
    own = pl.program_id(0) < pl.num_programs(0) // 2
    cond = cond_ref[...]
    mixed = guidance * cond - (guidance - 1.0) * null_ref[...]
    for at in row_blocks(noisy_ref.shape[0]):
        guided = dot(heads[at, :], weights[slot]) + mixed
        latent = noisy_ref[at, :].astype(F32)
        real_pred = latent - noise * (latent + guided)
        distance = jnp.abs(real_pred - target_ref[at, :].astype(F32))
        sum_ref[...] += jnp.sum(distance.reshape(-1, 8, distance.shape[1]), axis=0)
        term = jnp.where(own, near_ref[0, at, :].astype(F32), far_ref[0, at, :].astype(F32))
        diff_ref[at, :] = (noise * (guided - (cond + term))).astype(BF16)

    @pl.when(pl.program_id(0) == pl.num_programs(0) - 1)
    def _():
        total_ref[...] = jnp.broadcast_to(jnp.sum(sum_ref[...]), total_ref.shape)


def guide(attn, out, scal, noise, noisy, target, cond, null, near, far, seqs, head):
    rows, width = target.shape
    total = plan_heads(out.chunks)
    cols = out.operands[0].shape[-1] // 2
    chunks = len(out.chunks)
    n_attn, n_out = len(attn.operands), len(out.operands)

    def spot(i, s):
        return s[2 + i // 2] * 2 + i % 2

    column = pl.BlockSpec((1, cols), lambda i, s: (0, spot(i, s)))
    last = chunks - 1

    def near_spot(i, s):
        return (jnp.minimum(i, last) // 2, 0, jnp.minimum(i, last) % 2)

    def far_spot(i, s):
        return (jnp.maximum(i - last - 1, 0) // 2, 0, jnp.maximum(i - last - 1, 0) % 2)

    return pl.pallas_call(
        functools.partial(guide_kernel, attn.chunks[0], out.chunks, seqs, n_attn, n_out),
        grid_spec=pltpu.PrefetchScalarGridSpec(
            num_scalar_prefetch=1,
            grid=(2 * chunks,),
            in_specs=[SMEM]
            + [ANY] * (n_attn + n_out)
            + [
                pl.BlockSpec((rows, cols), lambda i, s: (s[0], spot(i, s))),
                pl.BlockSpec((rows, cols), lambda i, s: (0, spot(i, s))),
                column,
                column,
                pl.BlockSpec((1, rows, cols), near_spot),
                pl.BlockSpec((1, rows, cols), far_spot),
            ],
            out_specs=[
                pl.BlockSpec((rows, cols), lambda i, s: (0, spot(i, s))),
                pl.BlockSpec((8, 128), lambda i, s: (0, 0)),
            ],
            scratch_shapes=[
                pltpu.VMEM((8, cols), F32),
                pltpu.VMEM((rows, total * head), BF16),
                pltpu.VMEM((2, total * head, cols), BF16),
                pltpu.SemaphoreType.DMA((total,)),
                pltpu.SemaphoreType.DMA((2, total)),
            ],
        ),
        out_shape=[jax.ShapeDtypeStruct((rows, width), BF16), jax.ShapeDtypeStruct((8, 128), F32)],
        cost_estimate=pl.CostEstimate(
            flops=2 * rows * width * head * total,
            bytes_accessed=width * (2 * total * head + 8 * rows),
            transcendentals=0,
        ),
    )(scal, noise, *attn.operands, *out.operands, noisy, target, cond, null, near, far)


def backward_kernel(
    q_ref, k_ref, v_ref, go_ref, qkv_ref, gain_ref, cos_ref, sin_ref, out_ref, key_sum, value_sum
):
    tile, head = q_ref.shape
    scale = head ** (-0.5)
    i = pl.program_id(0)
    at = pl.ds(pl.multiple_of(i * tile, tile), tile)

    @pl.when(i == 0)
    def _():
        key_sum[...] = jnp.zeros_like(key_sum)
        value_sum[...] = jnp.zeros_like(value_sum)

    def unroll(raw, grad_rot, gain, cosine, sine):
        grad_normed = grad_rot * cosine + rotate_back(grad_rot * sine)
        inverse = lax.rsqrt(jnp.mean(raw * raw, axis=-1, keepdims=True) + norm_eps)
        scaled = gain * grad_normed
        mean = jnp.mean(scaled * raw, axis=-1, keepdims=True)
        return inverse * scaled - raw * inverse * inverse * inverse * mean

    probability = softmax_rows(q_ref[...], k_ref[...], scale)
    grad_prob = contract(go_ref[...], v_ref[...], 1, 1)
    inner = jnp.sum(grad_prob * probability, axis=-1, keepdims=True)
    grad_score = (probability * (grad_prob - inner) * scale).astype(BF16)
    grad_query = unroll(
        qkv_ref[0, at, :head],
        dot(grad_score, k_ref[...]),
        gain_ref[0:1, :],
        cos_ref[at, :],
        sin_ref[at, :],
    )
    out_ref[:head, at] = grad_query.T.astype(BF16)
    key_sum[...] += contract(grad_score, q_ref[...], 0, 0)
    value_sum[...] += contract(probability.astype(BF16), go_ref[...], 0, 0)

    @pl.when(i == pl.num_programs(0) - 1)
    def _():
        grad_key = unroll(
            qkv_ref[0, :, head : 2 * head],
            key_sum[...],
            gain_ref[1:2, :],
            cos_ref[...],
            sin_ref[...],
        )
        out_ref[head : 2 * head, :] = grad_key.T.astype(BF16)
        out_ref[2 * head :, :] = value_sum[...].T.astype(BF16)


def backward(query, key, value, grad_attn, qkv, gains, cosine, sine):
    length, head = query.shape
    tile = min(256, length)
    row = pl.BlockSpec((tile, head), lambda i: (i, 0))
    return pl.pallas_call(
        backward_kernel,
        grid=(length // tile,),
        in_specs=[
            row,
            resident((length, head)),
            resident((length, head)),
            row,
            resident(qkv.shape),
            resident(gains.shape),
            resident(cosine.shape),
            resident(sine.shape),
        ],
        out_specs=pl.BlockSpec((3 * head, length), lambda i: (0, 0)),
        out_shape=jax.ShapeDtypeStruct((3 * head, length), BF16),
        scratch_shapes=[pltpu.VMEM((length, head), F32), pltpu.VMEM((length, head), F32)],
        cost_estimate=pl.CostEstimate(
            flops=20 * length * length * head,
            bytes_accessed=12 * length * head,
            transcendentals=length * length,
        ),
    )(query, key, value, grad_attn, qkv, gains, cosine, sine)


def weight_kernel(scal, grad_ref, hidden_ref, out_ref):
    out_ref[0] = dot(grad_ref[...], hidden_ref[...]).astype(BF16)


def weight_grad(grads, hidden, blocks, count, scal, cols):
    features, length = grads.shape
    parts = 2
    tile = cols // parts
    return pl.pallas_call(
        weight_kernel,
        grid_spec=pltpu.PrefetchScalarGridSpec(
            num_scalar_prefetch=1,
            grid=(count, parts),
            in_specs=[
                pl.BlockSpec((features, length), lambda i, p, s: (0, 0)),
                pl.BlockSpec((length, tile), lambda i, p, s: (0, s[2 + blocks + i] * parts + p)),
            ],
            out_specs=pl.BlockSpec((1, features, tile), lambda i, p, s: (i, 0, p)),
        ),
        out_shape=jax.ShapeDtypeStruct((count, features, cols), BF16),
        cost_estimate=pl.CostEstimate(
            flops=2 * count * cols * features * length,
            bytes_accessed=2 * count * cols * (length + features),
            transcendentals=0,
        ),
    )(scal, grads, hidden)


def spread_heads(value, axis, order, which):
    held, orders = [value], list(order)
    for d in range(1, lax.axis_size(axis)):
        held.append(move(value, axis, d))
        orders += [(js ^ d, jb) if which == 0 else (js, jb ^ d) for js, jb in order]
    return held, orders


def scale_kernel(entries, *refs):
    diff_ref, out_ref = refs[-2:]
    total = sum(ref[0:1, 0:1] for ref in refs[:-2])
    inverse = 1.0 / (total / entries + 1e-05)
    out_ref[...] = (diff_ref[...].astype(F32) * inverse).astype(BF16)


def scale(diff, totals, entries):
    rows, width = diff.shape
    tile = min(64, rows)
    block = pl.BlockSpec((tile, width), lambda i: (i, 0))
    return pl.pallas_call(
        functools.partial(scale_kernel, entries),
        grid=(rows // tile,),
        in_specs=[resident(totals[0].shape)] * len(totals) + [block],
        out_specs=block,
        out_shape=jax.ShapeDtypeStruct((rows, width), BF16),
        cost_estimate=pl.CostEstimate(
            flops=4 * rows * width, bytes_accessed=4 * rows * width, transcendentals=0
        ),
    )(*totals, diff)


def turn_kernel(*refs):
    terms, out_ref = refs[:-1], refs[-1]
    head = out_ref.shape[2]
    for k in range(3):
        at = slice(k * head, (k + 1) * head)
        value = sum(term[0, at, :].astype(F32) for term in terms)
        out_ref[k] = value.T


def turn(terms, head):
    features, cols = terms[0].shape[1:]
    tile = cols // 2
    return pl.pallas_call(
        turn_kernel,
        grid=(cols // tile,),
        in_specs=[pl.BlockSpec((1, features, tile), lambda i: (0, 0, i))] * len(terms),
        out_specs=pl.BlockSpec((3, tile, head), lambda i: (0, i, 0)),
        out_shape=jax.ShapeDtypeStruct((3, cols, head), F32),
        cost_estimate=pl.CostEstimate(
            flops=3 * features * cols, bytes_accessed=10 * features * cols, transcendentals=0
        ),
    )(*terms)


def gather_out(weight, rep):
    size = lax.axis_size("rep")
    cols = weight.shape[1] // size
    far = [bit for bit in bits_of(size) if bit > 1]
    mine = lax.dynamic_slice_in_dim(weight, rep * cols, cols, 1)[None]
    held, order = spread_heads(mine, "branch", [(0, 0)], 1)
    middle = max(len(held) // 2, 1)
    near_plan, far_plan = Plan(), Plan()
    near_plan.chunks = [[] for _ in range(size // 2)]
    far_plan.chunks = [[] for _ in range(size // 2)]

    def add(value, heads):
        for plan, v in ((near_plan, value), (far_plan, move(value, "rep", 1))):
            op = plan.add(v)
            for chunk, lead, js, jb in heads:
                plan.chunks[chunk].append((op, lead, js, jb))

    value = jnp.concatenate(held[:middle], axis=0)
    others, heads = spread_heads(value, "seq", order[:middle], 0)
    pieces = [jnp.concatenate(others, axis=0)]
    for bit in far:
        pieces += [move(piece, "rep", bit) for piece in pieces]
    for q, piece in enumerate(pieces):
        add(piece, [(q, (n,), js, jb) for n, (js, jb) in enumerate(heads)])

    value = jnp.concatenate(held[middle:], axis=0)[None]
    for bit in far:
        value = jnp.concatenate([value, move(value, "rep", bit)], axis=0)
    seqs = lax.axis_size("seq")
    for d in range(seqs):
        piece = move(value, "seq", d) if d else value
        heads = [
            (q, (q, n), d, jb)
            for q in range(value.shape[0])
            for n, (_, jb) in enumerate(order[middle:])
        ]
        add(piece, heads)
    return near_plan, far_plan


def gather_heads(attended):
    seqs = len(attended)
    held = [attended[0]] + [move(attended[d], "seq", d) for d in range(1, seqs)]
    held, order = spread_heads(jnp.stack(held), "branch", [(d, 0) for d in range(seqs)], 1)
    plan = Plan()
    chunk = []
    for n, (js, jb) in enumerate(order):
        if n % seqs == 0:
            op = plan.add(held[n // seqs])
        chunk.append((op, (n % seqs,), js, jb))
    plan.chunks.append(chunk)
    return plan


def body(
    noisy,
    generated,
    caption,
    null_caption,
    caption_drop,
    timestep,
    window_start,
    teacher_qkv,
    teacher_out,
    teacher_gain,
    teacher_qk_gain,
    critic_qkv,
    critic_out,
    critic_gain,
    critic_qk_gain,
):
    length, width = noisy.shape[1:]
    head = critic_out.shape[0]
    seqs, reps = lax.axis_size("seq"), lax.axis_size("rep")
    seq, rep, branch = lax.axis_index("seq"), lax.axis_index("rep"), lax.axis_index("branch")
    rows, cols = length // seqs, width // reps
    fraction = (timestep.astype(F32) + 1.0) / 1001.0
    noise = 5.0 * fraction / (1.0 + 4.0 * fraction)
    used_caption = jnp.where(caption_drop[0] == 1, null_caption, caption[0])
    cond_shift = used_caption.astype(F32)[None, :]
    null_shift = null_caption.astype(F32)[None, :]
    both_shift = jnp.concatenate([cond_shift, null_shift], axis=0)
    latent = noisy[0]
    target = generated[0]
    far = [bit for bit in bits_of(reps) if bit > 1]
    chunks = [0]
    for bit in far:
        chunks += [j ^ bit for j in chunks]
    kept = len(chunks)
    chunks += [j ^ 1 for j in chunks]
    scal = jnp.stack([seq, branch] + [rep ^ j for j in chunks]).astype(jnp.int32)

    critic_near, critic_far = gather_out(critic_out, rep)
    cosine, sine = rope_tables(window_start[0], length)
    fake_qkv, hidden = project(latent, cond_shift, critic_gain[None], critic_qkv, True)
    later, fake_qkv = lax.optimization_barrier((rep, fake_qkv))
    fake_attn, (fake_q, fake_k, fake_v) = attend(
        scal, seqs, fake_qkv, critic_qk_gain, cosine, sine, True
    )
    fake_plan = gather_heads(fake_attn)
    teacher_near, teacher_far = gather_out(teacher_out, later)
    (both_qkv,) = project(latent, both_shift, teacher_gain[None], teacher_qkv, False)
    guided_attn, _ = attend(scal, seqs, both_qkv, teacher_qk_gain, cosine, sine, False)
    guided_plan = gather_heads(guided_attn)

    common = (noise, latent, target, cond_shift, seqs, head)
    near_term, near_part, near_grad = post(fake_plan, critic_near, 0, scal, *common, ())
    far_term, far_part, grad_all = post(fake_plan, critic_far, kept, scal, *common, (near_grad,))

    def grad_block(d):
        return lax.dynamic_slice_in_dim(grad_all, (seq ^ d) * head, head, 1).astype(BF16)

    grad_attn = jnp.zeros((length, head), BF16)
    for d in range(seqs):
        piece = move(grad_block(d), "seq", d) if d else grad_block(0)
        grad_attn = lax.dynamic_update_slice(grad_attn, piece, ((seq ^ d) * rows, 0))

    grads = backward(fake_q, fake_k, fake_v, grad_attn, fake_qkv, critic_qk_gain, cosine, sine)
    far_weight = weight_grad(grads, hidden, kept, kept, scal, cols)
    near_weight = weight_grad(grads, hidden, 0, kept, scal, cols)

    def reduce_rep(kept_part, sent_part):
        terms = [kept_part, move(sent_part, "rep", 1)]
        for bit in far[::-1]:
            split = bit // 2
            upper = sum(term[split : 2 * split].astype(F32) for term in terms).astype(BF16)
            terms = terms + [move(upper, "rep", bit)]
        return terms

    terms = reduce_rep(near_part, far_part)

    def out_block(d):
        return sum(
            lax.dynamic_slice(term, (0, (seq ^ d) * head, 0), (1, head, cols))[0].astype(F32)
            for term in terms
        )

    out_grad = out_block(0)
    for d in range(1, seqs):
        out_grad += move(out_block(d).astype(BF16), "seq", d).astype(F32)

    proj_terms = reduce_rep(near_weight, far_weight)
    proj_grad = turn(proj_terms, head)

    teacher_plan = Plan()
    shift_ops = len(teacher_near.operands)
    teacher_plan.operands = teacher_near.operands + teacher_far.operands
    teacher_plan.chunks = teacher_near.chunks + [
        [(op + shift_ops, lead, js, jb) for op, lead, js, jb in chunk]
        for chunk in teacher_far.chunks
    ]
    diff, partial = guide(
        guided_plan,
        teacher_plan,
        scal,
        noise,
        latent,
        target,
        cond_shift,
        null_shift,
        near_term,
        far_term,
        seqs,
        head,
    )
    totals = [partial] + [move(partial, "seq", d) for d in range(1, seqs)]
    result = scale(diff, totals, length * width)
    return result[None], proj_grad, out_grad


def solution(mesh):
    in_specs = (
        P("rep", None, None),
        P("rep", "seq", None),
        P("rep", None),
        P(),
        P("rep"),
        P("rep"),
        P("rep"),
        P(None, None, ("branch", "seq")),
        P(("branch", "seq"), None),
        P(),
        P(None, ("branch", "seq")),
        P(None, None, ("branch", "seq")),
        P(("branch", "seq"), None),
        P(),
        P(None, ("branch", "seq")),
    )
    out_specs = (
        P("rep", "seq", None),
        P(None, "rep", ("branch", "seq")),
        P(("branch", "seq"), "rep"),
    )
    return jax.shard_map(
        body,
        mesh=mesh,
        in_specs=in_specs,
        out_specs=out_specs,
        check_vma=False,
    )
```

time: 335 us -> 327 us (0.976)
  starting transfers between devices: 35.2 us -> 67.5 us
  local copies, waits for them, and re-layouts: 28.7 us -> 6.25 us
  waiting for transfers between devices: 96 us -> 84.3 us
  other arithmetic: 27.3 us -> 21.5 us
    ppermute x35 -> x37, starting transfers between devices: 35.2 us -> 67.5 us  [move(): return lax.ppermute(value, axis, swap(lax.axis_size(axis), bit))]
    ppermute x35 -> x37, waiting for transfers between devices: 96 us -> 84.3 us  [move(): return lax.ppermute(value, axis, swap(lax.axis_size(axis), bit))]
    slice x13 -> x0, local copies, waits for them, and re-layouts: 11.1 us -> none  [the longest x8 8.77 us: gather_out(): v[:, :, half:]]
    add x7 -> x1, other arithmetic: 10.6 us -> 2.16 us  [body(): out_grad += move(out_block(d).astype(BF16), 'seq', d).astype(F32)]
    convert_element_type x1 -> x3, other arithmetic: 0.07 us -> 6.02 us  [the longest x2 4.1 us: reduce_rep(): sum((term[split:2 * split].astype(F32) for term in terms)).astype(BF16)]
    pallas_call x1, Pallas kernels: 24.2 us -> 19.8 us  [guide(): pl.pallas_call(functools.partial(guide_kernel, attn.chunks[0], out.chunks...]
    concatenate x3 -> x0, local copies, waits for them, and re-layouts: 4.21 us -> none  [the longest x2 3.99 us: gather_out(): pieces = [jnp.concatenate(others, axis=0)]]
    pallas_call x7 -> x8, Pallas kernels: 96.5 us -> 100 us  [the longest x2 47.1 us: project(): pl.pallas_call(functools.partial(project_kernel, variants, keep), grid=(l...]
  transfers between devices with their start and end apart: 35 -> 37, of which waited for: 9 -> 12; matrix products, arithmetic and copies ran while one was open for 14% -> 7% of each run, Pallas kernels for 43% -> 43%
where the time goes in v2:
time: 327 us; the launch traced here: 325 us
  Pallas kernels  143 us (44%)
  waiting for transfers between devices  84.3 us (26%)
  starting transfers between devices  67.5 us (21%)
  other arithmetic  21.5 us (7%)
  local copies, waits for them, and re-layouts  6.25 us (2%)
    ppermute x37, waiting for transfers between devices, move(): return lax.ppermute(value, axis, swap(lax.axis_size(axis), bit))  84.3 us
    ppermute x37, starting transfers between devices, move(): return lax.ppermute(value, axis, swap(lax.axis_size(axis), bit))  67.5 us
    pallas_call x2, Pallas kernels, project(): pl.pallas_call(functools.partial(project_kernel, variants, keep), grid=(l...  47.1 us
    pallas_call x2, Pallas kernels, post(): pl.pallas_call(kernel, grid_spec=pltpu.PrefetchScalarGridSpec(num_scalar_...  24.4 us
    pallas_call x1, Pallas kernels, guide(): pl.pallas_call(functools.partial(guide_kernel, attn.chunks[0], out.chunks...  19.8 us
    pallas_call x2, Pallas kernels, attend(): pl.pallas_call(functools.partial(attend_kernel, variants, seqs, per), gri...  17.8 us
    pallas_call x2, Pallas kernels, weight_grad(): pl.pallas_call(weight_kernel, grid_spec=pltpu.PrefetchScalarGridSpec(num_...  14 us
    pallas_call x1, Pallas kernels, backward(): pl.pallas_call(backward_kernel, grid=(length // tile,), in_specs=[row, re...  8.69 us
  transfers between devices with their start and end apart: 37, of which 12 were waited for; matrix products, arithmetic and copies ran while one was open for 7% of the time, Pallas kernels for 43%

profile of v2, /device:TPU:0, one launch (start us, length us, event | category | flops | bytes accessed | tf_op | source)
XLA Modules:
  0.0 325.4 jit_solution(15377424012717519248)
XLA Ops:
  0.7 1.3 copy-done
  2.0 4.1 %collective-permute-start.22 = (bf16[1,128,1280]{2,1,0:T(8,128)(2,1)S(1)}, bf16[1,128,1280]{2,1,0:T(8,128)(2,1)S(1)}, u32[]{:S(2)}, u32[]{:S(2)}) collective-permute-start(bf16[1,128,1280]{2,1,0:T(8,128)(2,1)S(1)} %dynamic-slice_bitcast_fusion), channel_id=1, source_target_pairs={{0,16},{8,24},{16,0},{24,8},{1,17},{9,25},{17,1},{25,9},{2,18},{10... | collective-permute-start | bytes 983048 | tf_op jit(solution)/shard_map/ppermute | solution.py:29
  6.1 1.3 collective-permute-start.23
  8.3 0.8 reduce
  9.1 1.4 select_convert_fusion
  10.5 18.6 %shard_map.168 = (f32[1,1024,384]{2,1,0:T(8,128)}, bf16[1024,5120]{1,0:T(8,128)(2,1)}) custom-call(bf16[1024,5120]{1,0:T(8,128)(2,1)} %bitcast.33, f32[1,5120]{1,0:T(1,128)} %bitcast.42, f32[1,5120]{1,0:T(1,128)} %bitcast.53, bf16[3,5120,128]{2,1,0:T(8,128)(2,1)} %weight_ref.3), custom_call_target="tpu_custom_call" | custom-call | flops 4026531840 | bytes 24903680 | tf_op jit(solution)/shard_map/pallas_call | solution.py:121
  29.2 1.0 dynamic-slice_bitcast_fusion.1
  30.2 2.9 collective-permute-start.7
  33.0 1.3 collective-permute-start.8
  35.2 1.6 collective-permute-start.24
  36.8 1.6 collective-permute-start.20
  38.9 11.4 %collective-permute-done.24 = bf16[1,2,128,1280]{3,2,1,0:T(8,128)(2,1)S(1)} collective-permute-done((bf16[1,2,128,1280]{3,2,1,0:T(8,128)(2,1)S(1)}, bf16[1,2,128,1280]{3,2,1,0:T(8,128)(2,1)S(1)}, u32[]{:S(2)}, u32[]{:S(2)}) %collective-permute-start.24) | collective-permute-done | bytes 655392 | tf_op jit(solution)/shard_map/ppermute | solution.py:29
  50.5 1.6 collective-permute-start.25
  52.6 1.2 pad_maximum_fusion.2.refs_4_
  53.8 1.0 collective-permute-start.21
  54.7 2.9 fusion
  58.2 7.6 %shard_map.169 = (bf16[512,128]{1,0:T(8,128)(2,1)}, bf16[512,128]{1,0:T(8,128)(2,1)}, bf16[1024,128]{1,0:T(8,128)(2,1)}, bf16[1024,128]{1,0:T(8,128)(2,1)}, bf16[1024,128]{1,0:T(8,128)(2,1)}) custom-call(s32[6]{0:T(128)} %stack.45.scal, f32[1,1024,384]{2,1,0:T(8,128)} %get-tuple-element.26.qkv_ref, f32[2,128]{1,0:T(2,128)} %gain_ref.5, ...), custom_call_target="tpu_custom_call" | custom-call | flops 2147483648 | bytes 1572864 | tf_op jit(solution)/shard_map/pallas_call | solution.py:208
  66.4 16.2 %collective-permute-done.15 = bf16[512,128]{1,0:T(8,128)(2,1)S(1)} collective-permute-done((bf16[512,128]{1,0:T(8,128)(2,1)}, bf16[512,128]{1,0:T(8,128)(2,1)S(1)}, u32[]{:S(2)}, u32[]{:S(2)}) %collective-permute-start.15) | collective-permute-done | bytes 131104 | tf_op jit(solution)/shard_map/ppermute | solution.py:29
  82.6 16.2 %collective-permute-start.4 = (bf16[1,128,1280]{2,1,0:T(8,128)(2,1)S(1)}, bf16[1,128,1280]{2,1,0:T(8,128)(2,1)S(1)}, u32[]{:S(2)}, u32[]{:S(2)}) collective-permute-start(bf16[1,128,1280]{2,1,0:T(8,128)(2,1)S(1)} %dynamic-slice_bitcast_fusion.1), channel_id=1, source_target_pairs={{0,8},{8,0},{16,24},{24,16},{1,9},{9,1},{17,25},{25,17},{2,10},{10... | collective-permute-start | bytes 983048 | tf_op jit(solution)/shard_map/ppermute | solution.py:29
  98.8 0.9 pad_maximum_fusion.8.refs_0_
  99.8 4.4 %collective-permute-start.17 = (bf16[2,512,128]{2,1,0:T(8,128)(2,1)S(1)}, bf16[2,512,128]{2,1,0:T(8,128)(2,1)S(1)}, u32[]{:S(2)}, u32[]{:S(2)}) collective-permute-start(bf16[2,512,128]{2,1,0:T(8,128)(2,1)S(1)} %pad_maximum_fusion.8.refs_0_), channel_id=1, source_target_pairs={{0,16},{8,24},{16,0},{24,8},{1,17},{9,25},{17,1},{25,9},{2,18},{10... | collective-permute-start | bytes 786440 | tf_op jit(solution)/shard_map/ppermute | solution.py:29
  104.2 0.7 pad_maximum_fusion.9.shift_ref
  105.6 1.1 maximum_bitcast_fusion
  106.7 6.2 %collective-permute-done.4 = bf16[1,128,1280]{2,1,0:T(8,128)(2,1)S(1)} collective-permute-done((bf16[1,128,1280]{2,1,0:T(8,128)(2,1)S(1)}, bf16[1,128,1280]{2,1,0:T(8,128)(2,1)S(1)}, u32[]{:S(2)}, u32[]{:S(2)}) %collective-permute-start.4) | collective-permute-done | bytes 327712 | tf_op jit(solution)/shard_map/ppermute | solution.py:29
  112.9 0.7 collective-permute-start.9
  113.6 2.1 collective-permute-done.16.refs_1_
  116.7 28.5 %shard_map.166.qkv_ref = f32[2,1024,384]{2,1,0:T(8,128)} custom-call(bf16[1024,5120]{1,0:T(8,128)(2,1)} %bitcast.34, f32[2,5120]{1,0:T(2,128)} %pad_maximum_fusion.9.shift_ref, f32[1,5120]{1,0:T(1,128)} %bitcast.54, bf16[3,5120,128]{2,1,0:T(8,128)(2,1)} %weight_ref.2), custom_call_target="tpu_custom_call" | custom-call | flops 8053063680 | bytes 14417920 | tf_op jit(solution)/shard_map/pallas_call | solution.py:121
  145.2 0.9 pad_maximum_fusion.4
  146.1 4.4 %collective-permute-start.18 = (bf16[2,512,128]{2,1,0:T(8,128)(2,1)S(1)}, bf16[2,512,128]{2,1,0:T(8,128)(2,1)S(1)}, u32[]{:S(2)}, u32[]{:S(2)}) collective-permute-start(bf16[2,512,128]{2,1,0:T(8,128)(2,1)S(1)} %pad_maximum_fusion.8.refs_0_), channel_id=1, source_target_pairs={{0,24},{8,16},{16,8},{24,0},{1,25},{9,17},{17,9},{25,1},{2,26},{10... | collective-permute-start | bytes 786440 | tf_op jit(solution)/shard_map/ppermute | solution.py:29
  150.5 1.4 pad_maximum_fusion.1.refs_6_
  151.9 5.2 %collective-permute-done.18.refs_3_ = bf16[2,512,128]{2,1,0:T(8,128)(2,1)S(1)} collective-permute-done((bf16[2,512,128]{2,1,0:T(8,128)(2,1)S(1)}, bf16[2,512,128]{2,1,0:T(8,128)(2,1)S(1)}, u32[]{:S(2)}, u32[]{:S(2)}) %collective-permute-start.18) | collective-permute-done | bytes 262176 | tf_op jit(solution)/shard_map/ppermute | solution.py:29
  157.1 0.7 copy-done.9
  157.8 1.5 collective-permute-start.5
  159.3 12.1 %shard_map.170 = (bf16[2,512,1280]{2,1,0:T(8,128)(2,1)}, bf16[2,256,1280]{2,1,0:T(8,128)(2,1)}, f32[512,256]{1,0:T(8,128)}) custom-call(s32[6]{0:T(128)} %stack.45.scal, f32[1]{0:T(128)S(6)} %div.38.noise_ref, bf16[2,512,128]{2,1,0:T(8,128)(2,1)} %copy-done.6, bf16[2,512,128]{2,1,0:T(8,128)(2,1)} %copy-done.7, bf16[2,512,128]{2,1,0:T(8,128)(2,1)} %copy-done.8, ...), custom_call_target="tpu_custom_call" | custom-call | flops 4026531840 | bytes 15728640 | tf_op jit(solution)/shard_map/pallas_call | solution.py:348
  172.1 12.3 %shard_map.171 = (bf16[2,512,1280]{2,1,0:T(8,128)(2,1)}, bf16[2,256,1280]{2,1,0:T(8,128)(2,1)}, f32[512,256]{1,0:T(8,128)}) custom-call(s32[6]{0:T(128)} %stack.45.scal, f32[1]{0:T(128)S(6)} %div.38.noise_ref, bf16[2,512,128]{2,1,0:T(8,128)(2,1)} %copy-done.6, bf16[2,512,128]{2,1,0:T(8,128)(2,1)} %copy-done.7, bf16[2,512,128]{2,1,0:T(8,128)(2,1)} %copy-done.8, ...), custom_call_target="tpu_custom_call" | custom-call | flops 4026531840 | bytes 15728640 | tf_op jit(solution)/shard_map/pallas_call | solution.py:348
  184.5 1.1 dynamic-slice_convert_fusion
  185.6 1.5 collective-permute-start.31
  187.2 1.2 pad_maximum_fusion.refs_4_
  188.4 1.6 collective-permute-start.6
  190.0 15.0 %collective-permute-done.31 = bf16[512,128]{1,0:T(8,128)(2,1)S(1)} collective-permute-done((bf16[512,128]{1,0:T(8,128)(2,1)S(1)}, bf16[512,128]{1,0:T(8,128)(2,1)S(1)}, u32[]{:S(2)}, u32[]{:S(2)}) %collective-permute-start.31) | collective-permute-done | bytes 131104 | tf_op jit(solution)/shard_map/ppermute | solution.py:29
  205.1 0.7 copy-done.15
  205.8 8.7 %shard_map.174.grad_ref = bf16[384,1024]{1,0:T(8,128)(2,1)} custom-call(bf16[1024,128]{1,0:T(8,128)(2,1)} %get-tuple-element.34.q_ref, bf16[1024,128]{1,0:T(8,128)(2,1)} %get-tuple-element.35.k_ref, bf16[1024,128]{1,0:T(8,128)(2,1)} %get-tuple-element.36.v_ref, bf16[1024,128]{1,0:T(8,128)(2,1)} %copy-done.15, f32[1,1024,384]{2,1,0:T(8,128)} %get-tuple-element.26.qkv_ref, ...), custom_call_target="tpu_custom_call" | custom-call | flops 2684354560 | bytes 1572864 | tf_op jit(solution)/shard_map/pallas_call | solution.py:525
  214.4 7.0 %shard_map.176 = bf16[2,384,1280]{2,1,0:T(8,128)(2,1)} custom-call(s32[6]{0:T(128)} %stack.45.scal, bf16[384,1024]{1,0:T(8,128)(2,1)} %shard_map.174.grad_ref, bf16[1024,5120]{1,0:T(8,128)(2,1)} %get-tuple-element.38.hidden_ref), custom_call_target="tpu_custom_call" | custom-call | flops 2013265920 | bytes 7208960 | tf_op jit(solution)/shard_map/pallas_call | solution.py:557
  221.4 10.2 %shard_map.167 = (bf16[512,128]{1,0:T(8,128)(2,1)}, bf16[512,128]{1,0:T(8,128)(2,1)}) custom-call(s32[6]{0:T(128)} %stack.45.scal, f32[2,1024,384]{2,1,0:T(8,128)} %shard_map.166.qkv_ref, f32[2,128]{1,0:T(2,128)} %gain_ref.3, f32[1024,128]{1,0:T(8,128)} %get-tuple-element.44.cos_ref, f32[1024,128]{1,0:T(8,128)} %get-tuple-element.43.sin_ref), custom_call_target="tpu_custom_call" | custom-call | flops 4294967296 | bytes 3145728 | tf_op jit(solution)/shard_map/pallas_call | solution.py:208
  231.7 1.5 collective-permute-start
  233.2 1.4 add_convert_fusion.1
  234.6 1.6 collective-permute-start.35
  236.2 1.6 collective-permute-done
  237.8 6.8 %collective-permute-start.1 = (bf16[2,512,128]{2,1,0:T(8,128)(2,1)S(1)}, bf16[2,512,128]{2,1,0:T(8,128)(2,1)S(1)}, u32[]{:S(2)}, u32[]{:S(2)}) collective-permute-start(bf16[2,512,128]{2,1,0:T(8,128)(2,1)S(1)} %pad_maximum_fusion.7.refs_0_), channel_id=1, source_target_pairs={{0,8},{8,0},{16,24},{24,16},{1,9},{9,1},{17,25},{25,17},{2,10},{10... | collective-permute-start | bytes 786440 | tf_op jit(solution)/shard_map/ppermute | solution.py:29
  244.6 6.1 %collective-permute-done.1.refs_1_ = bf16[2,512,128]{2,1,0:T(8,128)(2,1)S(1)} collective-permute-done((bf16[2,512,128]{2,1,0:T(8,128)(2,1)S(1)}, bf16[2,512,128]{2,1,0:T(8,128)(2,1)S(1)}, u32[]{:S(2)}, u32[]{:S(2)}) %collective-permute-start.1) | collective-permute-done | bytes 262176 | tf_op jit(solution)/shard_map/ppermute | solution.py:29
  250.7 2.6 collective-permute-start.2
  253.4 11.2 %collective-permute-done.2.refs_2_ = bf16[2,512,128]{2,1,0:T(8,128)(2,1)S(1)} collective-permute-done((bf16[2,512,128]{2,1,0:T(8,128)(2,1)S(1)}, bf16[2,512,128]{2,1,0:T(8,128)(2,1)S(1)}, u32[]{:S(2)}, u32[]{:S(2)}) %collective-permute-start.2) | collective-permute-done | bytes 262176 | tf_op jit(solution)/shard_map/ppermute | solution.py:29
  265.7 7.0 %shard_map.175.refs_0_ = bf16[2,384,1280]{2,1,0:T(8,128)(2,1)} custom-call(s32[6]{0:T(128)} %stack.45.scal, bf16[384,1024]{1,0:T(8,128)(2,1)} %shard_map.174.grad_ref, bf16[1024,5120]{1,0:T(8,128)(2,1)} %get-tuple-element.38.hidden_ref), custom_call_target="tpu_custom_call" | custom-call | flops 2013265920 | bytes 7208960 | tf_op jit(solution)/shard_map/pallas_call | solution.py:557
  272.7 1.9 fusion.2
  274.6 2.3 collective-permute-start.3
  277.0 2.7 add_convert_fusion
  279.6 5.2 %collective-permute-done.3.refs_3_ = bf16[2,512,128]{2,1,0:T(8,128)(2,1)S(1)} collective-permute-done((bf16[2,512,128]{2,1,0:T(8,128)(2,1)S(1)}, bf16[2,512,128]{2,1,0:T(8,128)(2,1)S(1)}, u32[]{:S(2)}, u32[]{:S(2)}) %collective-permute-start.3) | collective-permute-done | bytes 262176 | tf_op jit(solution)/shard_map/ppermute | solution.py:29
  284.9 1.5 collective-permute-start.36
  286.4 1.5 collective-permute-start.33
  287.9 19.8 %shard_map.172 = (bf16[512,5120]{1,0:T(8,128)(2,1)}, f32[8,128]{1,0:T(8,128)}) custom-call(s32[6]{0:T(128)} %stack.45.scal, f32[1]{0:T(128)S(6)} %div.38.noise_ref, bf16[2,512,128]{2,1,0:T(8,128)(2,1)} %copy-done.10, bf16[2,512,128]{2,1,0:T(8,128)(2,1)} %copy-done.12, bf16[2,512,128]{2,1,0:T(8,128)(2,1)} %copy-done.13, bf16[2,512,128]{2,1,0:T(8,128)(2,1)} %copy-done.14, ...), custom_call_target="tpu_custom_call" | custom-call | flops 5368709120 | bytes 31457280 | tf_op jit(solution)/shard_map/pallas_call | solution.py:437
  308.2 3.4 %collective-permute-done.30.refs_1_ = f32[8,128]{1,0:T(8,128)S(1)} collective-permute-done((f32[8,128]{1,0:T(8,128)}, f32[8,128]{1,0:T(8,128)S(1)}, u32[]{:S(2)}, u32[]{:S(2)}) %collective-permute-start.30) | collective-permute-done | bytes 4128 | tf_op jit(solution)/shard_map/ppermute | solution.py:29
  312.2 7.9 %shard_map.173 = bf16[512,5120]{1,0:T(8,128)(2,1)} custom-call(f32[8,128]{1,0:T(8,128)} %get-tuple-element.32.refs_0_, f32[8,128]{1,0:T(8,128)} %copy-done.18, bf16[512,5120]{1,0:T(8,128)(2,1)} %get-tuple-element.33.refs_2_), custom_call_target="tpu_custom_call" | custom-call | flops 10485760 | bytes 10485760 | tf_op jit(solution)/shard_map/pallas_call | solution.py:596
  320.1 2.2 bitcast_add_fusion
  322.2 3.2 shard_map.177
  (89 shorter events, 7.0 us)
Async XLA Ops:
  0.6 1.3 copy-start
  2.0 33.1 %collective-permute-start.22 = (bf16[1,128,1280]{2,1,0:T(8,128)(2,1)S(1)}, bf16[1,128,1280]{2,1,0:T(8,128)(2,1)S(1)}, u32[]{:S(2)}, u32[]{:S(2)}) collective-permute-start(bf16[1,128,1280]{2,1,0:T(8,128)(2,1)S(1)} %dynamic-slice_bitcast_fusion), channel_id=1, source_target_pairs={{0,16},{8,24},{16,0},{24,8},{1,17},{9,25},{17,1},{25,9},{2,18},{10... | collective-permute-start | bytes 983048 | tf_op jit(solution)/shard_map/ppermute | solution.py:29
  6.1 29.0 %collective-permute-start.23 = (bf16[1,128,1280]{2,1,0:T(8,128)(2,1)S(1)}, bf16[1,128,1280]{2,1,0:T(8,128)(2,1)S(1)}, u32[]{:S(2)}, u32[]{:S(2)}) collective-permute-start(bf16[1,128,1280]{2,1,0:T(8,128)(2,1)S(1)} %dynamic-slice_bitcast_fusion), channel_id=1, source_target_pairs={{0,24},{8,16},{16,8},{24,0},{1,25},{9,17},{17,9},{25,1},{2,26},{10... | collective-permute-start | bytes 983048 | tf_op jit(solution)/shard_map/ppermute | solution.py:29
  7.5 29.3 %collective-permute-start.19 = (bf16[1,128,1280]{2,1,0:T(8,128)(2,1)S(1)}, bf16[1,128,1280]{2,1,0:T(8,128)(2,1)S(1)}, u32[]{:S(2)}, u32[]{:S(2)}) collective-permute-start(bf16[1,128,1280]{2,1,0:T(8,128)(2,1)S(1)} %dynamic-slice_bitcast_fusion), channel_id=1, source_target_pairs={{0,8},{8,0},{16,24},{24,16},{1,9},{9,1},{17,25},{25,17},{2,10},{10... | collective-permute-start | bytes 983048 | tf_op jit(solution)/shard_map/ppermute | solution.py:29
  10.5 93.7 %copy-start.16 = (f32[5120]{0:T(1024)}, f32[5120]{0:T(1024)S(1)}, u32[]{:S(2)}) copy-start(f32[5120]{0:T(1024)S(1)} %get-tuple-element.46) | copy-start | bytes 61444
  30.2 69.6 %collective-permute-start.7 = (bf16[1,128,1280]{2,1,0:T(8,128)(2,1)S(1)}, bf16[1,128,1280]{2,1,0:T(8,128)(2,1)}, u32[]{:S(2)}, u32[]{:S(2)}) collective-permute-start(bf16[1,128,1280]{2,1,0:T(8,128)(2,1)S(1)} %dynamic-slice_bitcast_fusion.1), channel_id=1, source_target_pairs={{0,16},{8,24},{16,0},{24,8},{1,17},{9,25},{17,1},{25,9},{2,18},{10... | collective-permute-start | bytes 983048 | tf_op jit(solution)/shard_map/ppermute | solution.py:29
  33.0 66.8 %collective-permute-start.8 = (bf16[1,128,1280]{2,1,0:T(8,128)(2,1)S(1)}, bf16[1,128,1280]{2,1,0:T(8,128)(2,1)}, u32[]{:S(2)}, u32[]{:S(2)}) collective-permute-start(bf16[1,128,1280]{2,1,0:T(8,128)(2,1)S(1)} %dynamic-slice_bitcast_fusion.1), channel_id=1, source_target_pairs={{0,24},{8,16},{16,8},{24,0},{1,25},{9,17},{17,9},{25,1},{2,26},{10... | collective-permute-start | bytes 983048 | tf_op jit(solution)/shard_map/ppermute | solution.py:29
  35.2 15.2 %collective-permute-start.24 = (bf16[1,2,128,1280]{3,2,1,0:T(8,128)(2,1)S(1)}, bf16[1,2,128,1280]{3,2,1,0:T(8,128)(2,1)S(1)}, u32[]{:S(2)}, u32[]{:S(2)}) collective-permute-start(bf16[1,2,128,1280]{3,2,1,0:T(8,128)(2,1)S(1)} %maximum_bitcast_fusion.1), channel_id=1, source_target_pairs={{0,2},{1,3},{2,0},{3,1},{4,6},{5,7},{6,4},{7,5},{8,10},{9,11},{10,... | collective-permute-start | bytes 1966088 | tf_op jit(solution)/shard_map/ppermute | solution.py:29
  36.8 15.8 %collective-permute-start.20 = (bf16[2,128,1280]{2,1,0:T(8,128)(2,1)S(1)}, bf16[2,128,1280]{2,1,0:T(8,128)(2,1)S(1)}, u32[]{:S(2)}, u32[]{:S(2)}) collective-permute-start(bf16[2,128,1280]{2,1,0:T(8,128)(2,1)S(1)} %pad_maximum_fusion.5), channel_id=1, source_target_pairs={{0,4},{4,0},{1,5},{5,1},{2,6},{6,2},{3,7},{7,3},{8,12},{12,8},{9,1... | collective-permute-start | bytes 1966088 | tf_op jit(solution)/shard_map/ppermute | solution.py:29
  50.4 65.3 %copy-start.4 = (bf16[2,2,128,1280]{3,2,1,0:T(8,128)(2,1)}, bf16[2,2,128,1280]{3,2,1,0:T(8,128)(2,1)S(1)}, u32[]{:S(2)}) copy-start(bf16[2,2,128,1280]{3,2,1,0:T(8,128)(2,1)S(1)} %pad_maximum_fusion.3.refs_6_) | copy-start | bytes 3932164
  50.5 65.8 %collective-permute-start.25 = (bf16[2,2,128,1280]{3,2,1,0:T(8,128)(2,1)S(1)}, bf16[2,2,128,1280]{3,2,1,0:T(8,128)(2,1)}, u32[]{:S(2)}, u32[]{:S(2)}) collective-permute-start(bf16[2,2,128,1280]{3,2,1,0:T(8,128)(2,1)S(1)} %pad_maximum_fusion.3.refs_6_), channel_id=1, source_target_pairs={{0,4},{4,0},{1,5},{5,1},{2,6},{6,2},{3,7},{7,3},{8,12},{12,8},{9,1... | collective-permute-start | bytes 3932168 | tf_op jit(solution)/shard_map/ppermute | solution.py:29
  53.8 62.5 %collective-permute-start.21 = (bf16[4,128,1280]{2,1,0:T(8,128)(2,1)}, bf16[4,128,1280]{2,1,0:T(8,128)(2,1)}, u32[]{:S(2)}, u32[]{:S(2)}) collective-permute-start(bf16[4,128,1280]{2,1,0:T(8,128)(2,1)} %pad_maximum_fusion.2.refs_4_), channel_id=1, source_target_pairs={{0,2},{1,3},{2,0},{3,1},{4,6},{5,7},{6,4},{7,5},{8,10},{9,11},{10,... | collective-permute-start | bytes 3932168 | tf_op jit(solution)/shard_map/ppermute | solution.py:29
  58.2 46.0 %copy-start.11 = (f32[5120]{0:T(1024)S(1)}, f32[5120]{0:T(1024)}, u32[]{:S(2)}) copy-start(f32[5120]{0:T(1024)} %get-tuple-element.45) | copy-start | bytes 61444
  65.8 16.8 %collective-permute-start.15 = (bf16[512,128]{1,0:T(8,128)(2,1)}, bf16[512,128]{1,0:T(8,128)(2,1)S(1)}, u32[]{:S(2)}, u32[]{:S(2)}) collective-permute-start(bf16[512,128]{1,0:T(8,128)(2,1)} %get-tuple-element.28), channel_id=1, source_target_pairs={{0,4},{4,0},{1,5},{5,1},{2,6},{6,2},{3,7},{7,3},{8,12},{12,8},{9,1... | collective-permute-start | bytes 393224 | tf_op jit(solution)/shard_map/ppermute | solution.py:29
  82.6 30.3 %collective-permute-start.4 = (bf16[1,128,1280]{2,1,0:T(8,128)(2,1)S(1)}, bf16[1,128,1280]{2,1,0:T(8,128)(2,1)S(1)}, u32[]{:S(2)}, u32[]{:S(2)}) collective-permute-start(bf16[1,128,1280]{2,1,0:T(8,128)(2,1)S(1)} %dynamic-slice_bitcast_fusion.1), channel_id=1, source_target_pairs={{0,8},{8,0},{16,24},{24,16},{1,9},{9,1},{17,25},{25,17},{2,10},{10... | collective-permute-start | bytes 983048 | tf_op jit(solution)/shard_map/ppermute | solution.py:29
  99.7 46.4 %copy-start.6 = (bf16[2,512,128]{2,1,0:T(8,128)(2,1)}, bf16[2,512,128]{2,1,0:T(8,128)(2,1)S(1)}, u32[]{:S(2)}) copy-start(bf16[2,512,128]{2,1,0:T(8,128)(2,1)S(1)} %pad_maximum_fusion.8.refs_0_) | copy-start | bytes 786436
  99.7 16.0 %collective-permute-start.16 = (bf16[2,512,128]{2,1,0:T(8,128)(2,1)S(1)}, bf16[2,512,128]{2,1,0:T(8,128)(2,1)S(1)}, u32[]{:S(2)}, u32[]{:S(2)}) collective-permute-start(bf16[2,512,128]{2,1,0:T(8,128)(2,1)S(1)} %pad_maximum_fusion.8.refs_0_), channel_id=1, source_target_pairs={{0,8},{8,0},{16,24},{24,16},{1,9},{9,1},{17,25},{25,17},{2,10},{10... | collective-permute-start | bytes 786440 | tf_op jit(solution)/shard_map/ppermute | solution.py:29
  99.8 15.9 %collective-permute-start.17 = (bf16[2,512,128]{2,1,0:T(8,128)(2,1)S(1)}, bf16[2,512,128]{2,1,0:T(8,128)(2,1)S(1)}, u32[]{:S(2)}, u32[]{:S(2)}) collective-permute-start(bf16[2,512,128]{2,1,0:T(8,128)(2,1)S(1)} %pad_maximum_fusion.8.refs_0_), channel_id=1, source_target_pairs={{0,16},{8,24},{16,0},{24,8},{1,17},{9,25},{17,1},{25,9},{2,18},{10... | collective-permute-start | bytes 786440 | tf_op jit(solution)/shard_map/ppermute | solution.py:29
  106.7 38.5 %copy-start.5 = (bf16[1,2,128,1280]{3,2,1,0:T(8,128)(2,1)}, bf16[1,2,128,1280]{3,2,1,0:T(8,128)(2,1)S(1)}, u32[]{:S(2)}) copy-start(bf16[1,2,128,1280]{3,2,1,0:T(8,128)(2,1)S(1)} %maximum_bitcast_fusion) | copy-start | bytes 1966084
  112.9 33.2 %collective-permute-start.9 = (bf16[1,2,128,1280]{3,2,1,0:T(8,128)(2,1)S(1)}, bf16[1,2,128,1280]{3,2,1,0:T(8,128)(2,1)}, u32[]{:S(2)}, u32[]{:S(2)}) collective-permute-start(bf16[1,2,128,1280]{3,2,1,0:T(8,128)(2,1)S(1)} %maximum_bitcast_fusion), channel_id=1, source_target_pairs={{0,2},{1,3},{2,0},{3,1},{4,6},{5,7},{6,4},{7,5},{8,10},{9,11},{10,... | collective-permute-start | bytes 1966088 | tf_op jit(solution)/shard_map/ppermute | solution.py:29
  115.7 29.5 %copy-start.7 = (bf16[2,512,128]{2,1,0:T(8,128)(2,1)}, bf16[2,512,128]{2,1,0:T(8,128)(2,1)S(1)}, u32[]{:S(2)}) copy-start(bf16[2,512,128]{2,1,0:T(8,128)(2,1)S(1)} %collective-permute-done.16.refs_1_) | copy-start | bytes 786436
  115.7 55.7 %collective-permute-start.28 = (bf16[2,2,128,1280]{3,2,1,0:T(8,128)(2,1)S(1)}, bf16[2,2,128,1280]{3,2,1,0:T(8,128)(2,1)}, u32[]{:S(2)}, u32[]{:S(2)}) collective-permute-start(bf16[2,2,128,1280]{3,2,1,0:T(8,128)(2,1)S(1)} %pad_maximum_fusion.3.refs_6_), channel_id=1, source_target_pairs={{0,1},{1,0},{2,3},{3,2},{4,5},{5,4},{6,7},{7,6},{8,9},{9,8},{10,11... | collective-permute-start | bytes 3932168 | tf_op jit(solution)/shard_map/ppermute | solution.py:29
  115.7 29.5 %copy-start.8 = (bf16[2,512,128]{2,1,0:T(8,128)(2,1)}, bf16[2,512,128]{2,1,0:T(8,128)(2,1)S(1)}, u32[]{:S(2)}) copy-start(bf16[2,512,128]{2,1,0:T(8,128)(2,1)S(1)} %collective-permute-done.17.refs_2_) | copy-start | bytes 786436
  115.7 56.3 %collective-permute-start.26 = (bf16[4,128,1280]{2,1,0:T(8,128)(2,1)}, bf16[4,128,1280]{2,1,0:T(8,128)(2,1)}, u32[]{:S(2)}, u32[]{:S(2)}) collective-permute-start(bf16[4,128,1280]{2,1,0:T(8,128)(2,1)} %pad_maximum_fusion.2.refs_4_), channel_id=1, source_target_pairs={{0,1},{1,0},{2,3},{3,2},{4,5},{5,4},{6,7},{7,6},{8,9},{9,8},{10,11... | collective-permute-start | bytes 3932168 | tf_op jit(solution)/shard_map/ppermute | solution.py:29
  116.2 55.9 %collective-permute-start.29 = (bf16[2,2,128,1280]{3,2,1,0:T(8,128)(2,1)}, bf16[2,2,128,1280]{3,2,1,0:T(8,128)(2,1)}, u32[]{:S(2)}, u32[]{:S(2)}) collective-permute-start(bf16[2,2,128,1280]{3,2,1,0:T(8,128)(2,1)} %collective-permute-done.25.refs_7_), channel_id=1, source_target_pairs={{0,1},{1,0},{2,3},{3,2},{4,5},{5,4},{6,7},{7,6},{8,9},{9,8},{10,11... | collective-permute-start | bytes 3932168 | tf_op jit(solution)/shard_map/ppermute | solution.py:29
  116.3 55.8 %collective-permute-start.27 = (bf16[4,128,1280]{2,1,0:T(8,128)(2,1)}, bf16[4,128,1280]{2,1,0:T(8,128)(2,1)}, u32[]{:S(2)}, u32[]{:S(2)}) collective-permute-start(bf16[4,128,1280]{2,1,0:T(8,128)(2,1)} %collective-permute-done.21.refs_5_), channel_id=1, source_target_pairs={{0,1},{1,0},{2,3},{3,2},{4,5},{5,4},{6,7},{7,6},{8,9},{9,8},{10,11... | collective-permute-start | bytes 3932168 | tf_op jit(solution)/shard_map/ppermute | solution.py:29
  146.1 11.0 %collective-permute-start.18 = (bf16[2,512,128]{2,1,0:T(8,128)(2,1)S(1)}, bf16[2,512,128]{2,1,0:T(8,128)(2,1)S(1)}, u32[]{:S(2)}, u32[]{:S(2)}) collective-permute-start(bf16[2,512,128]{2,1,0:T(8,128)(2,1)S(1)} %pad_maximum_fusion.8.refs_0_), channel_id=1, source_target_pairs={{0,24},{8,16},{16,8},{24,0},{1,25},{9,17},{17,9},{25,1},{2,26},{10... | collective-permute-start | bytes 786440 | tf_op jit(solution)/shard_map/ppermute | solution.py:29
  151.9 112.7 %copy-start.2 = (bf16[2,2,128,1280]{3,2,1,0:T(8,128)(2,1)}, bf16[2,2,128,1280]{3,2,1,0:T(8,128)(2,1)S(1)}, u32[]{:S(2)}) copy-start(bf16[2,2,128,1280]{3,2,1,0:T(8,128)(2,1)S(1)} %pad_maximum_fusion.1.refs_6_) | copy-start | bytes 3932164
  157.1 0.7 copy-start.9
  157.8 29.3 %collective-permute-start.5 = (bf16[2,128,1280]{2,1,0:T(8,128)(2,1)}, bf16[2,128,1280]{2,1,0:T(8,128)(2,1)}, u32[]{:S(2)}, u32[]{:S(2)}) collective-permute-start(bf16[2,128,1280]{2,1,0:T(8,128)(2,1)} %pad_maximum_fusion.4), channel_id=1, source_target_pairs={{0,4},{4,0},{1,5},{5,1},{2,6},{6,2},{3,7},{7,3},{8,12},{12,8},{9,1... | collective-permute-start | bytes 1966088 | tf_op jit(solution)/shard_map/ppermute | solution.py:29
  171.5 93.1 %collective-permute-start.10 = (bf16[2,2,128,1280]{3,2,1,0:T(8,128)(2,1)S(1)}, bf16[2,2,128,1280]{3,2,1,0:T(8,128)(2,1)}, u32[]{:S(2)}, u32[]{:S(2)}) collective-permute-start(bf16[2,2,128,1280]{3,2,1,0:T(8,128)(2,1)S(1)} %pad_maximum_fusion.1.refs_6_), channel_id=1, source_target_pairs={{0,4},{4,0},{1,5},{5,1},{2,6},{6,2},{3,7},{7,3},{8,12},{12,8},{9,1... | collective-permute-start | bytes 3932168 | tf_op jit(solution)/shard_map/ppermute | solution.py:29
  184.4 48.8 %collective-permute-start.34 = (bf16[2,256,1280]{2,1,0:T(8,128)(2,1)}, bf16[2,256,1280]{2,1,0:T(8,128)(2,1)}, u32[]{:S(2)}, u32[]{:S(2)}) collective-permute-start(bf16[2,256,1280]{2,1,0:T(8,128)(2,1)} %get-tuple-element.40), channel_id=1, source_target_pairs={{0,1},{1,0},{2,3},{3,2},{4,5},{5,4},{6,7},{7,6},{8,9},{9,8},{10,11... | collective-permute-start | bytes 3932168 | tf_op jit(solution)/shard_map/ppermute | solution.py:29
  185.6 19.4 %collective-permute-start.31 = (bf16[512,128]{1,0:T(8,128)(2,1)S(1)}, bf16[512,128]{1,0:T(8,128)(2,1)S(1)}, u32[]{:S(2)}, u32[]{:S(2)}) collective-permute-start(bf16[512,128]{1,0:T(8,128)(2,1)S(1)} %get-tuple-element.41), channel_id=1, source_target_pairs={{0,4},{4,0},{1,5},{5,1},{2,6},{6,2},{3,7},{7,3},{8,12},{12,8},{9,1... | collective-permute-start | bytes 393224 | tf_op jit(solution)/shard_map/ppermute | solution.py:29
  188.4 76.2 %copy-start.3 = (bf16[4,128,1280]{2,1,0:T(8,128)(2,1)}, bf16[4,128,1280]{2,1,0:T(8,128)(2,1)S(1)}, u32[]{:S(2)}) copy-start(bf16[4,128,1280]{2,1,0:T(8,128)(2,1)S(1)} %pad_maximum_fusion.refs_4_) | copy-start | bytes 3932164
  188.4 76.7 %collective-permute-start.6 = (bf16[4,128,1280]{2,1,0:T(8,128)(2,1)S(1)}, bf16[4,128,1280]{2,1,0:T(8,128)(2,1)}, u32[]{:S(2)}, u32[]{:S(2)}) collective-permute-start(bf16[4,128,1280]{2,1,0:T(8,128)(2,1)S(1)} %pad_maximum_fusion.refs_4_), channel_id=1, source_target_pairs={{0,2},{1,3},{2,0},{3,1},{4,6},{5,7},{6,4},{7,5},{8,10},{9,11},{10,... | collective-permute-start | bytes 3932168 | tf_op jit(solution)/shard_map/ppermute | solution.py:29
  205.0 0.7 copy-start.15
  221.4 53.2 %collective-permute-start.32 = (bf16[2,384,1280]{2,1,0:T(8,128)(2,1)}, bf16[2,384,1280]{2,1,0:T(8,128)(2,1)}, u32[]{:S(2)}, u32[]{:S(2)}) collective-permute-start(bf16[2,384,1280]{2,1,0:T(8,128)(2,1)} %shard_map.176), channel_id=1, source_target_pairs={{0,1},{1,0},{2,3},{3,2},{4,5},{5,4},{6,7},{7,6},{8,9},{9,8},{10,11... | collective-permute-start | bytes 5898248 | tf_op jit(solution)/shard_map/ppermute | solution.py:29
  231.7 6.1 %copy-start.17 = (bf16[512,128]{1,0:T(8,128)(2,1)S(1)}, bf16[512,128]{1,0:T(8,128)(2,1)}, u32[]{:S(2)}) copy-start(bf16[512,128]{1,0:T(8,128)(2,1)} %get-tuple-element.22) | copy-start | bytes 393220
  231.7 6.1 %collective-permute-start = (bf16[512,128]{1,0:T(8,128)(2,1)}, bf16[512,128]{1,0:T(8,128)(2,1)S(1)}, u32[]{:S(2)}, u32[]{:S(2)}) collective-permute-start(bf16[512,128]{1,0:T(8,128)(2,1)} %get-tuple-element.23), channel_id=1, source_target_pairs={{0,4},{4,0},{1,5},{5,1},{2,6},{6,2},{3,7},{7,3},{8,12},{12,8},{9,1... | collective-permute-start | bytes 393224 | tf_op jit(solution)/shard_map/ppermute | solution.py:29
  234.6 30.6 %collective-permute-start.35 = (bf16[1,256,1280]{2,1,0:T(8,128)(2,1)S(1)}, bf16[1,256,1280]{2,1,0:T(8,128)(2,1)S(1)}, u32[]{:S(2)}, u32[]{:S(2)}) collective-permute-start(bf16[1,256,1280]{2,1,0:T(8,128)(2,1)S(1)} %add_convert_fusion.1), channel_id=1, source_target_pairs={{0,2},{1,3},{2,0},{3,1},{4,6},{5,7},{6,4},{7,5},{8,10},{9,11},{10,... | collective-permute-start | bytes 1966088 | tf_op jit(solution)/shard_map/ppermute | solution.py:29
  237.8 36.8 %copy-start.10 = (bf16[2,512,128]{2,1,0:T(8,128)(2,1)}, bf16[2,512,128]{2,1,0:T(8,128)(2,1)S(1)}, u32[]{:S(2)}) copy-start(bf16[2,512,128]{2,1,0:T(8,128)(2,1)S(1)} %pad_maximum_fusion.7.refs_0_) | copy-start | bytes 786436
  237.8 12.9 %collective-permute-start.1 = (bf16[2,512,128]{2,1,0:T(8,128)(2,1)S(1)}, bf16[2,512,128]{2,1,0:T(8,128)(2,1)S(1)}, u32[]{:S(2)}, u32[]{:S(2)}) collective-permute-start(bf16[2,512,128]{2,1,0:T(8,128)(2,1)S(1)} %pad_maximum_fusion.7.refs_0_), channel_id=1, source_target_pairs={{0,8},{8,0},{16,24},{24,16},{1,9},{9,1},{17,25},{25,17},{2,10},{10... | collective-permute-start | bytes 786440 | tf_op jit(solution)/shard_map/ppermute | solution.py:29
  250.7 14.4 %copy-start.12 = (bf16[2,512,128]{2,1,0:T(8,128)(2,1)}, bf16[2,512,128]{2,1,0:T(8,128)(2,1)S(1)}, u32[]{:S(2)}) copy-start(bf16[2,512,128]{2,1,0:T(8,128)(2,1)S(1)} %collective-permute-done.1.refs_1_) | copy-start | bytes 786436
  250.7 13.8 %collective-permute-start.2 = (bf16[2,512,128]{2,1,0:T(8,128)(2,1)S(1)}, bf16[2,512,128]{2,1,0:T(8,128)(2,1)S(1)}, u32[]{:S(2)}, u32[]{:S(2)}) collective-permute-start(bf16[2,512,128]{2,1,0:T(8,128)(2,1)S(1)} %pad_maximum_fusion.7.refs_0_), channel_id=1, source_target_pairs={{0,16},{8,24},{16,0},{24,8},{1,17},{9,25},{17,1},{25,9},{2,18},{10... | collective-permute-start | bytes 786440 | tf_op jit(solution)/shard_map/ppermute | solution.py:29
  264.6 0.7 copy-start.13
  264.6 21.8 %collective-permute-start.13 = (bf16[2,2,128,1280]{3,2,1,0:T(8,128)(2,1)S(1)}, bf16[2,2,128,1280]{3,2,1,0:T(8,128)(2,1)}, u32[]{:S(2)}, u32[]{:S(2)}) collective-permute-start(bf16[2,2,128,1280]{3,2,1,0:T(8,128)(2,1)S(1)} %pad_maximum_fusion.1.refs_6_), channel_id=1, source_target_pairs={{0,1},{1,0},{2,3},{3,2},{4,5},{5,4},{6,7},{7,6},{8,9},{9,8},{10,11... | collective-permute-start | bytes 3932168 | tf_op jit(solution)/shard_map/ppermute | solution.py:29
  264.6 23.3 %collective-permute-start.11 = (bf16[4,128,1280]{2,1,0:T(8,128)(2,1)S(1)}, bf16[4,128,1280]{2,1,0:T(8,128)(2,1)}, u32[]{:S(2)}, u32[]{:S(2)}) collective-permute-start(bf16[4,128,1280]{2,1,0:T(8,128)(2,1)S(1)} %pad_maximum_fusion.refs_4_), channel_id=1, source_target_pairs={{0,1},{1,0},{2,3},{3,2},{4,5},{5,4},{6,7},{7,6},{8,9},{9,8},{10,11... | collective-permute-start | bytes 3932168 | tf_op jit(solution)/shard_map/ppermute | solution.py:29
  265.1 22.8 %collective-permute-start.14 = (bf16[2,2,128,1280]{3,2,1,0:T(8,128)(2,1)}, bf16[2,2,128,1280]{3,2,1,0:T(8,128)(2,1)}, u32[]{:S(2)}, u32[]{:S(2)}) collective-permute-start(bf16[2,2,128,1280]{3,2,1,0:T(8,128)(2,1)} %collective-permute-done.10.refs_7_), channel_id=1, source_target_pairs={{0,1},{1,0},{2,3},{3,2},{4,5},{5,4},{6,7},{7,6},{8,9},{9,8},{10,11... | collective-permute-start | bytes 3932168 | tf_op jit(solution)/shard_map/ppermute | solution.py:29
  265.3 22.6 %collective-permute-start.12 = (bf16[4,128,1280]{2,1,0:T(8,128)(2,1)}, bf16[4,128,1280]{2,1,0:T(8,128)(2,1)}, u32[]{:S(2)}, u32[]{:S(2)}) collective-permute-start(bf16[4,128,1280]{2,1,0:T(8,128)(2,1)} %collective-permute-done.6.refs_5_), channel_id=1, source_target_pairs={{0,1},{1,0},{2,3},{3,2},{4,5},{5,4},{6,7},{7,6},{8,9},{9,8},{10,11... | collective-permute-start | bytes 3932168 | tf_op jit(solution)/shard_map/ppermute | solution.py:29
  274.6 10.2 %collective-permute-start.3 = (bf16[2,512,128]{2,1,0:T(8,128)(2,1)S(1)}, bf16[2,512,128]{2,1,0:T(8,128)(2,1)S(1)}, u32[]{:S(2)}, u32[]{:S(2)}) collective-permute-start(bf16[2,512,128]{2,1,0:T(8,128)(2,1)S(1)} %pad_maximum_fusion.7.refs_0_), channel_id=1, source_target_pairs={{0,24},{8,16},{16,8},{24,0},{1,25},{9,17},{17,9},{25,1},{2,26},{10... | collective-permute-start | bytes 786440 | tf_op jit(solution)/shard_map/ppermute | solution.py:29
  284.9 3.0 copy-start.14
  284.9 35.2 %collective-permute-start.36 = (bf16[128,1280]{1,0:T(8,128)(2,1)}, bf16[128,1280]{1,0:T(8,128)(2,1)}, u32[]{:S(2)}, u32[]{:S(2)}) collective-permute-start(bf16[128,1280]{1,0:T(8,128)(2,1)} %fusion.2), channel_id=1, source_target_pairs={{0,4},{4,0},{1,5},{5,1},{2,6},{6,2},{3,7},{7,3},{8,12},{12,8},{9,1... | collective-permute-start | bytes 983048 | tf_op jit(solution)/shard_map/ppermute | solution.py:29
  286.4 35.9 %collective-permute-start.33 = (bf16[1,384,1280]{2,1,0:T(8,128)(2,1)}, bf16[1,384,1280]{2,1,0:T(8,128)(2,1)}, u32[]{:S(2)}, u32[]{:S(2)}) collective-permute-start(bf16[1,384,1280]{2,1,0:T(8,128)(2,1)} %add_convert_fusion), channel_id=1, source_target_pairs={{0,2},{1,3},{2,0},{3,1},{4,6},{5,7},{6,4},{7,5},{8,10},{9,11},{10,... | collective-permute-start | bytes 2949128 | tf_op jit(solution)/shard_map/ppermute | solution.py:29
  307.7 3.9 %collective-permute-start.30 = (f32[8,128]{1,0:T(8,128)}, f32[8,128]{1,0:T(8,128)S(1)}, u32[]{:S(2)}, u32[]{:S(2)}) collective-permute-start(f32[8,128]{1,0:T(8,128)} %get-tuple-element.32.refs_0_), channel_id=1, source_target_pairs={{0,4},{4,0},{1,5},{5,1},{2,6},{6,2},{3,7},{7,3},{8,12},{12,8},{9,1... | collective-permute-start | bytes 12296 | tf_op jit(solution)/shard_map/ppermute | solution.py:29
  311.6 0.6 copy-start.18
  322.2 3.2 copy-start.1

commit v3 on v2

--- a/solution.py
+++ b/solution.py
@@ -15,6 +15,7 @@
 ANY = pl.BlockSpec(memory_space=pl.ANY)
 SMEM = pl.BlockSpec(memory_space=pltpu.SMEM)
 F32, BF16 = jnp.float32, jnp.bfloat16
+GRANT = pltpu.CompilerParams(vmem_limit_bytes=32 << 20)
 
 
 def swap(size, bit):
@@ -78,7 +79,8 @@
     return pl.BlockSpec(shape, lambda *_: (0,) * len(shape), pipeline_mode=pl.Buffered(1))
 
 
-def project_kernel(variants, keep, noisy_ref, shift_ref, gain_ref, weight_ref, *refs):
+def project_kernel(variants, keep, held, noisy_ref, shift_ref, gain_ref, weight_ref, *refs):
+    refs = refs[held:]
     out_ref = refs[0]
     hidden_ref = refs[1] if keep else None
     joined, normed = refs[-2:]
@@ -108,37 +110,40 @@
         hidden_ref[...] = normed[0]
 
 
-def project(noisy, shifts, gain, weight, keep):
+def project(noisy, shifts, gain, weight, keep, start, count, into=()):
     length, width = noisy.shape
     head = weight.shape[2]
     variants = shifts.shape[0]
-    tile = min(256, length)
+    tile = min(256, count)
+    first = start // tile
     out_shape = [jax.ShapeDtypeStruct((variants, length, 3 * head), F32)]
-    out_specs = [pl.BlockSpec((variants, tile, 3 * head), lambda i: (0, i, 0))]
+    out_specs = [pl.BlockSpec((variants, tile, 3 * head), lambda i: (0, first + i, 0))]
     if keep:
         out_shape.append(jax.ShapeDtypeStruct((length, width), BF16))
-        out_specs.append(pl.BlockSpec((tile, width), lambda i: (i, 0)))
+        out_specs.append(pl.BlockSpec((tile, width), lambda i: (first + i, 0)))
     return pl.pallas_call(
-        functools.partial(project_kernel, variants, keep),
-        grid=(length // tile,),
+        functools.partial(project_kernel, variants, keep, len(into)),
+        grid=(count // tile,),
         in_specs=[
-            pl.BlockSpec((tile, width), lambda i: (i, 0)),
+            pl.BlockSpec((tile, width), lambda i: (first + i, 0)),
             resident((variants, width)),
             resident((1, width)),
             resident(weight.shape),
-        ],
+        ]
+        + [ANY] * len(into),
         out_specs=out_specs,
         out_shape=out_shape,
+        input_output_aliases={4 + n: n for n in range(len(into))},
         scratch_shapes=[
             pltpu.VMEM((width, 3 * head), BF16),
             pltpu.VMEM((variants, tile, width), BF16),
         ],
         cost_estimate=pl.CostEstimate(
-            flops=2 * variants * length * width * 3 * head,
-            bytes_accessed=2 * length * width * (2 if keep else 1) + 6 * width * head,
+            flops=2 * variants * count * width * 3 * head,
+            bytes_accessed=2 * count * width * (2 if keep else 1) + 6 * width * head,
             transcendentals=0,
         ),
-    )(noisy, shifts, gain, weight)
+    )(noisy, shifts, gain, weight, *into)
 
 
 def rope_rows(raw, gain, cosine, sine):
@@ -303,8 +308,9 @@
     refs = refs[3:]
     if resume:
         before_ref, refs = refs[0], refs[1:]
-    term_ref, part_ref, grad_ref = refs[:3]
-    heads, weights, cotangents, attn_sems, sems = refs[3:]
+    term_ref, part_ref, refs = refs[0], refs[1], refs[2:]
+    shares = refs[:seqs] if resume else ()
+    grad_ref, heads, weights, cotangents, attn_sems, sems = refs[len(shares) :]
     slot = stream(
         attn_plan, plan, seqs, scal, attn_refs, out_refs, heads, weights, attn_sems, sems
     )
@@ -325,6 +331,14 @@
         cotangents[at, :] = cotangent.astype(BF16)
         grad_ref[at, :] += contract(cotangents[at, :], weights[slot, own, :], 1, 1)
     part_ref[0] = contract(heads[:, own], cotangents[...], 0, 0).astype(BF16)
+    if resume:
+
+        @pl.when(pl.program_id(0) == pl.num_programs(0) - 1)
+        def _():
+            for d, share in enumerate(shares):
+                head = share.shape[1]
+                first = pl.multiple_of((scal[0] ^ d) * head, head)
+                share[...] = grad_ref[:, pl.ds(first, head)].astype(BF16)
 
 
 def plan_heads(plan):
@@ -341,6 +355,12 @@
         post_kernel, attn.chunks[0], out.chunks, seqs, n_attn, n_out, len(before)
     )
     grad_spec = pl.BlockSpec((rows, seqs * head), lambda i, s: (0, 0))
+    grad_specs, grad_shapes = [grad_spec], [jax.ShapeDtypeStruct((rows, seqs * head), F32)]
+    scratch = []
+    if before:
+        grad_specs = [pl.BlockSpec((rows, head), lambda i, s: (0, 0))] * seqs
+        grad_shapes = [jax.ShapeDtypeStruct((rows, head), BF16)] * seqs
+        scratch = [pltpu.VMEM((rows, seqs * head), F32)]
 
     def spot(i, s):
         return s[2 + blocks + i // 2] * 2 + i % 2
@@ -361,9 +381,10 @@
             out_specs=[
                 pl.BlockSpec((1, rows, cols), lambda i, s: (i // 2, 0, i % 2)),
                 pl.BlockSpec((1, seqs * head, cols), lambda i, s: (i // 2, 0, i % 2)),
-                grad_spec,
-            ],
-            scratch_shapes=[
+            ]
+            + grad_specs,
+            scratch_shapes=scratch
+            + [
                 pltpu.VMEM((rows, total * head), BF16),
                 pltpu.VMEM((2, total * head, cols), BF16),
                 pltpu.VMEM((rows, cols), BF16),
@@ -374,8 +395,8 @@
         out_shape=[
             jax.ShapeDtypeStruct((chunks, rows, 2 * cols), BF16),
             jax.ShapeDtypeStruct((chunks, seqs * head, 2 * cols), BF16),
-            jax.ShapeDtypeStruct((rows, seqs * head), F32),
-        ],
+        ]
+        + grad_shapes,
         cost_estimate=pl.CostEstimate(
             flops=4 * rows * chunks * cols * head * (total + 2 * seqs),
             bytes_accessed=2 * chunks * cols * (2 * total * head + 8 * rows),
@@ -467,12 +488,15 @@
             bytes_accessed=width * (2 * total * head + 8 * rows),
             transcendentals=0,
         ),
+        compiler_params=GRANT,
     )(scal, noise, *attn.operands, *out.operands, noisy, target, cond, null, near, far)
 
 
 def backward_kernel(
-    q_ref, k_ref, v_ref, go_ref, qkv_ref, gain_ref, cos_ref, sin_ref, out_ref, key_sum, value_sum
+    seqs, per, scal, q_ref, k_ref, v_ref, qkv_ref, gain_ref, cos_ref, sin_ref, *refs
 ):
+    shares = refs[:seqs]
+    out_ref, grad_rows, key_sum, value_sum = refs[seqs:]
     tile, head = q_ref.shape
     scale = head ** (-0.5)
     i = pl.program_id(0)
@@ -490,8 +514,14 @@
         mean = jnp.mean(scaled * raw, axis=-1, keepdims=True)
         return inverse * scaled - raw * inverse * inverse * inverse * mean
 
+    for d, share in enumerate(shares):
+
+        @pl.when(i // per == (scal[0] ^ d))
+        def _():
+            grad_rows[...] = share[...]
+
     probability = softmax_rows(q_ref[...], k_ref[...], scale)
-    grad_prob = contract(go_ref[...], v_ref[...], 1, 1)
+    grad_prob = contract(grad_rows[...], v_ref[...], 1, 1)
     inner = jnp.sum(grad_prob * probability, axis=-1, keepdims=True)
     grad_score = (probability * (grad_prob - inner) * scale).astype(BF16)
     grad_query = unroll(
@@ -503,7 +533,7 @@
     )
     out_ref[:head, at] = grad_query.T.astype(BF16)
     key_sum[...] += contract(grad_score, q_ref[...], 0, 0)
-    value_sum[...] += contract(probability.astype(BF16), go_ref[...], 0, 0)
+    value_sum[...] += contract(probability.astype(BF16), grad_rows[...], 0, 0)
 
     @pl.when(i == pl.num_programs(0) - 1)
     def _():
@@ -518,32 +548,48 @@
         out_ref[2 * head :, :] = value_sum[...].T.astype(BF16)
 
 
-def backward(query, key, value, grad_attn, qkv, gains, cosine, sine):
+def backward(scal, query, key, value, grad_attn, qkv, gains, cosine, sine):
     length, head = query.shape
-    tile = min(256, length)
-    row = pl.BlockSpec((tile, head), lambda i: (i, 0))
+    seqs = len(grad_attn)
+    rows = length // seqs
+    tile = min(256, rows)
+    per = rows // tile
+    row = pl.BlockSpec((tile, head), lambda i, s: (i, 0))
+
+    def share(d):
+        return pl.BlockSpec(
+            (tile, head), lambda i, s: (jnp.clip(i - (s[0] ^ d) * per, 0, per - 1), 0)
+        )
+
     return pl.pallas_call(
-        backward_kernel,
-        grid=(length // tile,),
-        in_specs=[
-            row,
-            resident((length, head)),
-            resident((length, head)),
-            row,
-            resident(qkv.shape),
-            resident(gains.shape),
-            resident(cosine.shape),
-            resident(sine.shape),
-        ],
-        out_specs=pl.BlockSpec((3 * head, length), lambda i: (0, 0)),
+        functools.partial(backward_kernel, seqs, per),
+        grid_spec=pltpu.PrefetchScalarGridSpec(
+            num_scalar_prefetch=1,
+            grid=(length // tile,),
+            in_specs=[
+                row,
+                resident((length, head)),
+                resident((length, head)),
+                resident(qkv.shape),
+                resident(gains.shape),
+                resident(cosine.shape),
+                resident(sine.shape),
+            ]
+            + [share(d) for d in range(seqs)],
+            out_specs=pl.BlockSpec((3 * head, length), lambda i, s: (0, 0)),
+            scratch_shapes=[
+                pltpu.VMEM((tile, head), BF16),
+                pltpu.VMEM((length, head), F32),
+                pltpu.VMEM((length, head), F32),
+            ],
+        ),
         out_shape=jax.ShapeDtypeStruct((3 * head, length), BF16),
-        scratch_shapes=[pltpu.VMEM((length, head), F32), pltpu.VMEM((length, head), F32)],
         cost_estimate=pl.CostEstimate(
             flops=20 * length * length * head,
             bytes_accessed=12 * length * head,
             transcendentals=length * length,
         ),
-    )(query, key, value, grad_attn, qkv, gains, cosine, sine)
+    )(scal, query, key, value, qkv, gains, cosine, sine, *grad_attn)
 
 
 def weight_kernel(scal, grad_ref, hidden_ref, out_ref):
@@ -602,6 +648,7 @@
         cost_estimate=pl.CostEstimate(
             flops=4 * rows * width, bytes_accessed=4 * rows * width, transcendentals=0
         ),
+        compiler_params=GRANT,
     )(*totals, diff)
 
 
@@ -626,6 +673,7 @@
         cost_estimate=pl.CostEstimate(
             flops=3 * features * cols, bytes_accessed=10 * features * cols, transcendentals=0
         ),
+        compiler_params=GRANT,
     )(*terms)
 
 
@@ -704,7 +752,7 @@
     head = critic_out.shape[0]
     seqs, reps = lax.axis_size("seq"), lax.axis_size("rep")
     seq, rep, branch = lax.axis_index("seq"), lax.axis_index("rep"), lax.axis_index("branch")
-    rows, cols = length // seqs, width // reps
+    cols = width // reps
     fraction = (timestep.astype(F32) + 1.0) / 1001.0
     noise = 5.0 * fraction / (1.0 + 4.0 * fraction)
     used_caption = jnp.where(caption_drop[0] == 1, null_caption, caption[0])
@@ -723,30 +771,33 @@
 
     critic_near, critic_far = gather_out(critic_out, rep)
     cosine, sine = rope_tables(window_start[0], length)
-    fake_qkv, hidden = project(latent, cond_shift, critic_gain[None], critic_qkv, True)
+    fake_qkv, hidden = project(latent, cond_shift, critic_gain[None], critic_qkv, True, 0, length)
     later, fake_qkv = lax.optimization_barrier((rep, fake_qkv))
     fake_attn, (fake_q, fake_k, fake_v) = attend(
         scal, seqs, fake_qkv, critic_qk_gain, cosine, sine, True
     )
     fake_plan = gather_heads(fake_attn)
     teacher_near, teacher_far = gather_out(teacher_out, later)
-    (both_qkv,) = project(latent, both_shift, teacher_gain[None], teacher_qkv, False)
+    half = length // 2
+    both_qkv = ()
+    for start in (0, half):
+        both_qkv = project(
+            latent, both_shift, teacher_gain[None], teacher_qkv, False, start, half, into=both_qkv
+        )
+    (both_qkv,) = both_qkv
     guided_attn, _ = attend(scal, seqs, both_qkv, teacher_qk_gain, cosine, sine, False)
     guided_plan = gather_heads(guided_attn)
 
     common = (noise, latent, target, cond_shift, seqs, head)
     near_term, near_part, near_grad = post(fake_plan, critic_near, 0, scal, *common, ())
-    far_term, far_part, grad_all = post(fake_plan, critic_far, kept, scal, *common, (near_grad,))
-
-    def grad_block(d):
-        return lax.dynamic_slice_in_dim(grad_all, (seq ^ d) * head, head, 1).astype(BF16)
-
-    grad_attn = jnp.zeros((length, head), BF16)
-    for d in range(seqs):
-        piece = move(grad_block(d), "seq", d) if d else grad_block(0)
-        grad_attn = lax.dynamic_update_slice(grad_attn, piece, ((seq ^ d) * rows, 0))
-
-    grads = backward(fake_q, fake_k, fake_v, grad_attn, fake_qkv, critic_qk_gain, cosine, sine)
+    far_term, far_part, *grad_heads = post(fake_plan, critic_far, kept, scal, *common, (near_grad,))
+
+    grad_attn = [grad_heads[0]]
+    grad_attn += [move(grad_heads[d], "seq", d) for d in range(1, seqs)]
+
+    grads = backward(
+        scal, fake_q, fake_k, fake_v, grad_attn, fake_qkv, critic_qk_gain, cosine, sine
+    )
     far_weight = weight_grad(grads, hidden, kept, kept, scal, cols)
     near_weight = weight_grad(grads, hidden, 0, kept, scal, cols)
 

time: 327 us -> 334 us (1.021)
  waiting for transfers between devices: 84.3 us -> 92 us
  starting transfers between devices: 67.5 us -> 60 us
  local copies, waits for them, and re-layouts: 6.25 us -> 10.2 us
    ppermute x37, waiting for transfers between devices: 84.3 us -> 92 us  [move(): return lax.ppermute(value, axis, swap(lax.axis_size(axis), bit))]
    ppermute x37, starting transfers between devices: 67.5 us -> 60 us  [move(): return lax.ppermute(value, axis, swap(lax.axis_size(axis), bit))]
    pallas_call x3 -> x4, Pallas kernels: 55.8 us -> 61.4 us  [the longest x3 51.8 us: project(): pl.pallas_call(functools.partial(project_kernel, variants, keep, len(into...]
    unnamed x38 -> x42, local copies, waits for them, and re-layouts: 3.46 us -> 8.6 us
    pallas_call x1, Pallas kernels: 7.86 us -> 4.49 us  [scale(): pl.pallas_call(functools.partial(scale_kernel, entries), grid=(rows // ti...]
  transfers between devices with their start and end apart: 37 -> 37, of which waited for: 12 -> 10; matrix products, arithmetic and copies ran while one was open for 7% -> 8% of each run, Pallas kernels for 43% -> 42%
where the time goes in v3:
time: 334 us; the launch traced here: 332 us
  Pallas kernels  144 us (43%)
  waiting for transfers between devices  92 us (28%)
  starting transfers between devices  60 us (18%)
  other arithmetic  23.7 us (7%)
  local copies, waits for them, and re-layouts  10.2 us (3%)
    ppermute x37, waiting for transfers between devices, move(): return lax.ppermute(value, axis, swap(lax.axis_size(axis), bit))  92 us
    ppermute x37, starting transfers between devices, move(): return lax.ppermute(value, axis, swap(lax.axis_size(axis), bit))  60 us
    pallas_call x3, Pallas kernels, project(): pl.pallas_call(functools.partial(project_kernel, variants, keep, len(into...  51.8 us
    pallas_call x2, Pallas kernels, post(): pl.pallas_call(kernel, grid_spec=pltpu.PrefetchScalarGridSpec(num_scalar_...  24.6 us
    pallas_call x1, Pallas kernels, guide(): pl.pallas_call(functools.partial(guide_kernel, attn.chunks[0], out.chunks...  18.1 us
    pallas_call x2, Pallas kernels, attend(): pl.pallas_call(functools.partial(attend_kernel, variants, seqs, per), gri...  18 us
    pallas_call x2, Pallas kernels, weight_grad(): pl.pallas_call(weight_kernel, grid_spec=pltpu.PrefetchScalarGridSpec(num_...  14 us
    pallas_call x1, Pallas kernels, backward(): pl.pallas_call(functools.partial(backward_kernel, seqs, per), grid_spec=p...  9.64 us
  transfers between devices with their start and end apart: 37, of which 10 were waited for; matrix products, arithmetic and copies ran while one was open for 8% of the time, Pallas kernels for 42%

profile of v3, /device:TPU:0, one launch (start us, length us, event | category | flops | bytes accessed | tf_op | source)
XLA Modules:
  0.0 332.4 jit_solution(10089432814268985593)
XLA Ops:
  0.7 1.3 copy-done
  2.0 4.1 %collective-permute-start.22 = (bf16[1,128,1280]{2,1,0:T(8,128)(2,1)S(1)}, bf16[1,128,1280]{2,1,0:T(8,128)(2,1)S(1)}, u32[]{:S(2)}, u32[]{:S(2)}) collective-permute-start(bf16[1,128,1280]{2,1,0:T(8,128)(2,1)S(1)} %dynamic-slice_bitcast_fusion), channel_id=1, source_target_pairs={{0,16},{8,24},{16,0},{24,8},{1,17},{9,25},{17,1},{25,9},{2,18},{10... | collective-permute-start | bytes 983048 | tf_op jit(solution)/shard_map/ppermute | solution.py:30
  6.1 1.3 collective-permute-start.23
  9.1 0.8 reduce
  9.8 1.4 select_convert_fusion
  11.2 17.5 %collective-permute-done.22 = bf16[1,128,1280]{2,1,0:T(8,128)(2,1)S(1)} collective-permute-done((bf16[1,128,1280]{2,1,0:T(8,128)(2,1)S(1)}, bf16[1,128,1280]{2,1,0:T(8,128)(2,1)S(1)}, u32[]{:S(2)}, u32[]{:S(2)}) %collective-permute-start.22) | collective-permute-done | bytes 327712 | tf_op jit(solution)/shard_map/ppermute | solution.py:30
  28.8 1.9 collective-permute-start.24
  30.7 0.9 pad_maximum_fusion.5
  31.6 1.5 collective-permute-start.20
  33.1 18.6 %shard_map.169 = (f32[1,1024,384]{2,1,0:T(8,128)}, bf16[1024,5120]{1,0:T(8,128)(2,1)}) custom-call(bf16[1024,5120]{1,0:T(8,128)(2,1)} %bitcast.40, f32[1,5120]{1,0:T(1,128)} %bitcast.33, f32[1,5120]{1,0:T(1,128)} %bitcast.56, bf16[3,5120,128]{2,1,0:T(8,128)(2,1)} %weight_ref.5), custom_call_target="tpu_custom_call" | custom-call | flops 4026531840 | bytes 24903680 | tf_op jit(solution)/shard_map/pallas_call | solution.py:124
  52.5 1.2 pad_maximum_fusion.2.refs_4_
  55.3 2.9 fusion
  58.2 7.6 %shard_map.170 = (bf16[512,128]{1,0:T(8,128)(2,1)}, bf16[512,128]{1,0:T(8,128)(2,1)}, bf16[1024,128]{1,0:T(8,128)(2,1)}, bf16[1024,128]{1,0:T(8,128)(2,1)}, bf16[1024,128]{1,0:T(8,128)(2,1)}) custom-call(s32[6]{0:T(128)} %stack.45.scal, f32[1,1024,384]{2,1,0:T(8,128)} %get-tuple-element.27.qkv_ref, f32[2,128]{1,0:T(2,128)} %gain_ref.5, ...), custom_call_target="tpu_custom_call" | custom-call | flops 2147483648 | bytes 1572864 | tf_op jit(solution)/shard_map/pallas_call | solution.py:213
  65.8 1.7 collective-permute-start.15
  67.5 1.0 dynamic-slice_bitcast_fusion.1
  68.5 8.6 %collective-permute-start.7 = (bf16[1,128,1280]{2,1,0:T(8,128)(2,1)S(1)}, bf16[1,128,1280]{2,1,0:T(8,128)(2,1)S(1)}, u32[]{:S(2)}, u32[]{:S(2)}) collective-permute-start(bf16[1,128,1280]{2,1,0:T(8,128)(2,1)S(1)} %dynamic-slice_bitcast_fusion.1), channel_id=1, source_target_pairs={{0,16},{8,24},{16,0},{24,8},{1,17},{9,25},{17,1},{25,9},{2,18},{10... | collective-permute-start | bytes 983048 | tf_op jit(solution)/shard_map/ppermute | solution.py:30
  77.5 5.3 %collective-permute-done.15 = bf16[512,128]{1,0:T(8,128)(2,1)S(1)} collective-permute-done((bf16[512,128]{1,0:T(8,128)(2,1)}, bf16[512,128]{1,0:T(8,128)(2,1)S(1)}, u32[]{:S(2)}, u32[]{:S(2)}) %collective-permute-start.15) | collective-permute-done | bytes 131104 | tf_op jit(solution)/shard_map/ppermute | solution.py:30
  82.8 8.7 %collective-permute-start.4 = (bf16[1,128,1280]{2,1,0:T(8,128)(2,1)S(1)}, bf16[1,128,1280]{2,1,0:T(8,128)(2,1)}, u32[]{:S(2)}, u32[]{:S(2)}) collective-permute-start(bf16[1,128,1280]{2,1,0:T(8,128)(2,1)S(1)} %dynamic-slice_bitcast_fusion.1), channel_id=1, source_target_pairs={{0,8},{8,0},{16,24},{24,16},{1,9},{9,1},{17,25},{25,17},{2,10},{10... | collective-permute-start | bytes 983048 | tf_op jit(solution)/shard_map/ppermute | solution.py:30
  91.5 0.7 pad_maximum_fusion.9.shift_ref
  92.1 5.7 %collective-permute-done.7 = bf16[1,128,1280]{2,1,0:T(8,128)(2,1)S(1)} collective-permute-done((bf16[1,128,1280]{2,1,0:T(8,128)(2,1)S(1)}, bf16[1,128,1280]{2,1,0:T(8,128)(2,1)S(1)}, u32[]{:S(2)}, u32[]{:S(2)}) %collective-permute-start.7) | collective-permute-done | bytes 327712 | tf_op jit(solution)/shard_map/ppermute | solution.py:30
  97.9 1.1 pad_maximum_fusion.8.refs_0_
  99.0 6.2 %collective-permute-start.16 = (bf16[2,512,128]{2,1,0:T(8,128)(2,1)S(1)}, bf16[2,512,128]{2,1,0:T(8,128)(2,1)}, u32[]{:S(2)}, u32[]{:S(2)}) collective-permute-start(bf16[2,512,128]{2,1,0:T(8,128)(2,1)S(1)} %pad_maximum_fusion.8.refs_0_), channel_id=1, source_target_pairs={{0,8},{8,0},{16,24},{24,16},{1,9},{9,1},{17,25},{25,17},{2,10},{10... | collective-permute-start | bytes 786440 | tf_op jit(solution)/shard_map/ppermute | solution.py:30
  105.8 16.5 %shard_map.166.refs_0_ = f32[2,1024,384]{2,1,0:T(8,128)} custom-call(bf16[1024,5120]{1,0:T(8,128)(2,1)} %bitcast.41, f32[2,5120]{1,0:T(2,128)} %pad_maximum_fusion.9.shift_ref, f32[1,5120]{1,0:T(1,128)} %bitcast.54, bf16[3,5120,128]{2,1,0:T(8,128)(2,1)} %weight_ref.4), custom_call_target="tpu_custom_call" | custom-call | flops 4026531840 | bytes 9175040 | tf_op jit(solution)/shard_map/pallas_call | solution.py:124
  123.1 16.7 %shard_map.167.qkv_ref = f32[2,1024,384]{2,1,0:T(8,128)} custom-call(bf16[1024,5120]{1,0:T(8,128)(2,1)} %bitcast.42, f32[2,5120]{1,0:T(2,128)} %pad_maximum_fusion.9.shift_ref, f32[1,5120]{1,0:T(1,128)} %bitcast.55, bf16[3,5120,128]{2,1,0:T(8,128)(2,1)} %weight_ref.4, f32[2,1024,384]{2,1,0:T(8,128)} %shard_map.166.refs_0_), custom_call_target="tpu_custom_call", output_to_operand_aliasing={{}: (4, {})} | custom-call | flops 4026531840 | bytes 9175040 | tf_op jit(solution)/shard_map/pallas_call | solution.py:124
  139.8 2.3 collective-permute-start.18
  142.1 1.9 pad_maximum_fusion.4
  143.9 0.9 maximum_bitcast_fusion
  144.8 5.5 %collective-permute-done.18.refs_3_ = bf16[2,512,128]{2,1,0:T(8,128)(2,1)S(1)} collective-permute-done((bf16[2,512,128]{2,1,0:T(8,128)(2,1)S(1)}, bf16[2,512,128]{2,1,0:T(8,128)(2,1)S(1)}, u32[]{:S(2)}, u32[]{:S(2)}) %collective-permute-start.18) | collective-permute-done | bytes 262176 | tf_op jit(solution)/shard_map/ppermute | solution.py:30
  150.4 1.5 collective-permute-start.9
  151.9 0.7 collective-permute-start.5
  152.6 12.0 %shard_map.171 = (bf16[2,512,1280]{2,1,0:T(8,128)(2,1)}, bf16[2,256,1280]{2,1,0:T(8,128)(2,1)}, f32[512,256]{1,0:T(8,128)}) custom-call(s32[6]{0:T(128)} %stack.45.scal, f32[1]{0:T(128)S(6)} %div.38.noise_ref, bf16[2,512,128]{2,1,0:T(8,128)(2,1)} %copy-done.12, bf16[2,512,128]{2,1,0:T(8,128)(2,1)} %collective-permute-done.16.refs_1_, ...), custom_call_target="tpu_custom_call" | custom-call | flops 4026531840 | bytes 15728640 | tf_op jit(solution)/shard_map/pallas_call | solution.py:368
  164.6 12.6 %shard_map.172 = (bf16[2,512,1280]{2,1,0:T(8,128)(2,1)}, bf16[2,256,1280]{2,1,0:T(8,128)(2,1)}, bf16[512,128]{1,0:T(8,128)(2,1)}, bf16[512,128]{1,0:T(8,128)(2,1)}) custom-call(s32[6]{0:T(128)} %stack.45.scal, f32[1]{0:T(128)S(6)} %div.38.noise_ref, bf16[2,512,128]{2,1,0:T(8,128)(2,1)} %copy-done.12, bf16[2,512,128]{2,1,0:T(8,128)(2,1)} %collective-permute-done.16.refs_1_, ...), custom_call_target="tpu_custom_call" | custom-call | flops 4026531840 | bytes 15728640 | tf_op jit(solution)/shard_map/pallas_call | solution.py:368
  177.3 1.4 pad_maximum_fusion.1.refs_6_
  178.7 1.4 collective-permute-start.10
  180.2 0.7 collective-permute-start.31
  180.8 1.3 pad_maximum_fusion.refs_4_
  182.1 0.7 collective-permute-start.6
  182.9 29.9 %collective-permute-done.31.refs_1_ = bf16[512,128]{1,0:T(8,128)(2,1)S(1)} collective-permute-done((bf16[512,128]{1,0:T(8,128)(2,1)S(1)}, bf16[512,128]{1,0:T(8,128)(2,1)S(1)}, u32[]{:S(2)}, u32[]{:S(2)}) %collective-permute-start.31) | collective-permute-done | bytes 131104 | tf_op jit(solution)/shard_map/ppermute | solution.py:30
  213.4 9.6 %shard_map.175.grad_ref = bf16[384,1024]{1,0:T(8,128)(2,1)} custom-call(s32[6]{0:T(128)} %stack.45.scal, bf16[1024,128]{1,0:T(8,128)(2,1)} %get-tuple-element.35.q_ref, bf16[1024,128]{1,0:T(8,128)(2,1)} %get-tuple-element.36.k_ref, bf16[1024,128]{1,0:T(8,128)(2,1)} %get-tuple-element.37.v_ref, f32[1,1024,384]{2,1,0:T(8,128)} %get-tuple-element.27.qkv_ref, ...), custom_call_target="tpu_custom_call" | custom-call | flops 2684354560 | bytes 1572864 | tf_op jit(solution)/shard_map/pallas_call | solution.py:564
  223.1 7.0 %shard_map.177 = bf16[2,384,1280]{2,1,0:T(8,128)(2,1)} custom-call(s32[6]{0:T(128)} %stack.45.scal, bf16[384,1024]{1,0:T(8,128)(2,1)} %shard_map.175.grad_ref, bf16[1024,5120]{1,0:T(8,128)(2,1)} %get-tuple-element.40.hidden_ref), custom_call_target="tpu_custom_call" | custom-call | flops 2013265920 | bytes 7208960 | tf_op jit(solution)/shard_map/pallas_call | solution.py:603
  230.1 10.4 %shard_map.168 = (bf16[512,128]{1,0:T(8,128)(2,1)}, bf16[512,128]{1,0:T(8,128)(2,1)}) custom-call(s32[6]{0:T(128)} %stack.45.scal, f32[2,1024,384]{2,1,0:T(8,128)} %shard_map.167.qkv_ref, f32[2,128]{1,0:T(2,128)} %gain_ref.3, f32[1024,128]{1,0:T(8,128)} %get-tuple-element.44.cos_ref, f32[1024,128]{1,0:T(8,128)} %get-tuple-element.43.sin_ref), custom_call_target="tpu_custom_call" | custom-call | flops 4294967296 | bytes 3145728 | tf_op jit(solution)/shard_map/pallas_call | solution.py:213
  240.6 1.3 collective-permute-start
  241.9 1.4 add_convert_fusion.1
  243.3 0.8 collective-permute-start.35
  244.1 2.6 collective-permute-done
  246.8 5.2 %collective-permute-start.1 = (bf16[2,512,128]{2,1,0:T(8,128)(2,1)S(1)}, bf16[2,512,128]{2,1,0:T(8,128)(2,1)S(1)}, u32[]{:S(2)}, u32[]{:S(2)}) collective-permute-start(bf16[2,512,128]{2,1,0:T(8,128)(2,1)S(1)} %pad_maximum_fusion.7.refs_0_), channel_id=1, source_target_pairs={{0,8},{8,0},{16,24},{24,16},{1,9},{9,1},{17,25},{25,17},{2,10},{10... | collective-permute-start | bytes 786440 | tf_op jit(solution)/shard_map/ppermute | solution.py:30
  251.9 6.2 %collective-permute-done.1.refs_1_ = bf16[2,512,128]{2,1,0:T(8,128)(2,1)S(1)} collective-permute-done((bf16[2,512,128]{2,1,0:T(8,128)(2,1)S(1)}, bf16[2,512,128]{2,1,0:T(8,128)(2,1)S(1)}, u32[]{:S(2)}, u32[]{:S(2)}) %collective-permute-start.1) | collective-permute-done | bytes 262176 | tf_op jit(solution)/shard_map/ppermute | solution.py:30
  258.1 2.8 collective-permute-start.2
  260.9 11.1 %collective-permute-done.2.refs_2_ = bf16[2,512,128]{2,1,0:T(8,128)(2,1)S(1)} collective-permute-done((bf16[2,512,128]{2,1,0:T(8,128)(2,1)S(1)}, bf16[2,512,128]{2,1,0:T(8,128)(2,1)S(1)}, u32[]{:S(2)}, u32[]{:S(2)}) %collective-permute-start.2) | collective-permute-done | bytes 262176 | tf_op jit(solution)/shard_map/ppermute | solution.py:30
  273.1 7.0 %shard_map.176.refs_0_ = bf16[2,384,1280]{2,1,0:T(8,128)(2,1)} custom-call(s32[6]{0:T(128)} %stack.45.scal, bf16[384,1024]{1,0:T(8,128)(2,1)} %shard_map.175.grad_ref, bf16[1024,5120]{1,0:T(8,128)(2,1)} %get-tuple-element.40.hidden_ref), custom_call_target="tpu_custom_call" | custom-call | flops 2013265920 | bytes 7208960 | tf_op jit(solution)/shard_map/pallas_call | solution.py:603
  280.1 2.0 fusion.2
  282.1 2.5 collective-permute-start.3
  284.6 2.7 add_convert_fusion
  287.3 5.0 %collective-permute-done.3.refs_3_ = bf16[2,512,128]{2,1,0:T(8,128)(2,1)S(1)} collective-permute-done((bf16[2,512,128]{2,1,0:T(8,128)(2,1)S(1)}, bf16[2,512,128]{2,1,0:T(8,128)(2,1)S(1)}, u32[]{:S(2)}, u32[]{:S(2)}) %collective-permute-start.3) | collective-permute-done | bytes 262176 | tf_op jit(solution)/shard_map/ppermute | solution.py:30
  292.3 1.2 collective-permute-start.36
  293.6 0.7 collective-permute-start.33
  294.3 1.7 copy-done.6
  296.0 18.1 %shard_map.173 = (bf16[512,5120]{1,0:T(8,128)(2,1)S(1)}, f32[8,128]{1,0:T(8,128)S(1)}) custom-call(s32[6]{0:T(128)S(1)} %copy-done.9, f32[1]{0:T(128)S(6)} %div.38.noise_ref, bf16[2,512,128]{2,1,0:T(8,128)(2,1)S(1)} %pad_maximum_fusion.7.refs_0_, bf16[2,512,128]{2,1,0:T(8,128)(2,1)S(1)} %collective-permute-done.1.refs_1_, ...), custom_call_target="tpu_custom_call" | custom-call | flops 5368709120 | bytes 31457280 | tf_op jit(solution)/shard_map/pallas_call | solution.py:458
  314.1 2.3 copy-done.3
  317.0 3.0 collective-permute-done.30.refs_1_
  320.1 2.5 copy-done.4
  322.5 4.5 %shard_map.174 = bf16[512,5120]{1,0:T(8,128)(2,1)} custom-call(f32[8,128]{1,0:T(8,128)S(1)} %get-tuple-element.33.refs_0_, f32[8,128]{1,0:T(8,128)S(1)} %collective-permute-done.30.refs_1_, bf16[512,5120]{1,0:T(8,128)(2,1)S(1)} %copy-done.4), custom_call_target="tpu_custom_call" | custom-call | flops 10485760 | bytes 10485760 | tf_op jit(solution)/shard_map/pallas_call | solution.py:642
  327.0 2.4 bitcast_add_fusion
  329.5 3.0 shard_map.178
  (91 shorter events, 6.3 us)
Async XLA Ops:
  0.6 1.3 copy-start
  2.0 26.8 %collective-permute-start.22 = (bf16[1,128,1280]{2,1,0:T(8,128)(2,1)S(1)}, bf16[1,128,1280]{2,1,0:T(8,128)(2,1)S(1)}, u32[]{:S(2)}, u32[]{:S(2)}) collective-permute-start(bf16[1,128,1280]{2,1,0:T(8,128)(2,1)S(1)} %dynamic-slice_bitcast_fusion), channel_id=1, source_target_pairs={{0,16},{8,24},{16,0},{24,8},{1,17},{9,25},{17,1},{25,9},{2,18},{10... | collective-permute-start | bytes 983048 | tf_op jit(solution)/shard_map/ppermute | solution.py:30
  6.1 22.7 %collective-permute-start.23 = (bf16[1,128,1280]{2,1,0:T(8,128)(2,1)S(1)}, bf16[1,128,1280]{2,1,0:T(8,128)(2,1)S(1)}, u32[]{:S(2)}, u32[]{:S(2)}) collective-permute-start(bf16[1,128,1280]{2,1,0:T(8,128)(2,1)S(1)} %dynamic-slice_bitcast_fusion), channel_id=1, source_target_pairs={{0,24},{8,16},{16,8},{24,0},{1,25},{9,17},{17,9},{25,1},{2,26},{10... | collective-permute-start | bytes 983048 | tf_op jit(solution)/shard_map/ppermute | solution.py:30
  7.5 23.3 %collective-permute-start.19 = (bf16[1,128,1280]{2,1,0:T(8,128)(2,1)S(1)}, bf16[1,128,1280]{2,1,0:T(8,128)(2,1)S(1)}, u32[]{:S(2)}, u32[]{:S(2)}) collective-permute-start(bf16[1,128,1280]{2,1,0:T(8,128)(2,1)S(1)} %dynamic-slice_bitcast_fusion), channel_id=1, source_target_pairs={{0,8},{8,0},{16,24},{24,16},{1,9},{9,1},{17,25},{25,17},{2,10},{10... | collective-permute-start | bytes 983048 | tf_op jit(solution)/shard_map/ppermute | solution.py:30
  28.8 22.9 %collective-permute-start.24 = (bf16[1,2,128,1280]{3,2,1,0:T(8,128)(2,1)S(1)}, bf16[1,2,128,1280]{3,2,1,0:T(8,128)(2,1)S(1)}, u32[]{:S(2)}, u32[]{:S(2)}) collective-permute-start(bf16[1,2,128,1280]{3,2,1,0:T(8,128)(2,1)S(1)} %maximum_bitcast_fusion.1), channel_id=1, source_target_pairs={{0,2},{1,3},{2,0},{3,1},{4,6},{5,7},{6,4},{7,5},{8,10},{9,11},{10,... | collective-permute-start | bytes 1966088 | tf_op jit(solution)/shard_map/ppermute | solution.py:30
  31.6 20.9 %collective-permute-start.20 = (bf16[2,128,1280]{2,1,0:T(8,128)(2,1)}, bf16[2,128,1280]{2,1,0:T(8,128)(2,1)}, u32[]{:S(2)}, u32[]{:S(2)}) collective-permute-start(bf16[2,128,1280]{2,1,0:T(8,128)(2,1)} %pad_maximum_fusion.5), channel_id=1, source_target_pairs={{0,4},{4,0},{1,5},{5,1},{2,6},{6,2},{3,7},{7,3},{8,12},{12,8},{9,1... | collective-permute-start | bytes 1966088 | tf_op jit(solution)/shard_map/ppermute | solution.py:30
  51.9 46.0 %copy-start.10 = (bf16[2,2,128,1280]{3,2,1,0:T(8,128)(2,1)}, bf16[2,2,128,1280]{3,2,1,0:T(8,128)(2,1)S(1)}, u32[]{:S(2)}) copy-start(bf16[2,2,128,1280]{3,2,1,0:T(8,128)(2,1)S(1)} %pad_maximum_fusion.3.refs_6_) | copy-start | bytes 3932164
  51.9 53.3 %collective-permute-start.25 = (bf16[2,2,128,1280]{3,2,1,0:T(8,128)(2,1)S(1)}, bf16[2,2,128,1280]{3,2,1,0:T(8,128)(2,1)}, u32[]{:S(2)}, u32[]{:S(2)}) collective-permute-start(bf16[2,2,128,1280]{3,2,1,0:T(8,128)(2,1)S(1)} %pad_maximum_fusion.3.refs_6_), channel_id=1, source_target_pairs={{0,4},{4,0},{1,5},{5,1},{2,6},{6,2},{3,7},{7,3},{8,12},{12,8},{9,1... | collective-permute-start | bytes 3932168 | tf_op jit(solution)/shard_map/ppermute | solution.py:30
  53.7 51.5 %copy-start.11 = (bf16[4,128,1280]{2,1,0:T(8,128)(2,1)}, bf16[4,128,1280]{2,1,0:T(8,128)(2,1)S(1)}, u32[]{:S(2)}) copy-start(bf16[4,128,1280]{2,1,0:T(8,128)(2,1)S(1)} %pad_maximum_fusion.2.refs_4_) | copy-start | bytes 3932164
  53.7 52.0 %collective-permute-start.21 = (bf16[4,128,1280]{2,1,0:T(8,128)(2,1)S(1)}, bf16[4,128,1280]{2,1,0:T(8,128)(2,1)}, u32[]{:S(2)}, u32[]{:S(2)}) collective-permute-start(bf16[4,128,1280]{2,1,0:T(8,128)(2,1)S(1)} %pad_maximum_fusion.2.refs_4_), channel_id=1, source_target_pairs={{0,2},{1,3},{2,0},{3,1},{4,6},{5,7},{6,4},{7,5},{8,10},{9,11},{10,... | collective-permute-start | bytes 3932168 | tf_op jit(solution)/shard_map/ppermute | solution.py:30
  58.2 33.3 %copy-start.7 = (f32[5120]{0:T(1024)S(1)}, f32[5120]{0:T(1024)}, u32[]{:S(2)}) copy-start(f32[5120]{0:T(1024)} %get-tuple-element.45) | copy-start | bytes 61444
  65.8 17.0 %collective-permute-start.15 = (bf16[512,128]{1,0:T(8,128)(2,1)}, bf16[512,128]{1,0:T(8,128)(2,1)S(1)}, u32[]{:S(2)}, u32[]{:S(2)}) collective-permute-start(bf16[512,128]{1,0:T(8,128)(2,1)} %get-tuple-element.29), channel_id=1, source_target_pairs={{0,4},{4,0},{1,5},{5,1},{2,6},{6,2},{3,7},{7,3},{8,12},{12,8},{9,1... | collective-permute-start | bytes 393224 | tf_op jit(solution)/shard_map/ppermute | solution.py:30
  68.5 29.4 %collective-permute-start.7 = (bf16[1,128,1280]{2,1,0:T(8,128)(2,1)S(1)}, bf16[1,128,1280]{2,1,0:T(8,128)(2,1)S(1)}, u32[]{:S(2)}, u32[]{:S(2)}) collective-permute-start(bf16[1,128,1280]{2,1,0:T(8,128)(2,1)S(1)} %dynamic-slice_bitcast_fusion.1), channel_id=1, source_target_pairs={{0,16},{8,24},{16,0},{24,8},{1,17},{9,25},{17,1},{25,9},{2,18},{10... | collective-permute-start | bytes 983048 | tf_op jit(solution)/shard_map/ppermute | solution.py:30
  77.0 21.9 %collective-permute-start.8 = (bf16[1,128,1280]{2,1,0:T(8,128)(2,1)S(1)}, bf16[1,128,1280]{2,1,0:T(8,128)(2,1)S(1)}, u32[]{:S(2)}, u32[]{:S(2)}) collective-permute-start(bf16[1,128,1280]{2,1,0:T(8,128)(2,1)S(1)} %dynamic-slice_bitcast_fusion.1), channel_id=1, source_target_pairs={{0,24},{8,16},{16,8},{24,0},{1,25},{9,17},{17,9},{25,1},{2,26},{10... | collective-permute-start | bytes 983048 | tf_op jit(solution)/shard_map/ppermute | solution.py:30
  82.8 22.4 %collective-permute-start.4 = (bf16[1,128,1280]{2,1,0:T(8,128)(2,1)S(1)}, bf16[1,128,1280]{2,1,0:T(8,128)(2,1)}, u32[]{:S(2)}, u32[]{:S(2)}) collective-permute-start(bf16[1,128,1280]{2,1,0:T(8,128)(2,1)S(1)} %dynamic-slice_bitcast_fusion.1), channel_id=1, source_target_pairs={{0,8},{8,0},{16,24},{24,16},{1,9},{9,1},{17,25},{25,17},{2,10},{10... | collective-permute-start | bytes 983048 | tf_op jit(solution)/shard_map/ppermute | solution.py:30
  97.9 7.9 %copy-start.14 = (bf16[1,128,1280]{2,1,0:T(8,128)(2,1)}, bf16[1,128,1280]{2,1,0:T(8,128)(2,1)S(1)}, u32[]{:S(2)}) copy-start(bf16[1,128,1280]{2,1,0:T(8,128)(2,1)S(1)} %collective-permute-done.7) | copy-start | bytes 983044
  97.9 54.0 %collective-permute-start.28 = (bf16[2,2,128,1280]{3,2,1,0:T(8,128)(2,1)S(1)}, bf16[2,2,128,1280]{3,2,1,0:T(8,128)(2,1)}, u32[]{:S(2)}, u32[]{:S(2)}) collective-permute-start(bf16[2,2,128,1280]{3,2,1,0:T(8,128)(2,1)S(1)} %pad_maximum_fusion.3.refs_6_), channel_id=1, source_target_pairs={{0,1},{1,0},{2,3},{3,2},{4,5},{5,4},{6,7},{7,6},{8,9},{9,8},{10,11... | collective-permute-start | bytes 3932168 | tf_op jit(solution)/shard_map/ppermute | solution.py:30
  98.9 40.8 %copy-start.12 = (bf16[2,512,128]{2,1,0:T(8,128)(2,1)}, bf16[2,512,128]{2,1,0:T(8,128)(2,1)S(1)}, u32[]{:S(2)}) copy-start(bf16[2,512,128]{2,1,0:T(8,128)(2,1)S(1)} %pad_maximum_fusion.8.refs_0_) | copy-start | bytes 786436
  99.0 6.9 %copy-start.16 = (bf16[1,128,1280]{2,1,0:T(8,128)(2,1)}, bf16[1,128,1280]{2,1,0:T(8,128)(2,1)S(1)}, u32[]{:S(2)}) copy-start(bf16[1,128,1280]{2,1,0:T(8,128)(2,1)S(1)} %collective-permute-done.8) | copy-start | bytes 983044
  99.0 24.0 %collective-permute-start.16 = (bf16[2,512,128]{2,1,0:T(8,128)(2,1)S(1)}, bf16[2,512,128]{2,1,0:T(8,128)(2,1)}, u32[]{:S(2)}, u32[]{:S(2)}) collective-permute-start(bf16[2,512,128]{2,1,0:T(8,128)(2,1)S(1)} %pad_maximum_fusion.8.refs_0_), channel_id=1, source_target_pairs={{0,8},{8,0},{16,24},{24,16},{1,9},{9,1},{17,25},{25,17},{2,10},{10... | collective-permute-start | bytes 786440 | tf_op jit(solution)/shard_map/ppermute | solution.py:30
  105.2 59.3 %collective-permute-start.26 = (bf16[4,128,1280]{2,1,0:T(8,128)(2,1)S(1)}, bf16[4,128,1280]{2,1,0:T(8,128)(2,1)}, u32[]{:S(2)}, u32[]{:S(2)}) collective-permute-start(bf16[4,128,1280]{2,1,0:T(8,128)(2,1)S(1)} %pad_maximum_fusion.2.refs_4_), channel_id=1, source_target_pairs={{0,1},{1,0},{2,3},{3,2},{4,5},{5,4},{6,7},{7,6},{8,9},{9,8},{10,11... | collective-permute-start | bytes 3932168 | tf_op jit(solution)/shard_map/ppermute | solution.py:30
  105.2 59.3 %collective-permute-start.29 = (bf16[2,2,128,1280]{3,2,1,0:T(8,128)(2,1)}, bf16[2,2,128,1280]{3,2,1,0:T(8,128)(2,1)}, u32[]{:S(2)}, u32[]{:S(2)}) collective-permute-start(bf16[2,2,128,1280]{3,2,1,0:T(8,128)(2,1)} %collective-permute-done.25.refs_7_), channel_id=1, source_target_pairs={{0,1},{1,0},{2,3},{3,2},{4,5},{5,4},{6,7},{7,6},{8,9},{9,8},{10,11... | collective-permute-start | bytes 3932168 | tf_op jit(solution)/shard_map/ppermute | solution.py:30
  105.7 58.8 %collective-permute-start.27 = (bf16[4,128,1280]{2,1,0:T(8,128)(2,1)}, bf16[4,128,1280]{2,1,0:T(8,128)(2,1)}, u32[]{:S(2)}, u32[]{:S(2)}) collective-permute-start(bf16[4,128,1280]{2,1,0:T(8,128)(2,1)} %collective-permute-done.21.refs_5_), channel_id=1, source_target_pairs={{0,1},{1,0},{2,3},{3,2},{4,5},{5,4},{6,7},{7,6},{8,9},{9,8},{10,11... | collective-permute-start | bytes 3932168 | tf_op jit(solution)/shard_map/ppermute | solution.py:30
  123.0 16.7 %collective-permute-start.17 = (bf16[2,512,128]{2,1,0:T(8,128)(2,1)S(1)}, bf16[2,512,128]{2,1,0:T(8,128)(2,1)}, u32[]{:S(2)}, u32[]{:S(2)}) collective-permute-start(bf16[2,512,128]{2,1,0:T(8,128)(2,1)S(1)} %pad_maximum_fusion.8.refs_0_), channel_id=1, source_target_pairs={{0,16},{8,24},{16,0},{24,8},{1,17},{9,25},{17,1},{25,9},{2,18},{10... | collective-permute-start | bytes 786440 | tf_op jit(solution)/shard_map/ppermute | solution.py:30
  139.7 4.2 %copy-start.15 = (bf16[1,128,1280]{2,1,0:T(8,128)(2,1)S(1)}, bf16[1,128,1280]{2,1,0:T(8,128)(2,1)}, u32[]{:S(2)}) copy-start(bf16[1,128,1280]{2,1,0:T(8,128)(2,1)} %copy-done.14) | copy-start | bytes 983044
  139.7 4.2 %copy-start.17 = (bf16[1,128,1280]{2,1,0:T(8,128)(2,1)S(1)}, bf16[1,128,1280]{2,1,0:T(8,128)(2,1)}, u32[]{:S(2)}) copy-start(bf16[1,128,1280]{2,1,0:T(8,128)(2,1)} %copy-done.16) | copy-start | bytes 983044
  139.8 10.6 %collective-permute-start.18 = (bf16[2,512,128]{2,1,0:T(8,128)(2,1)S(1)}, bf16[2,512,128]{2,1,0:T(8,128)(2,1)S(1)}, u32[]{:S(2)}, u32[]{:S(2)}) collective-permute-start(bf16[2,512,128]{2,1,0:T(8,128)(2,1)S(1)} %pad_maximum_fusion.8.refs_0_), channel_id=1, source_target_pairs={{0,24},{8,16},{16,8},{24,0},{1,25},{9,17},{17,9},{25,1},{2,26},{10... | collective-permute-start | bytes 786440 | tf_op jit(solution)/shard_map/ppermute | solution.py:30
  150.4 1.5 copy-start.13
  150.4 27.0 %collective-permute-start.9 = (bf16[1,2,128,1280]{3,2,1,0:T(8,128)(2,1)}, bf16[1,2,128,1280]{3,2,1,0:T(8,128)(2,1)}, u32[]{:S(2)}, u32[]{:S(2)}) collective-permute-start(bf16[1,2,128,1280]{3,2,1,0:T(8,128)(2,1)} %maximum_bitcast_fusion), channel_id=1, source_target_pairs={{0,2},{1,3},{2,0},{3,1},{4,6},{5,7},{6,4},{7,5},{8,10},{9,11},{10,... | collective-permute-start | bytes 1966088 | tf_op jit(solution)/shard_map/ppermute | solution.py:30
  151.9 28.9 %collective-permute-start.5 = (bf16[2,128,1280]{2,1,0:T(8,128)(2,1)}, bf16[2,128,1280]{2,1,0:T(8,128)(2,1)}, u32[]{:S(2)}, u32[]{:S(2)}) collective-permute-start(bf16[2,128,1280]{2,1,0:T(8,128)(2,1)} %pad_maximum_fusion.4), channel_id=1, source_target_pairs={{0,4},{4,0},{1,5},{5,1},{2,6},{6,2},{3,7},{7,3},{8,12},{12,8},{9,1... | collective-permute-start | bytes 1966088 | tf_op jit(solution)/shard_map/ppermute | solution.py:30
  177.2 2.9 copy-start.19
  177.2 64.7 %collective-permute-start.34 = (bf16[2,256,1280]{2,1,0:T(8,128)(2,1)}, bf16[2,256,1280]{2,1,0:T(8,128)(2,1)}, u32[]{:S(2)}, u32[]{:S(2)}) collective-permute-start(bf16[2,256,1280]{2,1,0:T(8,128)(2,1)} %get-tuple-element.42), channel_id=1, source_target_pairs={{0,1},{1,0},{2,3},{3,2},{4,5},{5,4},{6,7},{7,6},{8,9},{9,8},{10,11... | collective-permute-start | bytes 3932168 | tf_op jit(solution)/shard_map/ppermute | solution.py:30
  178.7 93.3 %collective-permute-start.10 = (bf16[2,2,128,1280]{3,2,1,0:T(8,128)(2,1)S(1)}, bf16[2,2,128,1280]{3,2,1,0:T(8,128)(2,1)}, u32[]{:S(2)}, u32[]{:S(2)}) collective-permute-start(bf16[2,2,128,1280]{3,2,1,0:T(8,128)(2,1)S(1)} %pad_maximum_fusion.1.refs_6_), channel_id=1, source_target_pairs={{0,4},{4,0},{1,5},{5,1},{2,6},{6,2},{3,7},{7,3},{8,12},{12,8},{9,1... | collective-permute-start | bytes 3932168 | tf_op jit(solution)/shard_map/ppermute | solution.py:30
  180.2 32.6 %collective-permute-start.31 = (bf16[512,128]{1,0:T(8,128)(2,1)S(1)}, bf16[512,128]{1,0:T(8,128)(2,1)S(1)}, u32[]{:S(2)}, u32[]{:S(2)}) collective-permute-start(bf16[512,128]{1,0:T(8,128)(2,1)S(1)} %copy-done.19), channel_id=1, source_target_pairs={{0,4},{4,0},{1,5},{5,1},{2,6},{6,2},{3,7},{7,3},{8,12},{12,8},{9,1... | collective-permute-start | bytes 393224 | tf_op jit(solution)/shard_map/ppermute | solution.py:30
  182.1 90.4 %collective-permute-start.6 = (bf16[4,128,1280]{2,1,0:T(8,128)(2,1)S(1)}, bf16[4,128,1280]{2,1,0:T(8,128)(2,1)}, u32[]{:S(2)}, u32[]{:S(2)}) collective-permute-start(bf16[4,128,1280]{2,1,0:T(8,128)(2,1)S(1)} %pad_maximum_fusion.refs_4_), channel_id=1, source_target_pairs={{0,2},{1,3},{2,0},{3,1},{4,6},{5,7},{6,4},{7,5},{8,10},{9,11},{10,... | collective-permute-start | bytes 3932168 | tf_op jit(solution)/shard_map/ppermute | solution.py:30
  212.8 0.7 copy-start.20
  230.1 52.0 %collective-permute-start.32 = (bf16[2,384,1280]{2,1,0:T(8,128)(2,1)}, bf16[2,384,1280]{2,1,0:T(8,128)(2,1)}, u32[]{:S(2)}, u32[]{:S(2)}) collective-permute-start(bf16[2,384,1280]{2,1,0:T(8,128)(2,1)} %shard_map.177), channel_id=1, source_target_pairs={{0,1},{1,0},{2,3},{3,2},{4,5},{5,4},{6,7},{7,6},{8,9},{9,8},{10,11... | collective-permute-start | bytes 5898248 | tf_op jit(solution)/shard_map/ppermute | solution.py:30
  240.6 6.2 %copy-start.18 = (bf16[512,128]{1,0:T(8,128)(2,1)S(1)}, bf16[512,128]{1,0:T(8,128)(2,1)}, u32[]{:S(2)}) copy-start(bf16[512,128]{1,0:T(8,128)(2,1)} %get-tuple-element.23) | copy-start | bytes 393220
  240.6 6.2 %collective-permute-start = (bf16[512,128]{1,0:T(8,128)(2,1)}, bf16[512,128]{1,0:T(8,128)(2,1)S(1)}, u32[]{:S(2)}, u32[]{:S(2)}) collective-permute-start(bf16[512,128]{1,0:T(8,128)(2,1)} %get-tuple-element.24), channel_id=1, source_target_pairs={{0,4},{4,0},{1,5},{5,1},{2,6},{6,2},{3,7},{7,3},{8,12},{12,8},{9,1... | collective-permute-start | bytes 393224 | tf_op jit(solution)/shard_map/ppermute | solution.py:30
  243.3 29.3 %collective-permute-start.35 = (bf16[1,256,1280]{2,1,0:T(8,128)(2,1)S(1)}, bf16[1,256,1280]{2,1,0:T(8,128)(2,1)}, u32[]{:S(2)}, u32[]{:S(2)}) collective-permute-start(bf16[1,256,1280]{2,1,0:T(8,128)(2,1)S(1)} %add_convert_fusion.1), channel_id=1, source_target_pairs={{0,2},{1,3},{2,0},{3,1},{4,6},{5,7},{6,4},{7,5},{8,10},{9,11},{10,... | collective-permute-start | bytes 1966088 | tf_op jit(solution)/shard_map/ppermute | solution.py:30
  246.8 11.3 %collective-permute-start.1 = (bf16[2,512,128]{2,1,0:T(8,128)(2,1)S(1)}, bf16[2,512,128]{2,1,0:T(8,128)(2,1)S(1)}, u32[]{:S(2)}, u32[]{:S(2)}) collective-permute-start(bf16[2,512,128]{2,1,0:T(8,128)(2,1)S(1)} %pad_maximum_fusion.7.refs_0_), channel_id=1, source_target_pairs={{0,8},{8,0},{16,24},{24,16},{1,9},{9,1},{17,25},{25,17},{2,10},{10... | collective-permute-start | bytes 786440 | tf_op jit(solution)/shard_map/ppermute | solution.py:30
  258.1 13.9 %collective-permute-start.2 = (bf16[2,512,128]{2,1,0:T(8,128)(2,1)S(1)}, bf16[2,512,128]{2,1,0:T(8,128)(2,1)S(1)}, u32[]{:S(2)}, u32[]{:S(2)}) collective-permute-start(bf16[2,512,128]{2,1,0:T(8,128)(2,1)S(1)} %pad_maximum_fusion.7.refs_0_), channel_id=1, source_target_pairs={{0,16},{8,24},{16,0},{24,8},{1,17},{9,25},{17,1},{25,9},{2,18},{10... | collective-permute-start | bytes 786440 | tf_op jit(solution)/shard_map/ppermute | solution.py:30
  272.0 21.5 %collective-permute-start.13 = (bf16[2,2,128,1280]{3,2,1,0:T(8,128)(2,1)S(1)}, bf16[2,2,128,1280]{3,2,1,0:T(8,128)(2,1)}, u32[]{:S(2)}, u32[]{:S(2)}) collective-permute-start(bf16[2,2,128,1280]{3,2,1,0:T(8,128)(2,1)S(1)} %pad_maximum_fusion.1.refs_6_), channel_id=1, source_target_pairs={{0,1},{1,0},{2,3},{3,2},{4,5},{5,4},{6,7},{7,6},{8,9},{9,8},{10,11... | collective-permute-start | bytes 3932168 | tf_op jit(solution)/shard_map/ppermute | solution.py:30
  272.0 22.2 %collective-permute-start.11 = (bf16[4,128,1280]{2,1,0:T(8,128)(2,1)S(1)}, bf16[4,128,1280]{2,1,0:T(8,128)(2,1)}, u32[]{:S(2)}, u32[]{:S(2)}) collective-permute-start(bf16[4,128,1280]{2,1,0:T(8,128)(2,1)S(1)} %pad_maximum_fusion.refs_4_), channel_id=1, source_target_pairs={{0,1},{1,0},{2,3},{3,2},{4,5},{5,4},{6,7},{7,6},{8,9},{9,8},{10,11... | collective-permute-start | bytes 3932168 | tf_op jit(solution)/shard_map/ppermute | solution.py:30
  272.6 21.7 %collective-permute-start.14 = (bf16[2,2,128,1280]{3,2,1,0:T(8,128)(2,1)}, bf16[2,2,128,1280]{3,2,1,0:T(8,128)(2,1)}, u32[]{:S(2)}, u32[]{:S(2)}) collective-permute-start(bf16[2,2,128,1280]{3,2,1,0:T(8,128)(2,1)} %collective-permute-done.10.refs_7_), channel_id=1, source_target_pairs={{0,1},{1,0},{2,3},{3,2},{4,5},{5,4},{6,7},{7,6},{8,9},{9,8},{10,11... | collective-permute-start | bytes 3932168 | tf_op jit(solution)/shard_map/ppermute | solution.py:30
  272.6 21.6 %collective-permute-start.12 = (bf16[4,128,1280]{2,1,0:T(8,128)(2,1)}, bf16[4,128,1280]{2,1,0:T(8,128)(2,1)}, u32[]{:S(2)}, u32[]{:S(2)}) collective-permute-start(bf16[4,128,1280]{2,1,0:T(8,128)(2,1)} %collective-permute-done.6.refs_5_), channel_id=1, source_target_pairs={{0,1},{1,0},{2,3},{3,2},{4,5},{5,4},{6,7},{7,6},{8,9},{9,8},{10,11... | collective-permute-start | bytes 3932168 | tf_op jit(solution)/shard_map/ppermute | solution.py:30
  282.1 12.2 %copy-start.5 = (bf16[2,512,1280]{2,1,0:T(8,128)(2,1)S(1)}, bf16[2,512,1280]{2,1,0:T(8,128)(2,1)}, u32[]{:S(2)}) copy-start(bf16[2,512,1280]{2,1,0:T(8,128)(2,1)} %get-tuple-element.30.refs_16_) | copy-start | bytes 7864324
  282.1 12.2 %copy-start.8 = (f32[5120]{0:T(1024)S(1)}, f32[5120]{0:T(1024)}, u32[]{:S(2)}) copy-start(f32[5120]{0:T(1024)} %get-tuple-element.45) | copy-start | bytes 61444
  282.1 12.2 %copy-start.9 = (s32[6]{0:T(128)S(1)}, s32[6]{0:T(128)}, u32[]{:S(2)}) copy-start(s32[6]{0:T(128)} %stack.45.scal) | copy-start | bytes 76
  282.1 10.3 %collective-permute-start.3 = (bf16[2,512,128]{2,1,0:T(8,128)(2,1)S(1)}, bf16[2,512,128]{2,1,0:T(8,128)(2,1)S(1)}, u32[]{:S(2)}, u32[]{:S(2)}) collective-permute-start(bf16[2,512,128]{2,1,0:T(8,128)(2,1)S(1)} %pad_maximum_fusion.7.refs_0_), channel_id=1, source_target_pairs={{0,24},{8,16},{16,8},{24,0},{1,25},{9,17},{17,9},{25,1},{2,26},{10... | collective-permute-start | bytes 786440 | tf_op jit(solution)/shard_map/ppermute | solution.py:30
  292.3 34.7 %collective-permute-start.36 = (bf16[128,1280]{1,0:T(8,128)(2,1)}, bf16[128,1280]{1,0:T(8,128)(2,1)}, u32[]{:S(2)}, u32[]{:S(2)}) collective-permute-start(bf16[128,1280]{1,0:T(8,128)(2,1)} %fusion.2), channel_id=1, source_target_pairs={{0,4},{4,0},{1,5},{5,1},{2,6},{6,2},{3,7},{7,3},{8,12},{12,8},{9,1... | collective-permute-start | bytes 983048 | tf_op jit(solution)/shard_map/ppermute | solution.py:30
  293.6 35.9 %collective-permute-start.33 = (bf16[1,384,1280]{2,1,0:T(8,128)(2,1)}, bf16[1,384,1280]{2,1,0:T(8,128)(2,1)}, u32[]{:S(2)}, u32[]{:S(2)}) collective-permute-start(bf16[1,384,1280]{2,1,0:T(8,128)(2,1)} %add_convert_fusion), channel_id=1, source_target_pairs={{0,2},{1,3},{2,0},{3,1},{4,6},{5,7},{6,4},{7,5},{8,10},{9,11},{10,... | collective-permute-start | bytes 2949128 | tf_op jit(solution)/shard_map/ppermute | solution.py:30
  294.3 1.7 copy-start.6
  314.1 2.4 copy-start.3
  316.5 3.6 %collective-permute-start.30 = (f32[8,128]{1,0:T(8,128)S(1)}, f32[8,128]{1,0:T(8,128)S(1)}, u32[]{:S(2)}, u32[]{:S(2)}) collective-permute-start(f32[8,128]{1,0:T(8,128)S(1)} %get-tuple-element.33.refs_0_), channel_id=1, source_target_pairs={{0,4},{4,0},{1,5},{5,1},{2,6},{6,2},{3,7},{7,3},{8,12},{12,8},{9,1... | collective-permute-start | bytes 12296 | tf_op jit(solution)/shard_map/ppermute | solution.py:30
  320.1 2.5 copy-start.4
  327.0 2.4 copy-start.2
  329.4 3.0 copy-start.1

commit v4 on v3

--- a/solution.py
+++ b/solution.py
@@ -83,14 +83,20 @@
     refs = refs[held:]
     out_ref = refs[0]
     hidden_ref = refs[1] if keep else None
-    joined, normed = refs[-2:]
+    joined, normed, sems = refs[-3:]
     tile, width = noisy_ref.shape
     head = weight_ref.shape[2]
+    copies = [
+        pltpu.make_async_copy(
+            weight_ref.at[k], joined.at[:, pl.ds(k * head, head)], sems.at[k]
+        )
+        for k in range(3)
+    ]
 
     @pl.when(pl.program_id(0) == 0)
     def _():
-        for k in range(3):
-            joined[:, k * head : (k + 1) * head] = weight_ref[k]
+        for copy in copies:
+            copy.start()
 
     def step(t, carry):
         for u in range(2):
@@ -104,6 +110,12 @@
         return carry
 
     lax.fori_loop(0, tile // 32, step, 0)
+
+    @pl.when(pl.program_id(0) == 0)
+    def _():
+        for copy in copies:
+            copy.wait()
+
     for v in range(variants):
         out_ref[v] = dot(normed[v], joined[...])
     if keep:
@@ -128,7 +140,7 @@
             pl.BlockSpec((tile, width), lambda i: (first + i, 0)),
             resident((variants, width)),
             resident((1, width)),
-            resident(weight.shape),
+            ANY,
         ]
         + [ANY] * len(into),
         out_specs=out_specs,
@@ -137,6 +149,7 @@
         scratch_shapes=[
             pltpu.VMEM((width, 3 * head), BF16),
             pltpu.VMEM((variants, tile, width), BF16),
+            pltpu.SemaphoreType.DMA((3,)),
         ],
         cost_estimate=pl.CostEstimate(
             flops=2 * variants * count * width * 3 * head,

time: 334 us -> 329 us (0.985)
  Pallas kernels: 144 us -> 139 us
    pallas_call x3, Pallas kernels: 51.8 us -> 46.9 us  [project(): pl.pallas_call(functools.partial(project_kernel, variants, keep, len(into...]
  transfers between devices with their start and end apart: 37 -> 37, of which waited for: 10 -> 10; matrix products, arithmetic and copies ran while one was open for 8% -> 8% of each run, Pallas kernels for 42% -> 41%
where the time goes in v4:
time: 329 us; the launch traced here: 328 us
  Pallas kernels  139 us (42%)
  waiting for transfers between devices  91.8 us (28%)
  starting transfers between devices  60.2 us (18%)
  other arithmetic  23.7 us (7%)
  local copies, waits for them, and re-layouts  10.2 us (3%)
    ppermute x37, waiting for transfers between devices, move(): return lax.ppermute(value, axis, swap(lax.axis_size(axis), bit))  91.8 us
    ppermute x37, starting transfers between devices, move(): return lax.ppermute(value, axis, swap(lax.axis_size(axis), bit))  60.2 us
    pallas_call x3, Pallas kernels, project(): pl.pallas_call(functools.partial(project_kernel, variants, keep, len(into...  46.9 us
    pallas_call x2, Pallas kernels, post(): pl.pallas_call(kernel, grid_spec=pltpu.PrefetchScalarGridSpec(num_scalar_...  24.6 us
    pallas_call x1, Pallas kernels, guide(): pl.pallas_call(functools.partial(guide_kernel, attn.chunks[0], out.chunks...  18 us
    pallas_call x2, Pallas kernels, attend(): pl.pallas_call(functools.partial(attend_kernel, variants, seqs, per), gri...  18 us
    pallas_call x2, Pallas kernels, weight_grad(): pl.pallas_call(weight_kernel, grid_spec=pltpu.PrefetchScalarGridSpec(num_...  14 us
    pallas_call x1, Pallas kernels, backward(): pl.pallas_call(functools.partial(backward_kernel, seqs, per), grid_spec=p...  9.64 us
  transfers between devices with their start and end apart: 37, of which 10 were waited for; matrix products, arithmetic and copies ran while one was open for 8% of the time, Pallas kernels for 41%

profile of v4, /device:TPU:0, one launch (start us, length us, event | category | flops | bytes accessed | tf_op | source)
XLA Modules:
  0.0 327.6 jit_solution(4860552371883337040)
XLA Ops:
  0.7 1.3 copy-done
  2.0 4.1 %collective-permute-start.22 = (bf16[1,128,1280]{2,1,0:T(8,128)(2,1)S(1)}, bf16[1,128,1280]{2,1,0:T(8,128)(2,1)S(1)}, u32[]{:S(2)}, u32[]{:S(2)}) collective-permute-start(bf16[1,128,1280]{2,1,0:T(8,128)(2,1)S(1)} %dynamic-slice_bitcast_fusion), channel_id=1, source_target_pairs={{0,16},{8,24},{16,0},{24,8},{1,17},{9,25},{17,1},{25,9},{2,18},{10... | collective-permute-start | bytes 983048 | tf_op jit(solution)/shard_map/ppermute | solution.py:30
  6.1 1.3 collective-permute-start.23
  9.1 0.8 reduce
  9.8 1.4 select_convert_fusion
  11.2 17.5 %collective-permute-done.22 = bf16[1,128,1280]{2,1,0:T(8,128)(2,1)S(1)} collective-permute-done((bf16[1,128,1280]{2,1,0:T(8,128)(2,1)S(1)}, bf16[1,128,1280]{2,1,0:T(8,128)(2,1)S(1)}, u32[]{:S(2)}, u32[]{:S(2)}) %collective-permute-start.22) | collective-permute-done | bytes 327712 | tf_op jit(solution)/shard_map/ppermute | solution.py:30
  28.8 1.9 collective-permute-start.24
  30.7 0.9 pad_maximum_fusion.5
  31.6 1.5 collective-permute-start.20
  33.1 17.4 %shard_map.169 = (f32[1,1024,384]{2,1,0:T(8,128)}, bf16[1024,5120]{1,0:T(8,128)(2,1)}) custom-call(bf16[1024,5120]{1,0:T(8,128)(2,1)} %bitcast.40, f32[1,5120]{1,0:T(1,128)} %bitcast.33, f32[1,5120]{1,0:T(1,128)} %bitcast.56, bf16[3,5120,128]{2,1,0:T(8,128)(2,1)} %weight_ref.5), custom_call_target="tpu_custom_call" | custom-call | flops 4026531840 | bytes 24903680 | tf_op jit(solution)/shard_map/pallas_call | solution.py:136
  51.3 1.2 pad_maximum_fusion.2.refs_4_
  54.0 2.9 fusion
  57.0 7.6 %shard_map.170 = (bf16[512,128]{1,0:T(8,128)(2,1)}, bf16[512,128]{1,0:T(8,128)(2,1)}, bf16[1024,128]{1,0:T(8,128)(2,1)}, bf16[1024,128]{1,0:T(8,128)(2,1)}, bf16[1024,128]{1,0:T(8,128)(2,1)}) custom-call(s32[6]{0:T(128)} %stack.45.scal, f32[1,1024,384]{2,1,0:T(8,128)} %get-tuple-element.27.qkv_ref, f32[2,128]{1,0:T(2,128)} %gain_ref.5, ...), custom_call_target="tpu_custom_call" | custom-call | flops 2147483648 | bytes 1572864 | tf_op jit(solution)/shard_map/pallas_call | solution.py:226
  64.6 1.7 collective-permute-start.15
  66.3 1.0 dynamic-slice_bitcast_fusion.1
  67.3 8.5 %collective-permute-start.7 = (bf16[1,128,1280]{2,1,0:T(8,128)(2,1)S(1)}, bf16[1,128,1280]{2,1,0:T(8,128)(2,1)S(1)}, u32[]{:S(2)}, u32[]{:S(2)}) collective-permute-start(bf16[1,128,1280]{2,1,0:T(8,128)(2,1)S(1)} %dynamic-slice_bitcast_fusion.1), channel_id=1, source_target_pairs={{0,16},{8,24},{16,0},{24,8},{1,17},{9,25},{17,1},{25,9},{2,18},{10... | collective-permute-start | bytes 983048 | tf_op jit(solution)/shard_map/ppermute | solution.py:30
  76.3 5.3 %collective-permute-done.15 = bf16[512,128]{1,0:T(8,128)(2,1)S(1)} collective-permute-done((bf16[512,128]{1,0:T(8,128)(2,1)}, bf16[512,128]{1,0:T(8,128)(2,1)S(1)}, u32[]{:S(2)}, u32[]{:S(2)}) %collective-permute-start.15) | collective-permute-done | bytes 131104 | tf_op jit(solution)/shard_map/ppermute | solution.py:30
  81.6 8.7 %collective-permute-start.4 = (bf16[1,128,1280]{2,1,0:T(8,128)(2,1)S(1)}, bf16[1,128,1280]{2,1,0:T(8,128)(2,1)}, u32[]{:S(2)}, u32[]{:S(2)}) collective-permute-start(bf16[1,128,1280]{2,1,0:T(8,128)(2,1)S(1)} %dynamic-slice_bitcast_fusion.1), channel_id=1, source_target_pairs={{0,8},{8,0},{16,24},{24,16},{1,9},{9,1},{17,25},{25,17},{2,10},{10... | collective-permute-start | bytes 983048 | tf_op jit(solution)/shard_map/ppermute | solution.py:30
  90.3 0.7 pad_maximum_fusion.9.shift_ref
  90.9 5.7 %collective-permute-done.7 = bf16[1,128,1280]{2,1,0:T(8,128)(2,1)S(1)} collective-permute-done((bf16[1,128,1280]{2,1,0:T(8,128)(2,1)S(1)}, bf16[1,128,1280]{2,1,0:T(8,128)(2,1)S(1)}, u32[]{:S(2)}, u32[]{:S(2)}) %collective-permute-start.7) | collective-permute-done | bytes 327712 | tf_op jit(solution)/shard_map/ppermute | solution.py:30
  96.7 1.1 pad_maximum_fusion.8.refs_0_
  97.8 6.2 %collective-permute-start.16 = (bf16[2,512,128]{2,1,0:T(8,128)(2,1)S(1)}, bf16[2,512,128]{2,1,0:T(8,128)(2,1)}, u32[]{:S(2)}, u32[]{:S(2)}) collective-permute-start(bf16[2,512,128]{2,1,0:T(8,128)(2,1)S(1)} %pad_maximum_fusion.8.refs_0_), channel_id=1, source_target_pairs={{0,8},{8,0},{16,24},{24,16},{1,9},{9,1},{17,25},{25,17},{2,10},{10... | collective-permute-start | bytes 786440 | tf_op jit(solution)/shard_map/ppermute | solution.py:30
  104.6 14.6 %shard_map.166.refs_0_ = f32[2,1024,384]{2,1,0:T(8,128)} custom-call(bf16[1024,5120]{1,0:T(8,128)(2,1)} %bitcast.41, f32[2,5120]{1,0:T(2,128)} %pad_maximum_fusion.9.shift_ref, f32[1,5120]{1,0:T(1,128)} %bitcast.54, bf16[3,5120,128]{2,1,0:T(8,128)(2,1)} %weight_ref.4), custom_call_target="tpu_custom_call" | custom-call | flops 4026531840 | bytes 9175040 | tf_op jit(solution)/shard_map/pallas_call | solution.py:136
  120.0 14.8 %shard_map.167.qkv_ref = f32[2,1024,384]{2,1,0:T(8,128)} custom-call(bf16[1024,5120]{1,0:T(8,128)(2,1)} %bitcast.42, f32[2,5120]{1,0:T(2,128)} %pad_maximum_fusion.9.shift_ref, f32[1,5120]{1,0:T(1,128)} %bitcast.55, bf16[3,5120,128]{2,1,0:T(8,128)(2,1)} %weight_ref.4, f32[2,1024,384]{2,1,0:T(8,128)} %shard_map.166.refs_0_), custom_call_target="tpu_custom_call", output_to_operand_aliasing={{}: (4, {})} | custom-call | flops 4026531840 | bytes 9175040 | tf_op jit(solution)/shard_map/pallas_call | solution.py:136
  134.9 2.3 collective-permute-start.18
  137.2 1.9 pad_maximum_fusion.4
  139.1 0.9 maximum_bitcast_fusion
  140.0 5.5 %collective-permute-done.18.refs_3_ = bf16[2,512,128]{2,1,0:T(8,128)(2,1)S(1)} collective-permute-done((bf16[2,512,128]{2,1,0:T(8,128)(2,1)S(1)}, bf16[2,512,128]{2,1,0:T(8,128)(2,1)S(1)}, u32[]{:S(2)}, u32[]{:S(2)}) %collective-permute-start.18) | collective-permute-done | bytes 262176 | tf_op jit(solution)/shard_map/ppermute | solution.py:30
  145.5 1.5 collective-permute-start.9
  147.7 12.0 %shard_map.171 = (bf16[2,512,1280]{2,1,0:T(8,128)(2,1)}, bf16[2,256,1280]{2,1,0:T(8,128)(2,1)}, f32[512,256]{1,0:T(8,128)}) custom-call(s32[6]{0:T(128)} %stack.45.scal, f32[1]{0:T(128)S(6)} %div.38.noise_ref, bf16[2,512,128]{2,1,0:T(8,128)(2,1)} %copy-done.12, bf16[2,512,128]{2,1,0:T(8,128)(2,1)} %collective-permute-done.16.refs_1_, ...), custom_call_target="tpu_custom_call" | custom-call | flops 4026531840 | bytes 15728640 | tf_op jit(solution)/shard_map/pallas_call | solution.py:381
  159.7 12.6 %shard_map.172 = (bf16[2,512,1280]{2,1,0:T(8,128)(2,1)}, bf16[2,256,1280]{2,1,0:T(8,128)(2,1)}, bf16[512,128]{1,0:T(8,128)(2,1)}, bf16[512,128]{1,0:T(8,128)(2,1)}) custom-call(s32[6]{0:T(128)} %stack.45.scal, f32[1]{0:T(128)S(6)} %div.38.noise_ref, bf16[2,512,128]{2,1,0:T(8,128)(2,1)} %copy-done.12, bf16[2,512,128]{2,1,0:T(8,128)(2,1)} %collective-permute-done.16.refs_1_, ...), custom_call_target="tpu_custom_call" | custom-call | flops 4026531840 | bytes 15728640 | tf_op jit(solution)/shard_map/pallas_call | solution.py:381
  172.5 1.4 pad_maximum_fusion.1.refs_6_
  173.9 1.4 collective-permute-start.10
  175.3 0.7 collective-permute-start.31
  176.0 1.3 pad_maximum_fusion.refs_4_
  177.3 0.7 collective-permute-start.6
  178.0 29.9 %collective-permute-done.31.refs_1_ = bf16[512,128]{1,0:T(8,128)(2,1)S(1)} collective-permute-done((bf16[512,128]{1,0:T(8,128)(2,1)S(1)}, bf16[512,128]{1,0:T(8,128)(2,1)S(1)}, u32[]{:S(2)}, u32[]{:S(2)}) %collective-permute-start.31) | collective-permute-done | bytes 131104 | tf_op jit(solution)/shard_map/ppermute | solution.py:30
  208.6 9.6 %shard_map.175.grad_ref = bf16[384,1024]{1,0:T(8,128)(2,1)} custom-call(s32[6]{0:T(128)} %stack.45.scal, bf16[1024,128]{1,0:T(8,128)(2,1)} %get-tuple-element.35.q_ref, bf16[1024,128]{1,0:T(8,128)(2,1)} %get-tuple-element.36.k_ref, bf16[1024,128]{1,0:T(8,128)(2,1)} %get-tuple-element.37.v_ref, f32[1,1024,384]{2,1,0:T(8,128)} %get-tuple-element.27.qkv_ref, ...), custom_call_target="tpu_custom_call" | custom-call | flops 2684354560 | bytes 1572864 | tf_op jit(solution)/shard_map/pallas_call | solution.py:577
  218.2 7.0 %shard_map.177 = bf16[2,384,1280]{2,1,0:T(8,128)(2,1)} custom-call(s32[6]{0:T(128)} %stack.45.scal, bf16[384,1024]{1,0:T(8,128)(2,1)} %shard_map.175.grad_ref, bf16[1024,5120]{1,0:T(8,128)(2,1)} %get-tuple-element.40.hidden_ref), custom_call_target="tpu_custom_call" | custom-call | flops 2013265920 | bytes 7208960 | tf_op jit(solution)/shard_map/pallas_call | solution.py:616
  225.3 10.4 %shard_map.168 = (bf16[512,128]{1,0:T(8,128)(2,1)}, bf16[512,128]{1,0:T(8,128)(2,1)}) custom-call(s32[6]{0:T(128)} %stack.45.scal, f32[2,1024,384]{2,1,0:T(8,128)} %shard_map.167.qkv_ref, f32[2,128]{1,0:T(2,128)} %gain_ref.3, f32[1024,128]{1,0:T(8,128)} %get-tuple-element.44.cos_ref, f32[1024,128]{1,0:T(8,128)} %get-tuple-element.43.sin_ref), custom_call_target="tpu_custom_call" | custom-call | flops 4294967296 | bytes 3145728 | tf_op jit(solution)/shard_map/pallas_call | solution.py:226
  235.7 1.3 collective-permute-start
  237.0 1.4 add_convert_fusion.1
  238.5 0.8 collective-permute-start.35
  239.3 2.6 collective-permute-done
  241.9 5.2 %collective-permute-start.1 = (bf16[2,512,128]{2,1,0:T(8,128)(2,1)S(1)}, bf16[2,512,128]{2,1,0:T(8,128)(2,1)S(1)}, u32[]{:S(2)}, u32[]{:S(2)}) collective-permute-start(bf16[2,512,128]{2,1,0:T(8,128)(2,1)S(1)} %pad_maximum_fusion.7.refs_0_), channel_id=1, source_target_pairs={{0,8},{8,0},{16,24},{24,16},{1,9},{9,1},{17,25},{25,17},{2,10},{10... | collective-permute-start | bytes 786440 | tf_op jit(solution)/shard_map/ppermute | solution.py:30
  247.1 6.2 %collective-permute-done.1.refs_1_ = bf16[2,512,128]{2,1,0:T(8,128)(2,1)S(1)} collective-permute-done((bf16[2,512,128]{2,1,0:T(8,128)(2,1)S(1)}, bf16[2,512,128]{2,1,0:T(8,128)(2,1)S(1)}, u32[]{:S(2)}, u32[]{:S(2)}) %collective-permute-start.1) | collective-permute-done | bytes 262176 | tf_op jit(solution)/shard_map/ppermute | solution.py:30
  253.2 2.8 collective-permute-start.2
  256.0 11.2 %collective-permute-done.2.refs_2_ = bf16[2,512,128]{2,1,0:T(8,128)(2,1)S(1)} collective-permute-done((bf16[2,512,128]{2,1,0:T(8,128)(2,1)S(1)}, bf16[2,512,128]{2,1,0:T(8,128)(2,1)S(1)}, u32[]{:S(2)}, u32[]{:S(2)}) %collective-permute-start.2) | collective-permute-done | bytes 262176 | tf_op jit(solution)/shard_map/ppermute | solution.py:30
  268.2 7.0 %shard_map.176.refs_0_ = bf16[2,384,1280]{2,1,0:T(8,128)(2,1)} custom-call(s32[6]{0:T(128)} %stack.45.scal, bf16[384,1024]{1,0:T(8,128)(2,1)} %shard_map.175.grad_ref, bf16[1024,5120]{1,0:T(8,128)(2,1)} %get-tuple-element.40.hidden_ref), custom_call_target="tpu_custom_call" | custom-call | flops 2013265920 | bytes 7208960 | tf_op jit(solution)/shard_map/pallas_call | solution.py:616
  275.2 2.0 fusion.2
  277.2 2.5 collective-permute-start.3
  279.8 2.7 add_convert_fusion
  282.4 5.0 %collective-permute-done.3.refs_3_ = bf16[2,512,128]{2,1,0:T(8,128)(2,1)S(1)} collective-permute-done((bf16[2,512,128]{2,1,0:T(8,128)(2,1)S(1)}, bf16[2,512,128]{2,1,0:T(8,128)(2,1)S(1)}, u32[]{:S(2)}, u32[]{:S(2)}) %collective-permute-start.3) | collective-permute-done | bytes 262176 | tf_op jit(solution)/shard_map/ppermute | solution.py:30
  287.5 1.2 collective-permute-start.36
  288.7 0.7 collective-permute-start.33
  289.5 1.7 copy-done.6
  291.2 18.0 %shard_map.173 = (bf16[512,5120]{1,0:T(8,128)(2,1)S(1)}, f32[8,128]{1,0:T(8,128)S(1)}) custom-call(s32[6]{0:T(128)S(1)} %copy-done.9, f32[1]{0:T(128)S(6)} %div.38.noise_ref, bf16[2,512,128]{2,1,0:T(8,128)(2,1)S(1)} %pad_maximum_fusion.7.refs_0_, bf16[2,512,128]{2,1,0:T(8,128)(2,1)S(1)} %collective-permute-done.1.refs_1_, ...), custom_call_target="tpu_custom_call" | custom-call | flops 5368709120 | bytes 31457280 | tf_op jit(solution)/shard_map/pallas_call | solution.py:471
  309.3 2.3 copy-done.3
  311.6 0.8 collective-permute-start.30
  312.4 2.8 collective-permute-done.30.refs_1_
  315.2 2.5 copy-done.4
  317.7 4.5 %shard_map.174 = bf16[512,5120]{1,0:T(8,128)(2,1)} custom-call(f32[8,128]{1,0:T(8,128)S(1)} %get-tuple-element.33.refs_0_, f32[8,128]{1,0:T(8,128)S(1)} %collective-permute-done.30.refs_1_, bf16[512,5120]{1,0:T(8,128)(2,1)S(1)} %copy-done.4), custom_call_target="tpu_custom_call" | custom-call | flops 10485760 | bytes 10485760 | tf_op jit(solution)/shard_map/pallas_call | solution.py:655
  322.2 2.4 bitcast_add_fusion
  324.6 3.0 shard_map.178
  (91 shorter events, 6.3 us)
Async XLA Ops:
  0.6 1.3 copy-start
  2.0 26.8 %collective-permute-start.22 = (bf16[1,128,1280]{2,1,0:T(8,128)(2,1)S(1)}, bf16[1,128,1280]{2,1,0:T(8,128)(2,1)S(1)}, u32[]{:S(2)}, u32[]{:S(2)}) collective-permute-start(bf16[1,128,1280]{2,1,0:T(8,128)(2,1)S(1)} %dynamic-slice_bitcast_fusion), channel_id=1, source_target_pairs={{0,16},{8,24},{16,0},{24,8},{1,17},{9,25},{17,1},{25,9},{2,18},{10... | collective-permute-start | bytes 983048 | tf_op jit(solution)/shard_map/ppermute | solution.py:30
  6.1 22.7 %collective-permute-start.23 = (bf16[1,128,1280]{2,1,0:T(8,128)(2,1)S(1)}, bf16[1,128,1280]{2,1,0:T(8,128)(2,1)S(1)}, u32[]{:S(2)}, u32[]{:S(2)}) collective-permute-start(bf16[1,128,1280]{2,1,0:T(8,128)(2,1)S(1)} %dynamic-slice_bitcast_fusion), channel_id=1, source_target_pairs={{0,24},{8,16},{16,8},{24,0},{1,25},{9,17},{17,9},{25,1},{2,26},{10... | collective-permute-start | bytes 983048 | tf_op jit(solution)/shard_map/ppermute | solution.py:30
  7.5 23.3 %collective-permute-start.19 = (bf16[1,128,1280]{2,1,0:T(8,128)(2,1)S(1)}, bf16[1,128,1280]{2,1,0:T(8,128)(2,1)S(1)}, u32[]{:S(2)}, u32[]{:S(2)}) collective-permute-start(bf16[1,128,1280]{2,1,0:T(8,128)(2,1)S(1)} %dynamic-slice_bitcast_fusion), channel_id=1, source_target_pairs={{0,8},{8,0},{16,24},{24,16},{1,9},{9,1},{17,25},{25,17},{2,10},{10... | collective-permute-start | bytes 983048 | tf_op jit(solution)/shard_map/ppermute | solution.py:30
  28.8 21.7 %collective-permute-start.24 = (bf16[1,2,128,1280]{3,2,1,0:T(8,128)(2,1)S(1)}, bf16[1,2,128,1280]{3,2,1,0:T(8,128)(2,1)S(1)}, u32[]{:S(2)}, u32[]{:S(2)}) collective-permute-start(bf16[1,2,128,1280]{3,2,1,0:T(8,128)(2,1)S(1)} %maximum_bitcast_fusion.1), channel_id=1, source_target_pairs={{0,2},{1,3},{2,0},{3,1},{4,6},{5,7},{6,4},{7,5},{8,10},{9,11},{10,... | collective-permute-start | bytes 1966088 | tf_op jit(solution)/shard_map/ppermute | solution.py:30
  31.6 19.7 %collective-permute-start.20 = (bf16[2,128,1280]{2,1,0:T(8,128)(2,1)}, bf16[2,128,1280]{2,1,0:T(8,128)(2,1)}, u32[]{:S(2)}, u32[]{:S(2)}) collective-permute-start(bf16[2,128,1280]{2,1,0:T(8,128)(2,1)} %pad_maximum_fusion.5), channel_id=1, source_target_pairs={{0,4},{4,0},{1,5},{5,1},{2,6},{6,2},{3,7},{7,3},{8,12},{12,8},{9,1... | collective-permute-start | bytes 1966088 | tf_op jit(solution)/shard_map/ppermute | solution.py:30
  50.7 46.0 %copy-start.10 = (bf16[2,2,128,1280]{3,2,1,0:T(8,128)(2,1)}, bf16[2,2,128,1280]{3,2,1,0:T(8,128)(2,1)S(1)}, u32[]{:S(2)}) copy-start(bf16[2,2,128,1280]{3,2,1,0:T(8,128)(2,1)S(1)} %pad_maximum_fusion.3.refs_6_) | copy-start | bytes 3932164
  50.7 53.3 %collective-permute-start.25 = (bf16[2,2,128,1280]{3,2,1,0:T(8,128)(2,1)S(1)}, bf16[2,2,128,1280]{3,2,1,0:T(8,128)(2,1)}, u32[]{:S(2)}, u32[]{:S(2)}) collective-permute-start(bf16[2,2,128,1280]{3,2,1,0:T(8,128)(2,1)S(1)} %pad_maximum_fusion.3.refs_6_), channel_id=1, source_target_pairs={{0,4},{4,0},{1,5},{5,1},{2,6},{6,2},{3,7},{7,3},{8,12},{12,8},{9,1... | collective-permute-start | bytes 3932168 | tf_op jit(solution)/shard_map/ppermute | solution.py:30
  52.5 51.5 %copy-start.11 = (bf16[4,128,1280]{2,1,0:T(8,128)(2,1)}, bf16[4,128,1280]{2,1,0:T(8,128)(2,1)S(1)}, u32[]{:S(2)}) copy-start(bf16[4,128,1280]{2,1,0:T(8,128)(2,1)S(1)} %pad_maximum_fusion.2.refs_4_) | copy-start | bytes 3932164
  52.5 52.0 %collective-permute-start.21 = (bf16[4,128,1280]{2,1,0:T(8,128)(2,1)S(1)}, bf16[4,128,1280]{2,1,0:T(8,128)(2,1)}, u32[]{:S(2)}, u32[]{:S(2)}) collective-permute-start(bf16[4,128,1280]{2,1,0:T(8,128)(2,1)S(1)} %pad_maximum_fusion.2.refs_4_), channel_id=1, source_target_pairs={{0,2},{1,3},{2,0},{3,1},{4,6},{5,7},{6,4},{7,5},{8,10},{9,11},{10,... | collective-permute-start | bytes 3932168 | tf_op jit(solution)/shard_map/ppermute | solution.py:30
  57.0 33.3 %copy-start.7 = (f32[5120]{0:T(1024)S(1)}, f32[5120]{0:T(1024)}, u32[]{:S(2)}) copy-start(f32[5120]{0:T(1024)} %get-tuple-element.45) | copy-start | bytes 61444
  64.6 17.0 %collective-permute-start.15 = (bf16[512,128]{1,0:T(8,128)(2,1)}, bf16[512,128]{1,0:T(8,128)(2,1)S(1)}, u32[]{:S(2)}, u32[]{:S(2)}) collective-permute-start(bf16[512,128]{1,0:T(8,128)(2,1)} %get-tuple-element.29), channel_id=1, source_target_pairs={{0,4},{4,0},{1,5},{5,1},{2,6},{6,2},{3,7},{7,3},{8,12},{12,8},{9,1... | collective-permute-start | bytes 393224 | tf_op jit(solution)/shard_map/ppermute | solution.py:30
  67.3 29.4 %collective-permute-start.7 = (bf16[1,128,1280]{2,1,0:T(8,128)(2,1)S(1)}, bf16[1,128,1280]{2,1,0:T(8,128)(2,1)S(1)}, u32[]{:S(2)}, u32[]{:S(2)}) collective-permute-start(bf16[1,128,1280]{2,1,0:T(8,128)(2,1)S(1)} %dynamic-slice_bitcast_fusion.1), channel_id=1, source_target_pairs={{0,16},{8,24},{16,0},{24,8},{1,17},{9,25},{17,1},{25,9},{2,18},{10... | collective-permute-start | bytes 983048 | tf_op jit(solution)/shard_map/ppermute | solution.py:30
  75.8 21.9 %collective-permute-start.8 = (bf16[1,128,1280]{2,1,0:T(8,128)(2,1)S(1)}, bf16[1,128,1280]{2,1,0:T(8,128)(2,1)S(1)}, u32[]{:S(2)}, u32[]{:S(2)}) collective-permute-start(bf16[1,128,1280]{2,1,0:T(8,128)(2,1)S(1)} %dynamic-slice_bitcast_fusion.1), channel_id=1, source_target_pairs={{0,24},{8,16},{16,8},{24,0},{1,25},{9,17},{17,9},{25,1},{2,26},{10... | collective-permute-start | bytes 983048 | tf_op jit(solution)/shard_map/ppermute | solution.py:30
  81.6 22.4 %collective-permute-start.4 = (bf16[1,128,1280]{2,1,0:T(8,128)(2,1)S(1)}, bf16[1,128,1280]{2,1,0:T(8,128)(2,1)}, u32[]{:S(2)}, u32[]{:S(2)}) collective-permute-start(bf16[1,128,1280]{2,1,0:T(8,128)(2,1)S(1)} %dynamic-slice_bitcast_fusion.1), channel_id=1, source_target_pairs={{0,8},{8,0},{16,24},{24,16},{1,9},{9,1},{17,25},{25,17},{2,10},{10... | collective-permute-start | bytes 983048 | tf_op jit(solution)/shard_map/ppermute | solution.py:30
  96.7 7.9 %copy-start.14 = (bf16[1,128,1280]{2,1,0:T(8,128)(2,1)}, bf16[1,128,1280]{2,1,0:T(8,128)(2,1)S(1)}, u32[]{:S(2)}) copy-start(bf16[1,128,1280]{2,1,0:T(8,128)(2,1)S(1)} %collective-permute-done.7) | copy-start | bytes 983044
  96.7 50.4 %collective-permute-start.28 = (bf16[2,2,128,1280]{3,2,1,0:T(8,128)(2,1)S(1)}, bf16[2,2,128,1280]{3,2,1,0:T(8,128)(2,1)}, u32[]{:S(2)}, u32[]{:S(2)}) collective-permute-start(bf16[2,2,128,1280]{3,2,1,0:T(8,128)(2,1)S(1)} %pad_maximum_fusion.3.refs_6_), channel_id=1, source_target_pairs={{0,1},{1,0},{2,3},{3,2},{4,5},{5,4},{6,7},{7,6},{8,9},{9,8},{10,11... | collective-permute-start | bytes 3932168 | tf_op jit(solution)/shard_map/ppermute | solution.py:30
  97.7 37.2 %copy-start.12 = (bf16[2,512,128]{2,1,0:T(8,128)(2,1)}, bf16[2,512,128]{2,1,0:T(8,128)(2,1)S(1)}, u32[]{:S(2)}) copy-start(bf16[2,512,128]{2,1,0:T(8,128)(2,1)S(1)} %pad_maximum_fusion.8.refs_0_) | copy-start | bytes 786436
  97.7 6.9 %copy-start.16 = (bf16[1,128,1280]{2,1,0:T(8,128)(2,1)}, bf16[1,128,1280]{2,1,0:T(8,128)(2,1)S(1)}, u32[]{:S(2)}) copy-start(bf16[1,128,1280]{2,1,0:T(8,128)(2,1)S(1)} %collective-permute-done.8) | copy-start | bytes 983044
  97.8 22.2 %collective-permute-start.16 = (bf16[2,512,128]{2,1,0:T(8,128)(2,1)S(1)}, bf16[2,512,128]{2,1,0:T(8,128)(2,1)}, u32[]{:S(2)}, u32[]{:S(2)}) collective-permute-start(bf16[2,512,128]{2,1,0:T(8,128)(2,1)S(1)} %pad_maximum_fusion.8.refs_0_), channel_id=1, source_target_pairs={{0,8},{8,0},{16,24},{24,16},{1,9},{9,1},{17,25},{25,17},{2,10},{10... | collective-permute-start | bytes 786440 | tf_op jit(solution)/shard_map/ppermute | solution.py:30
  104.0 55.7 %collective-permute-start.26 = (bf16[4,128,1280]{2,1,0:T(8,128)(2,1)S(1)}, bf16[4,128,1280]{2,1,0:T(8,128)(2,1)}, u32[]{:S(2)}, u32[]{:S(2)}) collective-permute-start(bf16[4,128,1280]{2,1,0:T(8,128)(2,1)S(1)} %pad_maximum_fusion.2.refs_4_), channel_id=1, source_target_pairs={{0,1},{1,0},{2,3},{3,2},{4,5},{5,4},{6,7},{7,6},{8,9},{9,8},{10,11... | collective-permute-start | bytes 3932168 | tf_op jit(solution)/shard_map/ppermute | solution.py:30
  104.0 55.7 %collective-permute-start.29 = (bf16[2,2,128,1280]{3,2,1,0:T(8,128)(2,1)}, bf16[2,2,128,1280]{3,2,1,0:T(8,128)(2,1)}, u32[]{:S(2)}, u32[]{:S(2)}) collective-permute-start(bf16[2,2,128,1280]{3,2,1,0:T(8,128)(2,1)} %collective-permute-done.25.refs_7_), channel_id=1, source_target_pairs={{0,1},{1,0},{2,3},{3,2},{4,5},{5,4},{6,7},{7,6},{8,9},{9,8},{10,11... | collective-permute-start | bytes 3932168 | tf_op jit(solution)/shard_map/ppermute | solution.py:30
  104.5 55.2 %collective-permute-start.27 = (bf16[4,128,1280]{2,1,0:T(8,128)(2,1)}, bf16[4,128,1280]{2,1,0:T(8,128)(2,1)}, u32[]{:S(2)}, u32[]{:S(2)}) collective-permute-start(bf16[4,128,1280]{2,1,0:T(8,128)(2,1)} %collective-permute-done.21.refs_5_), channel_id=1, source_target_pairs={{0,1},{1,0},{2,3},{3,2},{4,5},{5,4},{6,7},{7,6},{8,9},{9,8},{10,11... | collective-permute-start | bytes 3932168 | tf_op jit(solution)/shard_map/ppermute | solution.py:30
  120.0 15.0 %collective-permute-start.17 = (bf16[2,512,128]{2,1,0:T(8,128)(2,1)S(1)}, bf16[2,512,128]{2,1,0:T(8,128)(2,1)}, u32[]{:S(2)}, u32[]{:S(2)}) collective-permute-start(bf16[2,512,128]{2,1,0:T(8,128)(2,1)S(1)} %pad_maximum_fusion.8.refs_0_), channel_id=1, source_target_pairs={{0,16},{8,24},{16,0},{24,8},{1,17},{9,25},{17,1},{25,9},{2,18},{10... | collective-permute-start | bytes 786440 | tf_op jit(solution)/shard_map/ppermute | solution.py:30
  134.9 4.2 %copy-start.15 = (bf16[1,128,1280]{2,1,0:T(8,128)(2,1)S(1)}, bf16[1,128,1280]{2,1,0:T(8,128)(2,1)}, u32[]{:S(2)}) copy-start(bf16[1,128,1280]{2,1,0:T(8,128)(2,1)} %copy-done.14) | copy-start | bytes 983044
  134.9 4.2 %copy-start.17 = (bf16[1,128,1280]{2,1,0:T(8,128)(2,1)S(1)}, bf16[1,128,1280]{2,1,0:T(8,128)(2,1)}, u32[]{:S(2)}) copy-start(bf16[1,128,1280]{2,1,0:T(8,128)(2,1)} %copy-done.16) | copy-start | bytes 983044
  134.9 10.6 %collective-permute-start.18 = (bf16[2,512,128]{2,1,0:T(8,128)(2,1)S(1)}, bf16[2,512,128]{2,1,0:T(8,128)(2,1)S(1)}, u32[]{:S(2)}, u32[]{:S(2)}) collective-permute-start(bf16[2,512,128]{2,1,0:T(8,128)(2,1)S(1)} %pad_maximum_fusion.8.refs_0_), channel_id=1, source_target_pairs={{0,24},{8,16},{16,8},{24,0},{1,25},{9,17},{17,9},{25,1},{2,26},{10... | collective-permute-start | bytes 786440 | tf_op jit(solution)/shard_map/ppermute | solution.py:30
  145.5 1.5 copy-start.13
  145.5 26.9 %collective-permute-start.9 = (bf16[1,2,128,1280]{3,2,1,0:T(8,128)(2,1)}, bf16[1,2,128,1280]{3,2,1,0:T(8,128)(2,1)}, u32[]{:S(2)}, u32[]{:S(2)}) collective-permute-start(bf16[1,2,128,1280]{3,2,1,0:T(8,128)(2,1)} %maximum_bitcast_fusion), channel_id=1, source_target_pairs={{0,2},{1,3},{2,0},{3,1},{4,6},{5,7},{6,4},{7,5},{8,10},{9,11},{10,... | collective-permute-start | bytes 1966088 | tf_op jit(solution)/shard_map/ppermute | solution.py:30
  147.1 28.9 %collective-permute-start.5 = (bf16[2,128,1280]{2,1,0:T(8,128)(2,1)}, bf16[2,128,1280]{2,1,0:T(8,128)(2,1)}, u32[]{:S(2)}, u32[]{:S(2)}) collective-permute-start(bf16[2,128,1280]{2,1,0:T(8,128)(2,1)} %pad_maximum_fusion.4), channel_id=1, source_target_pairs={{0,4},{4,0},{1,5},{5,1},{2,6},{6,2},{3,7},{7,3},{8,12},{12,8},{9,1... | collective-permute-start | bytes 1966088 | tf_op jit(solution)/shard_map/ppermute | solution.py:30
  172.4 2.9 copy-start.19
  172.4 64.7 %collective-permute-start.34 = (bf16[2,256,1280]{2,1,0:T(8,128)(2,1)}, bf16[2,256,1280]{2,1,0:T(8,128)(2,1)}, u32[]{:S(2)}, u32[]{:S(2)}) collective-permute-start(bf16[2,256,1280]{2,1,0:T(8,128)(2,1)} %get-tuple-element.42), channel_id=1, source_target_pairs={{0,1},{1,0},{2,3},{3,2},{4,5},{5,4},{6,7},{7,6},{8,9},{9,8},{10,11... | collective-permute-start | bytes 3932168 | tf_op jit(solution)/shard_map/ppermute | solution.py:30
  173.9 93.3 %collective-permute-start.10 = (bf16[2,2,128,1280]{3,2,1,0:T(8,128)(2,1)S(1)}, bf16[2,2,128,1280]{3,2,1,0:T(8,128)(2,1)}, u32[]{:S(2)}, u32[]{:S(2)}) collective-permute-start(bf16[2,2,128,1280]{3,2,1,0:T(8,128)(2,1)S(1)} %pad_maximum_fusion.1.refs_6_), channel_id=1, source_target_pairs={{0,4},{4,0},{1,5},{5,1},{2,6},{6,2},{3,7},{7,3},{8,12},{12,8},{9,1... | collective-permute-start | bytes 3932168 | tf_op jit(solution)/shard_map/ppermute | solution.py:30
  175.3 32.6 %collective-permute-start.31 = (bf16[512,128]{1,0:T(8,128)(2,1)S(1)}, bf16[512,128]{1,0:T(8,128)(2,1)S(1)}, u32[]{:S(2)}, u32[]{:S(2)}) collective-permute-start(bf16[512,128]{1,0:T(8,128)(2,1)S(1)} %copy-done.19), channel_id=1, source_target_pairs={{0,4},{4,0},{1,5},{5,1},{2,6},{6,2},{3,7},{7,3},{8,12},{12,8},{9,1... | collective-permute-start | bytes 393224 | tf_op jit(solution)/shard_map/ppermute | solution.py:30
  177.3 90.4 %collective-permute-start.6 = (bf16[4,128,1280]{2,1,0:T(8,128)(2,1)S(1)}, bf16[4,128,1280]{2,1,0:T(8,128)(2,1)}, u32[]{:S(2)}, u32[]{:S(2)}) collective-permute-start(bf16[4,128,1280]{2,1,0:T(8,128)(2,1)S(1)} %pad_maximum_fusion.refs_4_), channel_id=1, source_target_pairs={{0,2},{1,3},{2,0},{3,1},{4,6},{5,7},{6,4},{7,5},{8,10},{9,11},{10,... | collective-permute-start | bytes 3932168 | tf_op jit(solution)/shard_map/ppermute | solution.py:30
  207.9 0.7 copy-start.20
  225.3 52.0 %collective-permute-start.32 = (bf16[2,384,1280]{2,1,0:T(8,128)(2,1)}, bf16[2,384,1280]{2,1,0:T(8,128)(2,1)}, u32[]{:S(2)}, u32[]{:S(2)}) collective-permute-start(bf16[2,384,1280]{2,1,0:T(8,128)(2,1)} %shard_map.177), channel_id=1, source_target_pairs={{0,1},{1,0},{2,3},{3,2},{4,5},{5,4},{6,7},{7,6},{8,9},{9,8},{10,11... | collective-permute-start | bytes 5898248 | tf_op jit(solution)/shard_map/ppermute | solution.py:30
  235.7 6.2 %copy-start.18 = (bf16[512,128]{1,0:T(8,128)(2,1)S(1)}, bf16[512,128]{1,0:T(8,128)(2,1)}, u32[]{:S(2)}) copy-start(bf16[512,128]{1,0:T(8,128)(2,1)} %get-tuple-element.23) | copy-start | bytes 393220
  235.7 6.2 %collective-permute-start = (bf16[512,128]{1,0:T(8,128)(2,1)}, bf16[512,128]{1,0:T(8,128)(2,1)S(1)}, u32[]{:S(2)}, u32[]{:S(2)}) collective-permute-start(bf16[512,128]{1,0:T(8,128)(2,1)} %get-tuple-element.24), channel_id=1, source_target_pairs={{0,4},{4,0},{1,5},{5,1},{2,6},{6,2},{3,7},{7,3},{8,12},{12,8},{9,1... | collective-permute-start | bytes 393224 | tf_op jit(solution)/shard_map/ppermute | solution.py:30
  238.5 29.3 %collective-permute-start.35 = (bf16[1,256,1280]{2,1,0:T(8,128)(2,1)S(1)}, bf16[1,256,1280]{2,1,0:T(8,128)(2,1)}, u32[]{:S(2)}, u32[]{:S(2)}) collective-permute-start(bf16[1,256,1280]{2,1,0:T(8,128)(2,1)S(1)} %add_convert_fusion.1), channel_id=1, source_target_pairs={{0,2},{1,3},{2,0},{3,1},{4,6},{5,7},{6,4},{7,5},{8,10},{9,11},{10,... | collective-permute-start | bytes 1966088 | tf_op jit(solution)/shard_map/ppermute | solution.py:30
  241.9 11.3 %collective-permute-start.1 = (bf16[2,512,128]{2,1,0:T(8,128)(2,1)S(1)}, bf16[2,512,128]{2,1,0:T(8,128)(2,1)S(1)}, u32[]{:S(2)}, u32[]{:S(2)}) collective-permute-start(bf16[2,512,128]{2,1,0:T(8,128)(2,1)S(1)} %pad_maximum_fusion.7.refs_0_), channel_id=1, source_target_pairs={{0,8},{8,0},{16,24},{24,16},{1,9},{9,1},{17,25},{25,17},{2,10},{10... | collective-permute-start | bytes 786440 | tf_op jit(solution)/shard_map/ppermute | solution.py:30
  253.2 13.9 %collective-permute-start.2 = (bf16[2,512,128]{2,1,0:T(8,128)(2,1)S(1)}, bf16[2,512,128]{2,1,0:T(8,128)(2,1)S(1)}, u32[]{:S(2)}, u32[]{:S(2)}) collective-permute-start(bf16[2,512,128]{2,1,0:T(8,128)(2,1)S(1)} %pad_maximum_fusion.7.refs_0_), channel_id=1, source_target_pairs={{0,16},{8,24},{16,0},{24,8},{1,17},{9,25},{17,1},{25,9},{2,18},{10... | collective-permute-start | bytes 786440 | tf_op jit(solution)/shard_map/ppermute | solution.py:30
  267.2 21.5 %collective-permute-start.13 = (bf16[2,2,128,1280]{3,2,1,0:T(8,128)(2,1)S(1)}, bf16[2,2,128,1280]{3,2,1,0:T(8,128)(2,1)}, u32[]{:S(2)}, u32[]{:S(2)}) collective-permute-start(bf16[2,2,128,1280]{3,2,1,0:T(8,128)(2,1)S(1)} %pad_maximum_fusion.1.refs_6_), channel_id=1, source_target_pairs={{0,1},{1,0},{2,3},{3,2},{4,5},{5,4},{6,7},{7,6},{8,9},{9,8},{10,11... | collective-permute-start | bytes 3932168 | tf_op jit(solution)/shard_map/ppermute | solution.py:30
  267.2 22.3 %collective-permute-start.11 = (bf16[4,128,1280]{2,1,0:T(8,128)(2,1)S(1)}, bf16[4,128,1280]{2,1,0:T(8,128)(2,1)}, u32[]{:S(2)}, u32[]{:S(2)}) collective-permute-start(bf16[4,128,1280]{2,1,0:T(8,128)(2,1)S(1)} %pad_maximum_fusion.refs_4_), channel_id=1, source_target_pairs={{0,1},{1,0},{2,3},{3,2},{4,5},{5,4},{6,7},{7,6},{8,9},{9,8},{10,11... | collective-permute-start | bytes 3932168 | tf_op jit(solution)/shard_map/ppermute | solution.py:30
  267.7 21.7 %collective-permute-start.14 = (bf16[2,2,128,1280]{3,2,1,0:T(8,128)(2,1)}, bf16[2,2,128,1280]{3,2,1,0:T(8,128)(2,1)}, u32[]{:S(2)}, u32[]{:S(2)}) collective-permute-start(bf16[2,2,128,1280]{3,2,1,0:T(8,128)(2,1)} %collective-permute-done.10.refs_7_), channel_id=1, source_target_pairs={{0,1},{1,0},{2,3},{3,2},{4,5},{5,4},{6,7},{7,6},{8,9},{9,8},{10,11... | collective-permute-start | bytes 3932168 | tf_op jit(solution)/shard_map/ppermute | solution.py:30
  267.8 21.7 %collective-permute-start.12 = (bf16[4,128,1280]{2,1,0:T(8,128)(2,1)}, bf16[4,128,1280]{2,1,0:T(8,128)(2,1)}, u32[]{:S(2)}, u32[]{:S(2)}) collective-permute-start(bf16[4,128,1280]{2,1,0:T(8,128)(2,1)} %collective-permute-done.6.refs_5_), channel_id=1, source_target_pairs={{0,1},{1,0},{2,3},{3,2},{4,5},{5,4},{6,7},{7,6},{8,9},{9,8},{10,11... | collective-permute-start | bytes 3932168 | tf_op jit(solution)/shard_map/ppermute | solution.py:30
  277.2 12.2 %copy-start.5 = (bf16[2,512,1280]{2,1,0:T(8,128)(2,1)S(1)}, bf16[2,512,1280]{2,1,0:T(8,128)(2,1)}, u32[]{:S(2)}) copy-start(bf16[2,512,1280]{2,1,0:T(8,128)(2,1)} %get-tuple-element.30.refs_16_) | copy-start | bytes 7864324
  277.2 12.2 %copy-start.8 = (f32[5120]{0:T(1024)S(1)}, f32[5120]{0:T(1024)}, u32[]{:S(2)}) copy-start(f32[5120]{0:T(1024)} %get-tuple-element.45) | copy-start | bytes 61444
  277.2 12.3 %copy-start.9 = (s32[6]{0:T(128)S(1)}, s32[6]{0:T(128)}, u32[]{:S(2)}) copy-start(s32[6]{0:T(128)} %stack.45.scal) | copy-start | bytes 76
  277.2 10.2 %collective-permute-start.3 = (bf16[2,512,128]{2,1,0:T(8,128)(2,1)S(1)}, bf16[2,512,128]{2,1,0:T(8,128)(2,1)S(1)}, u32[]{:S(2)}, u32[]{:S(2)}) collective-permute-start(bf16[2,512,128]{2,1,0:T(8,128)(2,1)S(1)} %pad_maximum_fusion.7.refs_0_), channel_id=1, source_target_pairs={{0,24},{8,16},{16,8},{24,0},{1,25},{9,17},{17,9},{25,1},{2,26},{10... | collective-permute-start | bytes 786440 | tf_op jit(solution)/shard_map/ppermute | solution.py:30
  287.5 34.8 %collective-permute-start.36 = (bf16[128,1280]{1,0:T(8,128)(2,1)}, bf16[128,1280]{1,0:T(8,128)(2,1)}, u32[]{:S(2)}, u32[]{:S(2)}) collective-permute-start(bf16[128,1280]{1,0:T(8,128)(2,1)} %fusion.2), channel_id=1, source_target_pairs={{0,4},{4,0},{1,5},{5,1},{2,6},{6,2},{3,7},{7,3},{8,12},{12,8},{9,1... | collective-permute-start | bytes 983048 | tf_op jit(solution)/shard_map/ppermute | solution.py:30
  288.7 35.9 %collective-permute-start.33 = (bf16[1,384,1280]{2,1,0:T(8,128)(2,1)}, bf16[1,384,1280]{2,1,0:T(8,128)(2,1)}, u32[]{:S(2)}, u32[]{:S(2)}) collective-permute-start(bf16[1,384,1280]{2,1,0:T(8,128)(2,1)} %add_convert_fusion), channel_id=1, source_target_pairs={{0,2},{1,3},{2,0},{3,1},{4,6},{5,7},{6,4},{7,5},{8,10},{9,11},{10,... | collective-permute-start | bytes 2949128 | tf_op jit(solution)/shard_map/ppermute | solution.py:30
  289.5 1.7 copy-start.6
  309.3 2.4 copy-start.3
  311.6 3.6 %collective-permute-start.30 = (f32[8,128]{1,0:T(8,128)S(1)}, f32[8,128]{1,0:T(8,128)S(1)}, u32[]{:S(2)}, u32[]{:S(2)}) collective-permute-start(f32[8,128]{1,0:T(8,128)S(1)} %get-tuple-element.33.refs_0_), channel_id=1, source_target_pairs={{0,4},{4,0},{1,5},{5,1},{2,6},{6,2},{3,7},{7,3},{8,12},{12,8},{9,1... | collective-permute-start | bytes 12296 | tf_op jit(solution)/shard_map/ppermute | solution.py:30
  315.2 2.5 copy-start.4
  322.2 2.4 copy-start.2
  324.6 3.0 copy-start.1
